TPU v7x, 32 devices: a whole 2x2x4 slice. The times are simulated.
32 devices in a mesh: dp: 16 (over z, y, x), tensor: 2 (over core).
Axes of the slice: x: 2, y: 2, z: 4, core: 2. Of those that a mesh axis runs over, the one named last changes fastest.
Arguments:
- block_input: bfloat16 [16384, 1024], P('dp'), may hold values from -6 to 6
- segments: int32 [16384], P('dp'), may hold values from 0 to 4, as said below
- variates: int32 [16384], P('dp'), may hold values from 0 to 3
- time_ids: int32 [16384], P('dp'), may hold values from 0 to 511
- attn_gain: float32 [1024], replicated, may hold values from 0.25 to 1.75
- w_qkv: bfloat16 [1024, 3, 1024], P(None, None, 'tensor'), may hold values from -0.1875 to 0.1875
- head_bias: float32 [2, 16], P(None, 'tensor'), may hold values from -3 to 3
- w_out: bfloat16 [1024, 1024], P('tensor'), may hold values from -0.75 to 0.75
- ffn_gain: float32 [1024], replicated, may hold values from 0.25 to 1.75
- w_gate_up: bfloat16 [1024, 2, 4096], P(None, None, 'tensor'), may hold values from -0.1875 to 0.1875
- w_down: bfloat16 [4096, 1024], P('tensor'), may hold values from -0.09375 to 0.09375
- cotangent: bfloat16 [16384, 1024], P('dp'), may hold values from -6 to 6
Outputs:
- block_output: bfloat16 [16384, 1024], P('dp')
- input_grad: float32 [16384, 1024], P('dp')
- attn_gain_grad: float32 [1024], replicated
- w_qkv_grad: float32 [1024, 3, 1024], P(None, None, 'tensor')
- head_bias_grad: float32 [2, 16], P(None, 'tensor')
- w_out_grad: float32 [1024, 1024], P('tensor')
- ffn_gain_grad: float32 [1024], replicated
- w_gate_up_grad: float32 [1024, 2, 4096], P(None, None, 'tensor')
- w_down_grad: float32 [4096, 1024], P('tensor')
Inputs may be any that keep to these rules, and one draw needn't show every extreme that they name: `segments`: each sequence of 1024 tokens holds 5 documents, numbered 0 to 4 in order of position; each holds 60 tokens or more and one holds exactly 60.
All inputs are finite; a program needn't handle non-finite values.
Results may differ from a plain program's by a relative error of at most 0.035.
Values may be sent and summed in bfloat16 or wider, within the bound.
A program may use at most 256 MiB of HBM per device.

v0:
```python
import math

import jax
import jax.numpy as jnp
from jax import lax
from jax.sharding import PartitionSpec as P

LEN = 1024


EPSILON = 1e-05
MASKED = -1000000000.0


def rope_tables(time_ids, head_dim):
    half_dim = head_dim // 2
    freqs = jnp.exp(jnp.arange(half_dim, dtype=jnp.float32) * (-2.0 * math.log(10000.0) / head_dim))
    angles = time_ids.astype(jnp.float32)[:, None] * freqs[None, :]
    return (jnp.cos(angles)[:, None, :], jnp.sin(angles)[:, None, :])


def rotate(vectors, cosine, sine_part):
    half_dim = vectors.shape[-1] // 2
    first_half = vectors[..., :half_dim]
    second_half = vectors[..., half_dim:]
    return jnp.concatenate(
        [
            first_half * cosine - second_half * sine_part,
            second_half * cosine + first_half * sine_part,
        ],
        axis=-1,
    )


def rotate_back(grads, cosine, sine_part):
    half_dim = grads.shape[-1] // 2
    first_half = grads[..., :half_dim]
    second_half = grads[..., half_dim:]
    return jnp.concatenate(
        [
            first_half * cosine + second_half * sine_part,
            second_half * cosine - first_half * sine_part,
        ],
        axis=-1,
    )


def norm_rows(rows_now, gain):
    inverse = lax.rsqrt(jnp.mean(rows_now * rows_now, axis=-1, keepdims=True) + EPSILON)
    return (rows_now * inverse * gain, inverse)


def norm_back(rows_now, inverse, gain, grads):
    scaled = grads * gain
    gain_grad = jnp.sum(grads * rows_now * inverse, axis=0)
    rows_grad = inverse * scaled - rows_now * (inverse * inverse * inverse) * jnp.mean(
        scaled * rows_now, axis=-1, keepdims=True
    )
    return (rows_grad, gain_grad)


def scores_of(queries, keys_rot, same_var, allowed, head_bias, score_scale):
    raw_scores = (
        jnp.einsum("sqhd,skhd->shqk", queries, keys_rot, preferred_element_type=jnp.float32)
        * score_scale
    )
    biased = raw_scores + jnp.where(
        same_var[:, None], head_bias[0][None, :, None, None], head_bias[1][None, :, None, None]
    )
    return jnp.where(allowed[:, None], biased, MASKED)


def local(
    block_input,
    segments,
    variates,
    time_ids,
    attn_gain,
    w_qkv,
    head_bias,
    w_out,
    ffn_gain,
    w_gate_up,
    w_down,
    cotangent,
):
    row_count = block_input.shape[0]
    heads_here = head_bias.shape[1]
    head_dim = w_qkv.shape[2] // heads_here
    seq_count = row_count // LEN
    score_scale = head_dim ** (-0.5)
    input_rows = block_input.astype(jnp.float32)
    attn_normed, attn_inverse = norm_rows(input_rows, attn_gain)
    attn_normed_low = attn_normed.astype(jnp.bfloat16)
    projected = jnp.einsum(
        "td,dck->tck", attn_normed_low, w_qkv, preferred_element_type=jnp.float32
    )
    cosine, sine_part = rope_tables(time_ids, head_dim)
    head_shape = (row_count, heads_here, head_dim)
    seq_shape = (seq_count, LEN, heads_here, head_dim)
    queries = (
        rotate(projected[:, 0].reshape(head_shape), cosine, sine_part)
        .astype(jnp.bfloat16)
        .reshape(seq_shape)
    )
    keys_rot = (
        rotate(projected[:, 1].reshape(head_shape), cosine, sine_part)
        .astype(jnp.bfloat16)
        .reshape(seq_shape)
    )
    values = projected[:, 2].astype(jnp.bfloat16).reshape(seq_shape)
    seg_ids = segments.reshape(seq_count, LEN)
    var_ids = variates.reshape(seq_count, LEN)
    allowed = seg_ids[:, :, None] == seg_ids[:, None, :]
    same_var = var_ids[:, :, None] == var_ids[:, None, :]
    scores = scores_of(queries, keys_rot, same_var, allowed, head_bias, score_scale)
    row_max = jnp.max(scores, axis=-1, keepdims=True)
    exp_total = jnp.sum(jnp.exp(scores - row_max), axis=-1, keepdims=True)
    log_total = row_max + jnp.log(exp_total)
    probs_low = jnp.exp(scores - log_total).astype(jnp.bfloat16)
    attended = jnp.einsum("shqk,skhd->sqhd", probs_low, values, preferred_element_type=jnp.float32)
    attended = attended.reshape(row_count, heads_here * head_dim).astype(jnp.bfloat16)
    attn_branch = lax.psum(
        jnp.dot(attended, w_out, preferred_element_type=jnp.float32).astype(jnp.bfloat16), "tensor"
    ).astype(jnp.float32)
    mid_rows = input_rows + attn_branch
    ffn_normed, ffn_inverse = norm_rows(mid_rows, ffn_gain)
    ffn_normed_low = ffn_normed.astype(jnp.bfloat16)
    gate_up = jnp.einsum(
        "td,dcf->tcf", ffn_normed_low, w_gate_up, preferred_element_type=jnp.float32
    )
    gate_vals = gate_up[:, 0]
    up_vals = gate_up[:, 1]
    sigmoid_gate = jax.nn.sigmoid(gate_vals)
    silu_gate = gate_vals * sigmoid_gate
    hidden_low = (silu_gate * up_vals).astype(jnp.bfloat16)
    ffn_branch = lax.psum(
        jnp.dot(hidden_low, w_down, preferred_element_type=jnp.float32).astype(jnp.bfloat16),
        "tensor",
    ).astype(jnp.float32)
    block_output = (mid_rows + ffn_branch).astype(jnp.bfloat16)
    grad_down = jnp.einsum("tf,td->fd", hidden_low, cotangent, preferred_element_type=jnp.float32)
    grad_hidden = jnp.einsum("td,fd->tf", cotangent, w_down, preferred_element_type=jnp.float32)
    grad_gate = grad_hidden * up_vals * sigmoid_gate * (1.0 + gate_vals * (1.0 - sigmoid_gate))
    grad_up = grad_hidden * silu_gate
    grad_gate_up = jnp.stack([grad_gate, grad_up], axis=1).astype(jnp.bfloat16)
    grad_w_gate_up = jnp.einsum(
        "td,tcf->dcf", ffn_normed_low, grad_gate_up, preferred_element_type=jnp.float32
    )
    grad_ffn_normed = lax.psum(
        jnp.einsum(
            "tcf,dcf->td", grad_gate_up, w_gate_up, preferred_element_type=jnp.float32
        ).astype(jnp.bfloat16),
        "tensor",
    ).astype(jnp.float32)
    norm_grad_mid, grad_ffn_gain = norm_back(mid_rows, ffn_inverse, ffn_gain, grad_ffn_normed)
    grad_mid = cotangent.astype(jnp.float32) + norm_grad_mid
    grad_branch = grad_mid.astype(jnp.bfloat16)
    grad_w_out = jnp.einsum("tk,td->kd", attended, grad_branch, preferred_element_type=jnp.float32)
    grad_attended = jnp.einsum("td,kd->tk", grad_branch, w_out, preferred_element_type=jnp.float32)
    grad_attended = grad_attended.astype(jnp.bfloat16).reshape(seq_shape)
    scores_again = scores_of(queries, keys_rot, same_var, allowed, head_bias, score_scale)
    probs_again = jnp.exp(scores_again - log_total)
    probs_again_low = probs_again.astype(jnp.bfloat16)
    grad_probs = jnp.einsum(
        "sqhd,skhd->shqk", grad_attended, values, preferred_element_type=jnp.float32
    )
    grad_values = jnp.einsum(
        "shqk,sqhd->skhd", probs_again_low, grad_attended, preferred_element_type=jnp.float32
    )
    grad_scores = probs_again * (
        grad_probs - jnp.sum(probs_again * grad_probs, axis=-1, keepdims=True)
    )
    grad_scores_low = grad_scores.astype(jnp.bfloat16)
    same_low = same_var.astype(jnp.bfloat16)
    other_low = jnp.logical_not(same_var).astype(jnp.bfloat16)
    grad_bias = jnp.stack(
        [
            jnp.einsum(
                "shqk,sqk->h", grad_scores_low, same_low, preferred_element_type=jnp.float32
            ),
            jnp.einsum(
                "shqk,sqk->h", grad_scores_low, other_low, preferred_element_type=jnp.float32
            ),
        ],
        axis=0,
    )
    grad_queries = (
        jnp.einsum("shqk,skhd->sqhd", grad_scores_low, keys_rot, preferred_element_type=jnp.float32)
        * score_scale
    )
    grad_keys = (
        jnp.einsum("shqk,sqhd->skhd", grad_scores_low, queries, preferred_element_type=jnp.float32)
        * score_scale
    )
    grad_query_lin = rotate_back(grad_queries.reshape(head_shape), cosine, sine_part).reshape(
        row_count, heads_here * head_dim
    )
    grad_key_lin = rotate_back(grad_keys.reshape(head_shape), cosine, sine_part).reshape(
        row_count, heads_here * head_dim
    )
    grad_value_lin = grad_values.reshape(row_count, heads_here * head_dim)
    grad_projected = jnp.stack([grad_query_lin, grad_key_lin, grad_value_lin], axis=1).astype(
        jnp.bfloat16
    )
    grad_w_qkv = jnp.einsum(
        "td,tck->dck", attn_normed_low, grad_projected, preferred_element_type=jnp.float32
    )
    grad_attn_normed = lax.psum(
        jnp.einsum("tck,dck->td", grad_projected, w_qkv, preferred_element_type=jnp.float32).astype(
            jnp.bfloat16
        ),
        "tensor",
    ).astype(jnp.float32)
    norm_grad_input, grad_attn_gain = norm_back(
        input_rows, attn_inverse, attn_gain, grad_attn_normed
    )
    input_grad = grad_mid + norm_grad_input
    grad_attn_gain, grad_w_qkv, grad_bias, grad_w_out, grad_ffn_gain, grad_w_gate_up, grad_down = (
        lax.psum(
            (
                grad_attn_gain,
                grad_w_qkv,
                grad_bias,
                grad_w_out,
                grad_ffn_gain,
                grad_w_gate_up,
                grad_down,
            ),
            "dp",
        )
    )
    return (
        block_output,
        input_grad,
        grad_attn_gain,
        grad_w_qkv,
        grad_bias,
        grad_w_out,
        grad_ffn_gain,
        grad_w_gate_up,
        grad_down,
    )


def solution(mesh):
    placed = (
        P("dp", None),
        P("dp"),
        P("dp"),
        P("dp"),
        P(),
        P(None, None, "tensor"),
        P(None, "tensor"),
        P("tensor", None),
        P(),
        P(None, None, "tensor"),
        P("tensor", None),
        P("dp", None),
    )
    return jax.shard_map(
        local,
        mesh=mesh,
        in_specs=placed,
        out_specs=(
            P("dp", None),
            P("dp", None),
            P(),
            P(None, None, "tensor"),
            P(None, "tensor"),
            P("tensor", None),
            P(),
            P(None, None, "tensor"),
            P("tensor", None),
        ),
        check_vma=False,
    )
```

profile of v0, /device:TPU:0, one launch (start us, length us, event | category | flops | bytes accessed | tf_op | source)
XLA Modules:
  0.0 1262.6 jit_solution(3701285473080118339)
XLA Ops:
  21.2 14.6 %fusion.73 = (f32[8,1024]{1,0:T(8,128)S(1)}, f32[8,1024,1024]{1,2,0:T(8,128)}) fusion(f32[8]{0:T(128)S(1)} %get-tuple-element.60, f32[8]{0:T(128)S(1)} %get-tuple-element.59, pred[1024,1024]{0,1:T(8,128)(4,1)S(1)} %get-tuple-element.54, bf16[1024,8,32]{0,2,1:T(8,128)(2,1)S(1)} %get-tuple-element.48, bf16[1024,8,32]{0,2,1:T(8,128)(2,1)S(1)} %get-tuple-element.49, ...), kind=kOutput, calls=%fused_computation.115 | convolution fusion | flops 1119870976 | bytes 37781568 | tf_op jit(solution)/shard_map/sqhd,skhd->shqk/dot_general | solution.py:64
  35.9 13.0 %exponential_reduce_fusion = f32[8,1024]{1,0:T(8,128)S(1)} fusion(f32[8,1024,1024]{1,2,0:T(8,128)} %get-tuple-element.62, f32[8,1024]{1,0:T(8,128)S(1)} %get-tuple-element.61), kind=kLoop, calls=%fused_computation.3 | loop fusion | flops 16769024 | bytes 33619968 | tf_op jit(solution)/shard_map/reduce_sum | solution.py:118
  49.0 13.5 %fusion.40 = bf16[8,64,1024]{2,1,0:T(8,128)(2,1)S(1)} fusion(bf16[1024,8,64]{0,2,1:T(8,128)(2,1)S(1)} %bitcast.100, f32[8,1024,1024]{1,2,0:T(8,128)} %get-tuple-element.62, f32[8,1024]{1,0:T(8,128)S(1)} %log_add_fusion), kind=kOutput, calls=%fused_computation.72 | convolution fusion | flops 1091043328 | bytes 35684352 | tf_op jit(solution)/shard_map/shqk,skhd->sqhd/dot_general | solution.py:121
  66.1 24.0 %all-reduce.8.cloned.1.call-done = bf16[1024,1024]{1,0:T(8,128)(2,1)} async-done(((bf16[1024,1024]{1,0:T(8,128)(2,1)}), bf16[1024,1024]{1,0:T(8,128)(2,1)}) %all-reduce.8.cloned.1.call-update) | async-done | bytes 2097168 | tf_op jit(solution)/shard_map/psum | solution.py:123
  93.6 16.0 %fusion.10 = f32[1024,2,2048]{2,0,1:T(8,128)} fusion(bf16[1024,2,2048]{2,1,0:T(2,128)(2,1)} %param.21, bf16[1024,1024]{1,0:T(8,128)(2,1)S(1)} %copy-done.4, bf16[1024,1024]{1,0:T(8,128)(2,1)S(1)} %copy-done.1, f32[1024]{0:T(1024)S(1)} %copy-done.32, f32[1024]{0:T(1024)S(1)} %get-tuple-element.58), kind=kOutput, calls=%fused_computation.28 | convolution fusion | flops 8596226048 | bytes 29368320 | tf_op jit(solution)/shard_map/td,dcf->tcf/dot_general | solution.py:129
  109.6 13.9 %fusion.35 = (bf16[1024,1,2048]{2,0,1:T(8,128)(2,1)}, bf16[1024,1,2048]{2,0,1:T(8,128)(2,1)}, bf16[1024,2048]{1,0:T(8,128)(2,1)}) fusion(f32[1024,2,2048]{2,0,1:T(8,128)} %fusion.10, bf16[1024,1024]{1,0:T(8,128)(2,1)S(1)} %copy-done.19, bf16[2048,1024]{1,0:T(8,128)(2,1)S(1)} %copy-done.38), kind=kOutput, calls=%fused_computation.60 | convolution fusion | flops 4326424576 | bytes 35651584 | tf_op jit(solution)/shard_map/td,fd->tf/dot_general | solution.py:143
  123.5 16.7 %bitcast_convert_fusion.1 = bf16[1024,1024]{1,0:T(8,128)(2,1)} fusion(bf16[1024,2,2048]{2,1,0:T(2,128)(2,1)} %param.21, bf16[1024,1,2048]{2,0,1:T(8,128)(2,1)} %get-tuple-element.32, bf16[1024,1,2048]{2,0,1:T(8,128)(2,1)} %get-tuple-element.31), kind=kOutput, calls=%fused_computation.55 | convolution fusion | flops 8595177472 | bytes 18874368 | tf_op jit(solution)/shard_map/tcf,dcf->td/dot_general | solution.py:151
  140.3 9.3 convolution_convert_fusion
  149.6 13.2 %all-reduce.10.cloned.1.call-done = bf16[1024,1024]{1,0:T(8,128)(2,1)} async-done(((bf16[1024,1024]{1,0:T(8,128)(2,1)}), bf16[1024,1024]{1,0:T(8,128)(2,1)}) %all-reduce.10.cloned.1.call-update) | async-done | bytes 2097168 | tf_op jit(solution)/shard_map/psum | solution.py:150
  173.9 14.6 %fusion.43 = bf16[8,64,1024]{2,1,0:T(8,128)(2,1)} fusion(bf16[1024,8,64]{0,2,1:T(8,128)(2,1)} %bitcast.106, f32[8,1024,1024]{1,2,0:T(8,128)} %get-tuple-element.62, f32[8,1024]{1,0:T(8,128)S(1)} %log_add_fusion), kind=kOutput, calls=%fused_computation.73 | convolution fusion | flops 1091043328 | bytes 35684352 | tf_op jit(solution)/shard_map/shqk,sqhd->skhd/dot_general | solution.py:168
  188.5 22.5 %multiply_reduce_fusion = (f32[8,1024]{1,0:T(8,128)S(1)}, f32[8,1024,1024]{1,2,0:T(8,128)}) fusion(f32[8,1024,1024]{1,2,0:T(8,128)} %get-tuple-element.62, f32[8,1024]{1,0:T(8,128)S(1)} %log_add_fusion, bf16[1024,8,64]{0,2,1:T(8,128)(2,1)} %bitcast.107, bf16[1024,8,64]{0,2,1:T(8,128)(2,1)} %bitcast.101), kind=kOutput, calls=%fused_computation.1 | convolution fusion | flops 1098899456 | bytes 69271552 | tf_op jit(solution)/shard_map/sqhd,skhd->shqk/dot_general | solution.py:165
  210.9 28.1 %multiply_convert_fusion = bf16[8,1024,1024]{1,2,0:T(8,128)(2,1)} fusion(f32[8,1024,1024]{1,2,0:T(8,128)} %get-tuple-element.64, f32[8,1024,1024]{1,2,0:T(8,128)} %get-tuple-element.62, f32[8,1024]{1,0:T(8,128)S(1)} %get-tuple-element.63, f32[8,1024]{1,0:T(8,128)S(1)} %log_add_fusion), kind=kLoop, calls=%fused_computation | loop fusion | flops 33554432 | bytes 83951616 | tf_op jit(solution)/shard_map/convert_element_type | solution.py:174
  239.0 10.5 multiply_bitcast_fusion.1
  249.5 12.7 %multiply_bitcast_fusion = f32[1024,8,64]{0,2,1:T(8,128)} fusion(bf16[8,1024,1024]{1,2,0:T(8,128)(2,1)} %multiply_convert_fusion, bf16[1024,8,32]{0,2,1:T(8,128)(2,1)} %copy-done.15, bf16[1024,8,32]{0,2,1:T(8,128)(2,1)} %copy-done.14), kind=kOutput, calls=%fused_computation.66 | convolution fusion | flops 1076363264 | bytes 19922944 | tf_op jit(solution)/shard_map/shqk,sqhd->skhd/dot_general | solution.py:193
  273.4 6.5 bitcast_convert_fusion
  280.0 11.6 fusion.74
  291.6 15.7 %fusion.12 = f32[1024,2,2048]{2,0,1:T(8,128)} fusion(bf16[1024,1,2048]{2,0,1:T(8,128)(2,1)} %get-tuple-element.32, bf16[1024,1,2048]{2,0,1:T(8,128)(2,1)S(1)} %copy-done.41, bf16[1024,1024]{1,0:T(8,128)(2,1)S(1)} %copy-done.6, bf16[1024,1024]{1,0:T(8,128)(2,1)S(1)} %copy-done.3, f32[1024]{0:T(1024)S(1)} %copy-done.32, f32[1024]{0:T(1024)S(1)} %get-tuple-element.58), kind=kOutput, calls=%fused_computation.30 | convolution fusion | flops 8613003264 | bytes 29368320 | tf_op jit(solution)/shard_map/td,tcf->dcf/dot_general | solution.py:147
  310.0 6.0 fusion.46
  316.0 17.9 %fusion.52 = f32[1,8]{1,0:T(1,128)S(1)} fusion(pred[1024,1024,1]{0,1,2:T(32,128)(4,1)} %get-tuple-element.53, bf16[8,1024,1024]{1,2,0:T(8,128)(2,1)} %multiply_convert_fusion), kind=kOutput, calls=%fused_computation.77 | convolution fusion | flops 16777216 | bytes 17825824 | tf_op jit(solution)/shard_map/shqk,sqk->h/dot_general | solution.py:182
  333.9 18.2 %fusion.47 = f32[1,8]{1,0:T(1,128)S(1)} fusion(pred[1024,1024,1]{0,1,2:T(32,128)(4,1)S(1)} %copy-done.24, bf16[8,1024,1024]{1,2,0:T(8,128)(2,1)} %multiply_convert_fusion), kind=kOutput, calls=%fused_computation.76 | convolution fusion | flops 16777216 | bytes 17825824 | tf_op jit(solution)/shard_map/shqk,sqk->h/dot_general | solution.py:179
  356.2 47.0 %all-reduce = (f32[1024]{0:T(1024)}, f32[2,8]{1,0:T(2,128)}, f32[1024]{0:T(1024)}) all-reduce(f32[1024]{0:T(1024)S(1)} %get-tuple-element.20, f32[2,8]{1,0:T(2,128)S(1)} %pad_maximum_fusion.16, f32[1024]{0:T(1024)S(1)} %copy-done.33), channel_id=1, replica_groups=mesh['dp'=16,'tensor'=2] {'dp'}, use_global_device_ids=true, to_apply=%region_12.13 | all-reduce | flops 2064 | bytes 16512 | tf_op jit(solution)/shard_map/psum | solution.py:220
  403.2 8.0 fusion.21
  411.2 805.2 %all-reduce.12.cloned.1.call-done = (f32[1024,3,512]{2,0,1:T(8,128)}, f32[512,1024]{1,0:T(8,128)}, f32[1024,2,2048]{2,0,1:T(8,128)}, f32[2048,1024]{1,0:T(8,128)}) async-done(((f32[1024,3,512]{2,0,1:T(8,128)}, f32[512,1024]{1,0:T(8,128)}, f32[1024,2,2048]{2,0,1:T(8,128)}, f32[2048,1024]{1,0:T(8,128)}), (f32[1024,3,512]{2,0,1:T(8,128)}, f32[512,1024]{1,0:T(8,128)}, f32[1024,2,2048]{2,0,1:T(8,128)}, ...) | async-done | bytes 33554448 | tf_op jit(solution)/shard_map/psum | solution.py:220
  1216.4 28.7 %copy.33 = f32[1024,2,2048]{2,1,0:T(2,128)} copy(f32[1024,2,2048]{2,0,1:T(8,128)} %get-tuple-element.27) | data formatting | bytes 33554432
  (130 shorter events, 60.6 us)
Async XLA Ops:
  7.2 83.0 %all-reduce.8.cloned.1.call-start = ((), (), s32[]{:S(2)}) async-start(), calls=%async_computation | async-start | bytes 4194304 | tf_op jit(solution)/shard_map/psum | solution.py:123
  15.5 33.4 %copy-start.9 = (bf16[1024,1,512]{0,2,1:T(8,128)(2,1)}, bf16[1024,1,512]{0,2,1:T(8,128)(2,1)S(1)}, u32[]{:S(2)}) copy-start(bf16[1024,1,512]{0,2,1:T(8,128)(2,1)S(1)} %slice.113) | copy-start | bytes 3145732
  21.2 14.7 %copy-start.14 = (bf16[1024,8,32]{0,2,1:T(8,128)(2,1)}, bf16[1024,8,32]{0,2,1:T(8,128)(2,1)S(1)}, u32[]{:S(2)}) copy-start(bf16[1024,8,32]{0,2,1:T(8,128)(2,1)S(1)} %get-tuple-element.40) | copy-start | bytes 1572868
  21.2 14.7 %copy-start.15 = (bf16[1024,8,32]{0,2,1:T(8,128)(2,1)}, bf16[1024,8,32]{0,2,1:T(8,128)(2,1)S(1)}, u32[]{:S(2)}) copy-start(bf16[1024,8,32]{0,2,1:T(8,128)(2,1)S(1)} %get-tuple-element.41) | copy-start | bytes 1572868
  21.2 14.7 %copy-start.16 = (bf16[1024,8,32]{0,2,1:T(8,128)(2,1)}, bf16[1024,8,32]{0,2,1:T(8,128)(2,1)S(1)}, u32[]{:S(2)}) copy-start(bf16[1024,8,32]{0,2,1:T(8,128)(2,1)S(1)} %get-tuple-element.48) | copy-start | bytes 1572868
  21.2 14.7 %copy-start.17 = (bf16[1024,8,32]{0,2,1:T(8,128)(2,1)}, bf16[1024,8,32]{0,2,1:T(8,128)(2,1)S(1)}, u32[]{:S(2)}) copy-start(bf16[1024,8,32]{0,2,1:T(8,128)(2,1)S(1)} %get-tuple-element.49) | copy-start | bytes 1572868
  48.9 14.5 %copy-start.39 = (bf16[512,1024]{1,0:T(8,128)(2,1)S(1)}, bf16[512,1024]{1,0:T(8,128)(2,1)}, u32[]{:S(2)}) copy-start(bf16[512,1024]{1,0:T(8,128)(2,1)} %param.19) | copy-start | bytes 3145732
  66.1 27.2 %copy-start.32 = (f32[1024]{0:T(1024)S(1)}, f32[1024]{0:T(1024)}, u32[]{:S(2)}) copy-start(f32[1024]{0:T(1024)} %param.20) | copy-start | bytes 12292
  66.1 96.7 %all-reduce.10.cloned.1.call-start = ((), (), s32[]{:S(2)}) async-start(), calls=%async_computation.1 | async-start | bytes 4194304 | tf_op jit(solution)/shard_map/psum | solution.py:150
  93.6 16.0 %copy-start.19 = (bf16[1024,1024]{1,0:T(8,128)(2,1)S(1)}, bf16[1024,1024]{1,0:T(8,128)(2,1)}, u32[]{:S(2)}) copy-start(bf16[1024,1024]{1,0:T(8,128)(2,1)} %param.23) | copy-start | bytes 6291460
  93.6 16.0 %copy-start.38 = (bf16[2048,1024]{1,0:T(8,128)(2,1)S(1)}, bf16[2048,1024]{1,0:T(8,128)(2,1)}, u32[]{:S(2)}) copy-start(bf16[2048,1024]{1,0:T(8,128)(2,1)} %param.22) | copy-start | bytes 12582916
  140.2 211.9 %all-reduce.14.cloned.1.call-start = ((), (), s32[]{:S(2)}) async-start(), calls=%async_computation.3 | async-start | bytes 8388608 | tf_op jit(solution)/shard_map/psum | solution.py:137
  249.5 14.9 %copy-start.21 = (f32[1024,32]{0,1:T(8,128)S(1)}, f32[1024,32]{0,1:T(8,128)}, u32[]{:S(2)}) copy-start(f32[1024,32]{0,1:T(8,128)} %copy-done.20) | copy-start | bytes 393220
  249.5 14.9 %copy-start.23 = (f32[1024,32]{0,1:T(8,128)S(1)}, f32[1024,32]{0,1:T(8,128)}, u32[]{:S(2)}) copy-start(f32[1024,32]{0,1:T(8,128)} %copy-done.22) | copy-start | bytes 393220
  279.9 936.5 %all-reduce.12.cloned.1.call-start = ((), (), s32[]{:S(2)}) async-start(), calls=%async_computation.2 | async-start | bytes 67108864 | tf_op jit(solution)/shard_map/psum | solution.py:220
  280.0 11.6 copy-start.3
  280.0 11.6 copy-start.6
  280.0 11.6 copy-start.41
  291.6 15.8 %copy-start.8 = (f32[1024,1024]{1,0:T(8,128)S(1)}, f32[1024,1024]{1,0:T(8,128)}, u32[]{:S(2)}) copy-start(f32[1024,1024]{1,0:T(8,128)} %copy-done.7) | copy-start | bytes 12582916
  291.6 15.7 %copy-start.13 = (bf16[8,64,1024]{2,1,0:T(8,128)(2,1)S(1)}, bf16[8,64,1024]{2,1,0:T(8,128)(2,1)}, u32[]{:S(2)}) copy-start(bf16[8,64,1024]{2,1,0:T(8,128)(2,1)} %copy-done.12) | copy-start | bytes 3145732
  316.0 17.9 %copy-start.24 = (pred[1024,1024,1]{0,1,2:T(32,128)(4,1)S(1)}, pred[1024,1024,1]{0,1,2:T(32,128)(4,1)}, u32[]{:S(2)}) copy-start(pred[1024,1024,1]{0,1,2:T(32,128)(4,1)} %get-tuple-element.52) | copy-start | bytes 3145732
  352.1 51.1 %copy-start.34 = (f32[1024]{0:T(1024)S(1)}, f32[1024]{0:T(1024)}, u32[]{:S(2)}) copy-start(f32[1024]{0:T(1024)} %get-tuple-element.55) | copy-start | bytes 12292
  1216.4 28.7 %slice-start = ((s8[6291456]{0:T(1024)(128)(4,1)}), s8[4194304]{0:T(1024)(128)(4,1)S(1)}, s32[]{:S(2)}) async-start(s8[6291456]{0:T(1024)(128)(4,1)} %bitcast.104), calls=%async_computation.4 | async-start | bytes 8388608
  1216.4 28.8 %slice-start.1 = ((s8[6291456]{0:T(1024)(128)(4,1)}), s8[2097152]{0:T(1024)(128)(4,1)S(1)}, s32[]{:S(2)}) async-start(s8[6291456]{0:T(1024)(128)(4,1)} %bitcast.104), calls=%async_computation.5 | async-start | bytes 4194304
  (24 other events, 75.3 us)
Sparse Core Ops, SparseCore 0:
  66.2 23.9 all-reduce.7
  140.4 22.3 all-reduce.9
  280.0 29.7 all-reduce.13
  318.3 898.0 all-reduce.11
where the time goes:
time: 1270 us; the launch traced here: 1260 us
  waiting for transfers between devices  843 us (66%)
  matrix products  233 us (18%)
  other arithmetic  77 us (6%)
  local copies, waits for them, and re-layouts  48.4 us (4%)
  blocking collectives  47 us (4%)
  between operations  14.7 us (1%)
    psum x1, waiting for transfers between devices, local(): lax.psum((grad_attn_gain, grad_w_qkv, grad_bias, grad_w_out, grad_ffn_gai...  805 us
    psum x1, blocking collectives, local(): lax.psum((grad_attn_gain, grad_w_qkv, grad_bias, grad_w_out, grad_ffn_gai...  47 us
    unnamed x92, local copies, waits for them, and re-layouts  41.1 us
    convert_element_type x1, other arithmetic, local(): grad_scores_low = grad_scores.astype(jnp.bfloat16)  28.1 us
  transfers between devices with their start and end apart: 4, of which 3 were waited for; matrix products, arithmetic and copies ran while one was open for 7% of the time, Pallas kernels for 0%

commit v1 on v0

--- a/solution.py
+++ b/solution.py
@@ -1,15 +1,508 @@
+import functools
 import math
 
 import jax
 import jax.numpy as jnp
 from jax import lax
+from jax.experimental import pallas as pl
+from jax.experimental.pallas import tpu as pltpu
 from jax.sharding import PartitionSpec as P
 
 LEN = 1024
-
-
 EPSILON = 1e-05
 MASKED = -1000000000.0
+BF = jnp.bfloat16
+F32 = jnp.float32
+MESH = pl.DeviceIdType.MESH
+VMEM_LIMIT = 60 * 1024 * 1024
+LANES = 128
+HEAD = 64
+VAR_COLS = 4
+SEG_COL = 12
+ONE_COL = 20
+
+
+def dot_nn(a, b):
+    return lax.dot_general(a, b, (((1,), (0,)), ((), ())), preferred_element_type=F32)
+
+
+def dot_nt(a, b):
+    return lax.dot_general(a, b, (((1,), (1,)), ((), ())), preferred_element_type=F32)
+
+
+def dot_tn(a, b):
+    return lax.dot_general(a, b, (((0,), (0,)), ((), ())), preferred_element_type=F32)
+
+
+def whole_spec():
+    return pl.BlockSpec(memory_space=pltpu.VMEM)
+
+
+def split3(v):
+    hi = v.astype(BF).astype(F32)
+    mid = (v - hi).astype(BF).astype(F32)
+    return hi, mid, v - hi - mid
+
+
+def half_swap(u):
+    lane = lax.broadcasted_iota(jnp.int32, u.shape, 1) % HEAD
+    return jnp.where(lane < HEAD // 2, pltpu.roll(u, LANES - HEAD // 2, 1), pltpu.roll(u, HEAD // 2, 1))
+
+
+def qkv_body(x_ref, gain_ref, w_ref, cos_ref, sin_ref, xn_ref, q_ref, k_ref, v_ref):
+    x = x_ref[...].astype(F32)
+    inv = lax.rsqrt(jnp.mean(x * x, axis=-1, keepdims=True) + EPSILON)
+    xn = (x * inv * gain_ref[...]).astype(BF)
+    xn_ref[...] = xn
+    cosine = cos_ref[...]
+    sine = sin_ref[...]
+    for part, out, factor in ((0, q_ref, HEAD**-0.5), (1, k_ref, 1.0)):
+        lin = dot_nn(xn, w_ref[part])
+        for s in range(lin.shape[1] // LANES):
+            u = lin[:, s * LANES : (s + 1) * LANES]
+            rot = (u * cosine + half_swap(u) * sine).astype(BF)
+            if factor != 1.0:
+                rot = (rot.astype(F32) * factor).astype(BF)
+            out[:, s * LANES : (s + 1) * LANES] = rot
+    v_ref[...] = dot_nn(xn, w_ref[2]).astype(BF)
+
+
+def qkv_call(x, gain, w, cosine, sine):
+    rows, dim = x.shape
+    width = w.shape[2]
+    blk = min(256, rows)
+    row = lambda cols: pl.BlockSpec((blk, cols), lambda i: (i, 0))
+    return pl.pallas_call(
+        qkv_body,
+        grid=(rows // blk,),
+        out_shape=[jax.ShapeDtypeStruct((rows, dim), BF)] + [jax.ShapeDtypeStruct((rows, width), BF)] * 3,
+        in_specs=[
+            row(dim),
+            pl.BlockSpec((1, dim), lambda i: (0, 0)),
+            pl.BlockSpec(w.shape, lambda i: (0, 0, 0)),
+            row(LANES),
+            row(LANES),
+        ],
+        out_specs=[row(dim), row(width), row(width), row(width)],
+        compiler_params=pltpu.CompilerParams(vmem_limit_bytes=VMEM_LIMIT),
+        name="qkv",
+    )(x, gain, w, cosine, sine)
+
+
+def attn_fwd_body(q_ref, k_ref, v_ref, base_ref, segq_ref, extk_ref, bias_ref, o_ref, o32_ref, extq_ref):
+    rows = q_ref.shape[0]
+    blk = 256
+    lane = lax.broadcasted_iota(jnp.int32, (blk, LANES), 1)
+    kx = jnp.concatenate([k_ref[...], extk_ref[...]], axis=1)
+    ones = jnp.ones((rows, LANES), BF)
+    vx = jnp.concatenate([v_ref[...], ones], axis=1)
+    for i in range(rows // blk):
+        sl = slice(i * blk, (i + 1) * blk)
+        q = q_ref[sl, :].astype(F32)
+        base = base_ref[sl, :]
+        segq = segq_ref[sl, :]
+        outs = []
+        for h in range(2):
+            ext = base * bias_ref[0, h : h + 1, :] + segq
+            mine = (lane >= HEAD) if h else (lane < HEAD)
+            qx = jnp.concatenate([jnp.where(mine, q, 0.0), ext], axis=1).astype(BF)
+            s = dot_nt(qx, kx)
+            top = jnp.max(s, axis=-1, keepdims=True)
+            p = jnp.exp(s - top).astype(BF)
+            ox = dot_nn(p, vx)
+            total = ox[:, LANES:]
+            outs.append(ox[:, :LANES] / total)
+            lse = top + jnp.log(total)
+            hi, mid, low = split3(lse)
+            ext = jnp.where(
+                lane == ONE_COL, -hi, jnp.where(lane == ONE_COL + 1, -mid, jnp.where(lane == ONE_COL + 2, -low, ext))
+            )
+            extq_ref[0, h, sl, :] = ext.astype(BF)
+        o = jnp.where(lane < HEAD, outs[0], outs[1])
+        o32_ref[sl, :] = o
+        o_ref[sl, :] = o.astype(BF)
+
+
+def attn_fwd_call(q, k, v, base, segq, extk, bias_rows):
+    rows, width = q.shape
+    pairs = width // LANES
+    col = pl.BlockSpec((rows, LANES), lambda p: (0, p))
+    full = pl.BlockSpec((rows, LANES), lambda p: (0, 0))
+    return pl.pallas_call(
+        attn_fwd_body,
+        grid=(pairs,),
+        out_shape=[
+            jax.ShapeDtypeStruct((rows, width), BF),
+            jax.ShapeDtypeStruct((rows, width), F32),
+            jax.ShapeDtypeStruct((pairs, 2, rows, LANES), BF),
+        ],
+        in_specs=[col, col, col, full, full, full, pl.BlockSpec((1, 2, LANES), lambda p: (p, 0, 0))],
+        out_specs=[col, col, pl.BlockSpec((1, 2, rows, LANES), lambda p: (p, 0, 0, 0))],
+        compiler_params=pltpu.CompilerParams(vmem_limit_bytes=VMEM_LIMIT),
+        name="attn_fwd",
+    )(q, k, v, base, segq, extk, bias_rows)
+
+
+def attn_bwd_body(
+    q_ref, k_ref, v_ref, do_ref, o32_ref, extq_ref, extk_ref, oh_ref, cos_ref, sin_ref, dq_ref, dk_ref, dv_ref, gb_ref, dqt_ref
+):
+    rows = q_ref.shape[0]
+    blk = 256
+    lane = lax.broadcasted_iota(jnp.int32, (blk, LANES), 1)
+    kx = jnp.concatenate([k_ref[...], extk_ref[...]], axis=1)
+    kxt = kx.T
+    lane_all = lax.broadcasted_iota(jnp.int32, (rows, LANES), 1)
+    vx = jnp.concatenate([v_ref[...], jnp.where(lane_all < 3, 1.0, 0.0).astype(BF)], axis=1)
+    dv = jnp.zeros((rows, LANES), F32)
+    dk = jnp.zeros((rows, LANES), F32)
+    for h in range(2):
+        same = jnp.zeros((8, blk), F32)
+        other = jnp.zeros((8, blk), F32)
+        for i in range(rows // blk):
+            sl = slice(i * blk, (i + 1) * blk)
+            mine = (lane >= HEAD) if h else (lane < HEAD)
+            q = jnp.where(mine, q_ref[sl, :].astype(F32), 0.0).astype(BF)
+            do32 = jnp.where(mine, do_ref[sl, :].astype(F32), 0.0)
+            do = do32.astype(BF)
+            delta = jnp.sum(do32 * o32_ref[sl, :], axis=-1, keepdims=True)
+            hi, mid, low = split3(delta)
+            dext = jnp.where(lane == 0, -hi, jnp.where(lane == 1, -mid, jnp.where(lane == 2, -low, 0.0))).astype(BF)
+            st = dot_nt(kx, jnp.concatenate([q, extq_ref[0, h, sl, :]], axis=1))
+            pt = jnp.exp(st)
+            dpt = dot_nt(vx, jnp.concatenate([do, dext], axis=1))
+            dst = (pt * dpt).astype(BF)
+            dv = dv + dot_nn(pt.astype(BF), do)
+            dk = dk + dot_nn(dst, q)
+            dqt = dot_nn(kxt, dst)
+            dqt_ref[h * HEAD : (h + 1) * HEAD, sl] = dqt[h * HEAD : (h + 1) * HEAD, :]
+            g = dqt[LANES : LANES + 8, :]
+            oh = oh_ref[0, :, sl]
+            same = same + g * oh
+            other = other + g * oh_ref[1, :, sl]
+        gb_ref[0, h, 0] = same
+        gb_ref[0, h, 1] = other
+    cosine = cos_ref[...]
+    sine = sin_ref[...]
+    dq = dqt_ref[...].T * HEAD**-0.5
+    dq_ref[...] = (dq * cosine - half_swap(dq) * sine).astype(BF)
+    dk_ref[...] = (dk * cosine - half_swap(dk) * sine).astype(BF)
+    dv_ref[...] = dv.astype(BF)
+
+
+def attn_bwd_call(q, k, v, do, o32, extq, extk, onehot, cosine, sine):
+    rows, width = q.shape
+    pairs = width // LANES
+    col = pl.BlockSpec((rows, LANES), lambda p: (0, p))
+    full = pl.BlockSpec((rows, LANES), lambda p: (0, 0))
+    blk = 256
+    return pl.pallas_call(
+        attn_bwd_body,
+        grid=(pairs,),
+        out_shape=[jax.ShapeDtypeStruct((rows, width), BF)] * 3 + [jax.ShapeDtypeStruct((pairs, 2, 2, 8, blk), F32)],
+        in_specs=[
+            col, col, col, col, col,
+            pl.BlockSpec((1, 2, rows, LANES), lambda p: (p, 0, 0, 0)),
+            full,
+            pl.BlockSpec((2, 8, rows), lambda p: (0, 0, 0)),
+            full, full,
+        ],
+        out_specs=[col, col, col, pl.BlockSpec((1, 2, 2, 8, blk), lambda p: (p, 0, 0, 0, 0))],
+        scratch_shapes=[pltpu.VMEM((LANES, rows), F32)],
+        compiler_params=pltpu.CompilerParams(vmem_limit_bytes=VMEM_LIMIT),
+        name="attn_bwd",
+    )(q, k, v, do, o32, extq, extk, onehot, cosine, sine)
+
+
+def partner_barrier():
+    dp = lax.axis_index("dp")
+    other = 1 - lax.axis_index("tensor")
+    barrier = pltpu.get_barrier_semaphore()
+    pl.semaphore_signal(barrier, inc=1, device_id=(dp, other), device_id_type=MESH)
+    pl.semaphore_wait(barrier, 1)
+    return (dp, other)
+
+
+def send_rows(src, dst, sl, ssem, rsem, peer):
+    return pltpu.make_async_remote_copy(
+        src_ref=src.at[sl], dst_ref=dst.at[sl], send_sem=ssem, recv_sem=rsem, device_id=peer, device_id_type=MESH
+    )
+
+
+CHUNKS = 4
+
+
+def attn_out_body(x_ref, o_ref, w_ref, gain_ref, mid_ref, xn_ref, mine, theirs, ssem, rsem):
+    peer = partner_barrier()
+    rows = x_ref.shape[0]
+    blk = rows // CHUNKS
+    copies = []
+    for c in range(CHUNKS):
+        sl = slice(c * blk, (c + 1) * blk)
+        mine[sl, :] = dot_nn(o_ref[sl, :], w_ref[...]).astype(BF)
+        copy = send_rows(mine, theirs, pl.ds(c * blk, blk), ssem.at[c], rsem.at[c], peer)
+        copy.start()
+        copies.append(copy)
+    for c in range(CHUNKS):
+        sl = slice(c * blk, (c + 1) * blk)
+        copies[c].wait_recv()
+        mid = x_ref[sl, :].astype(F32) + (mine[sl, :].astype(F32) + theirs[sl, :].astype(F32))
+        inv = lax.rsqrt(jnp.mean(mid * mid, axis=-1, keepdims=True) + EPSILON)
+        mid_ref[sl, :] = mid
+        xn_ref[sl, :] = (mid * inv * gain_ref[...]).astype(BF)
+    for c in range(CHUNKS):
+        copies[c].wait_send()
+
+
+def attn_out_call(x, o, w, gain):
+    rows, dim = x.shape
+    return pl.pallas_call(
+        attn_out_body,
+        out_shape=[jax.ShapeDtypeStruct((rows, dim), F32), jax.ShapeDtypeStruct((rows, dim), BF)],
+        in_specs=[whole_spec()] * 4,
+        out_specs=[whole_spec()] * 2,
+        scratch_shapes=[
+            pltpu.VMEM((rows, dim), BF),
+            pltpu.VMEM((rows, dim), BF),
+            pltpu.SemaphoreType.DMA((CHUNKS,)),
+            pltpu.SemaphoreType.DMA((CHUNKS,)),
+        ],
+        compiler_params=pltpu.CompilerParams(collective_id=1, has_side_effects=True, vmem_limit_bytes=VMEM_LIMIT),
+        name="attn_out",
+    )(x, o, w, gain)
+
+
+def ffn_body(xn_ref, ct_ref, wg_ref, wu_ref, wd_ref, out_ref, gx_ref, gd_ref, gg_ref, gu_ref, acc_o, acc_g, hid, dg, du):
+    j = pl.program_id(0)
+    rows = xn_ref.shape[0]
+    blk = 256
+
+    @pl.when(j == 0)
+    def _():
+        acc_o[...] = jnp.zeros_like(acc_o)
+        acc_g[...] = jnp.zeros_like(acc_g)
+
+    wg = wg_ref[...]
+    wu = wu_ref[...]
+    wd = wd_ref[...]
+    for i in range(rows // blk):
+        sl = slice(i * blk, (i + 1) * blk)
+        xn = xn_ref[sl, :]
+        gate = dot_nn(xn, wg)
+        up = dot_nn(xn, wu)
+        gh = dot_nt(ct_ref[sl, :], wd)
+        sig = jax.nn.sigmoid(gate)
+        silu = gate * sig
+        hidden = (silu * up).astype(BF)
+        dgate = (gh * up * sig * (1.0 + gate * (1.0 - sig))).astype(BF)
+        dup = (gh * silu).astype(BF)
+        hid[sl, :] = hidden
+        dg[sl, :] = dgate
+        du[sl, :] = dup
+        acc_o[sl, :] += dot_nn(hidden, wd)
+        acc_g[sl, :] += dot_nt(dgate, wg) + dot_nt(dup, wu)
+    gd_ref[...] = dot_tn(hid[...], ct_ref[...]).astype(BF)
+    gg_ref[...] = dot_tn(xn_ref[...], dg[...]).astype(BF)
+    gu_ref[...] = dot_tn(xn_ref[...], du[...]).astype(BF)
+
+    @pl.when(j == pl.num_programs(0) - 1)
+    def _():
+        out_ref[...] = acc_o[...].astype(BF)
+        gx_ref[...] = acc_g[...].astype(BF)
+
+
+def ffn_call(xn, ct, wg, wu, wd):
+    rows, dim = xn.shape
+    hidden = wd.shape[0]
+    blk = 256
+    full = pl.BlockSpec((rows, dim), lambda j: (0, 0))
+    colw = pl.BlockSpec((dim, blk), lambda j: (0, j))
+    roww = pl.BlockSpec((blk, dim), lambda j: (j, 0))
+    return pl.pallas_call(
+        ffn_body,
+        grid=(hidden // blk,),
+        out_shape=[
+            jax.ShapeDtypeStruct((rows, dim), BF),
+            jax.ShapeDtypeStruct((rows, dim), BF),
+            jax.ShapeDtypeStruct((hidden, dim), BF),
+            jax.ShapeDtypeStruct((dim, hidden), BF),
+            jax.ShapeDtypeStruct((dim, hidden), BF),
+        ],
+        in_specs=[full, full, colw, colw, roww],
+        out_specs=[full, full, roww, colw, colw],
+        scratch_shapes=[pltpu.VMEM((rows, dim), F32)] * 2 + [pltpu.VMEM((rows, blk), BF)] * 3,
+        compiler_params=pltpu.CompilerParams(vmem_limit_bytes=VMEM_LIMIT),
+        name="ffn",
+    )(xn, ct, wg, wu, wd)
+
+
+def norm_back(rows_now, gain, grads):
+    inv = lax.rsqrt(jnp.mean(rows_now * rows_now, axis=-1, keepdims=True) + EPSILON)
+    scaled = grads * gain
+    gain_grad = jnp.sum(grads * rows_now * inv, axis=0, keepdims=True)
+    back = inv * scaled - rows_now * (inv * inv * inv) * jnp.mean(scaled * rows_now, axis=-1, keepdims=True)
+    return back, gain_grad
+
+
+def ffn_back_body(
+    gx_ref, fo_ref, mid_ref, ct_ref, gain_ref, w_ref, at_ref,
+    out_ref, gm_ref, do_ref, gw_ref, gg_ref, gx_in, fo_in, gb, ssem, rsem,
+):
+    peer = partner_barrier()
+    rows = mid_ref.shape[0]
+    blk = rows // CHUNKS
+    copies = []
+    for n, (src, dst) in enumerate(((gx_ref, gx_in), (fo_ref, fo_in))):
+        for c in range(CHUNKS):
+            at = n * CHUNKS + c
+            copy = send_rows(src, dst, pl.ds(c * blk, blk), ssem.at[at], rsem.at[at], peer)
+            copy.start()
+            copies.append(copy)
+    gain_sum = jnp.zeros((1, mid_ref.shape[1]), F32)
+    for c in range(CHUNKS):
+        sl = slice(c * blk, (c + 1) * blk)
+        copies[c].wait_recv()
+        grads = gx_ref[sl, :].astype(F32) + gx_in[sl, :].astype(F32)
+        back, gain_grad = norm_back(mid_ref[sl, :], gain_ref[...], grads)
+        gain_sum = gain_sum + gain_grad
+        gm = ct_ref[sl, :].astype(F32) + back
+        gm_ref[sl, :] = gm
+        gb[sl, :] = gm.astype(BF)
+        do_ref[sl, :] = dot_nt(gb[sl, :], w_ref[...]).astype(BF)
+    gg_ref[...] = gain_sum
+    gw_ref[...] = dot_tn(at_ref[...], gb[...]).astype(BF)
+    for c in range(CHUNKS):
+        sl = slice(c * blk, (c + 1) * blk)
+        copies[CHUNKS + c].wait_recv()
+        out_ref[sl, :] = (mid_ref[sl, :] + (fo_ref[sl, :].astype(F32) + fo_in[sl, :].astype(F32))).astype(BF)
+    for copy in copies:
+        copy.wait_send()
+
+
+def ffn_back_call(gx, fo, mid, ct, gain, w, at):
+    rows, dim = mid.shape
+    width = w.shape[0]
+    return pl.pallas_call(
+        ffn_back_body,
+        out_shape=[
+            jax.ShapeDtypeStruct((rows, dim), BF),
+            jax.ShapeDtypeStruct((rows, dim), F32),
+            jax.ShapeDtypeStruct((rows, width), BF),
+            jax.ShapeDtypeStruct((width, dim), BF),
+            jax.ShapeDtypeStruct((1, dim), F32),
+        ],
+        in_specs=[whole_spec()] * 7,
+        out_specs=[whole_spec()] * 5,
+        scratch_shapes=[
+            pltpu.VMEM((rows, dim), BF),
+            pltpu.VMEM((rows, dim), BF),
+            pltpu.VMEM((rows, dim), BF),
+            pltpu.SemaphoreType.DMA((2 * CHUNKS,)),
+            pltpu.SemaphoreType.DMA((2 * CHUNKS,)),
+        ],
+        compiler_params=pltpu.CompilerParams(collective_id=2, has_side_effects=True, vmem_limit_bytes=VMEM_LIMIT),
+        name="ffn_back",
+    )(gx, fo, mid, ct, gain, w, at)
+
+
+def qkv_back_body(dq_ref, dk_ref, dv_ref, w_ref, xn_ref, x_ref, gain_ref, gm_ref, ig_ref, gw_ref, gg_ref, mine, theirs, ssem, rsem):
+    peer = partner_barrier()
+    rows = x_ref.shape[0]
+    blk = rows // CHUNKS
+    parts = (dq_ref, dk_ref, dv_ref)
+    copies = []
+    for c in range(CHUNKS):
+        sl = slice(c * blk, (c + 1) * blk)
+        total = dot_nt(dq_ref[sl, :], w_ref[0])
+        total = total + dot_nt(dk_ref[sl, :], w_ref[1])
+        total = total + dot_nt(dv_ref[sl, :], w_ref[2])
+        mine[sl, :] = total.astype(BF)
+        copy = send_rows(mine, theirs, pl.ds(c * blk, blk), ssem.at[c], rsem.at[c], peer)
+        copy.start()
+        copies.append(copy)
+    for n in range(3):
+        gw_ref[n] = dot_tn(xn_ref[...], parts[n][...]).astype(BF)
+    gain_sum = jnp.zeros((1, x_ref.shape[1]), F32)
+    for c in range(CHUNKS):
+        sl = slice(c * blk, (c + 1) * blk)
+        copies[c].wait_recv()
+        grads = mine[sl, :].astype(F32) + theirs[sl, :].astype(F32)
+        back, gain_grad = norm_back(x_ref[sl, :].astype(F32), gain_ref[...], grads)
+        gain_sum = gain_sum + gain_grad
+        ig_ref[sl, :] = gm_ref[sl, :] + back
+    gg_ref[...] = gain_sum
+    for copy in copies:
+        copy.wait_send()
+
+
+def qkv_back_call(dq, dk, dv, w, xn, x, gain, gm):
+    rows, dim = x.shape
+    return pl.pallas_call(
+        qkv_back_body,
+        out_shape=[
+            jax.ShapeDtypeStruct((rows, dim), F32),
+            jax.ShapeDtypeStruct(w.shape, BF),
+            jax.ShapeDtypeStruct((1, dim), F32),
+        ],
+        in_specs=[whole_spec()] * 8,
+        out_specs=[whole_spec()] * 3,
+        scratch_shapes=[
+            pltpu.VMEM((rows, dim), BF),
+            pltpu.VMEM((rows, dim), BF),
+            pltpu.SemaphoreType.DMA((CHUNKS,)),
+            pltpu.SemaphoreType.DMA((CHUNKS,)),
+        ],
+        compiler_params=pltpu.CompilerParams(collective_id=3, has_side_effects=True, vmem_limit_bytes=VMEM_LIMIT),
+        name="qkv_back",
+    )(dq, dk, dv, w, xn, x, gain, gm)
+
+
+def tables(time_ids):
+    half = HEAD // 2
+    freqs = jnp.exp(jnp.arange(half, dtype=F32) * (-2.0 * math.log(10000.0) / HEAD))
+    angles = time_ids.astype(F32)[:, None] * freqs[None, :]
+    cosine = jnp.cos(angles)
+    sine = jnp.sin(angles)
+    return jnp.tile(cosine, (1, 4)), jnp.tile(jnp.concatenate([-sine, sine], axis=1), (1, 2))
+
+
+def mask_tables(segments, variates, head_bias):
+    lane = jnp.arange(LANES)[None, :]
+    var_here = (lane % VAR_COLS == variates[:, None]) & (lane < 3 * VAR_COLS)
+    seg_here = (lane - SEG_COL == segments[:, None]) & (lane >= SEG_COL) & (lane < ONE_COL)
+    seg_cols = (lane >= SEG_COL) & (lane < ONE_COL)
+    ones = (lane >= ONE_COL) & (lane < ONE_COL + 3)
+    base = jnp.where(var_here, 1.0, 0.0)
+    segq = jnp.where(seg_cols & ~seg_here, MASKED, 0.0)
+    extk = jnp.where(var_here | seg_here | ones, 1.0, 0.0).astype(BF)
+    gap = head_bias[0] - head_bias[1]
+    hi = lax.reduce_precision(gap, 8, 7)
+    mid = lax.reduce_precision(gap - hi, 8, 7)
+    low = gap - hi - mid
+    kind = lane // VAR_COLS
+    rows = jnp.where(kind == 0, hi[:, None], jnp.where(kind == 1, mid[:, None], jnp.where(kind == 2, low[:, None], 0.0)))
+    match = jnp.arange(8)[:, None] == variates[None, :]
+    valid = jnp.arange(8)[:, None] < VAR_COLS
+    onehot = jnp.stack([jnp.where(match, 1.0, 0.0), jnp.where(valid & ~match, 1.0, 0.0)])
+    return base, segq, extk, rows.reshape(-1, 2, LANES), onehot
+
+
+def fast_local(
+    block_input, segments, variates, time_ids, attn_gain, w_qkv, head_bias, w_out, ffn_gain, w_gate_up, w_down, cotangent
+):
+    w3 = jnp.transpose(w_qkv, (1, 0, 2))
+    cosine, sine = tables(time_ids)
+    base, segq, extk, bias_rows, onehot = mask_tables(segments, variates, head_bias)
+    gain1 = attn_gain[None, :]
+    gain2 = ffn_gain[None, :]
+    xn, q, k, v = qkv_call(block_input, gain1, w3, cosine, sine)
+    attended, o32, extq = attn_fwd_call(q, k, v, base, segq, extk, bias_rows)
+    mid, xn2 = attn_out_call(block_input, attended, w_out, gain2)
+    ffn_part, gx_part, g_down, g_gate, g_up = ffn_call(xn2, cotangent, w_gate_up[:, 0], w_gate_up[:, 1], w_down)
+    block_output, grad_mid, do, g_out, g_gain2 = ffn_back_call(gx_part, ffn_part, mid, cotangent, gain2, w_out, attended)
+    dq, dk, dv, gb = attn_bwd_call(q, k, v, do, o32, extq, extk, onehot, cosine, sine)
+    input_grad, g_qkv, g_gain1 = qkv_back_call(dq, dk, dv, w3, xn, block_input, gain1, grad_mid)
+    g_bias = jnp.sum(gb, axis=(3, 4)).reshape(-1, 2).T
+    return block_output, input_grad, g_gain1[0], g_qkv, g_bias, g_out, g_gain2[0], g_gate, g_up, g_down
 
 
 def rope_tables(time_ids, head_dim):
@@ -50,7 +543,7 @@
     return (rows_now * inverse * gain, inverse)
 
 
-def norm_back(rows_now, inverse, gain, grads):
+def plain_norm_back(rows_now, inverse, gain, grads):
     scaled = grads * gain
     gain_grad = jnp.sum(grads * rows_now * inverse, axis=0)
     rows_grad = inverse * scaled - rows_now * (inverse * inverse * inverse) * jnp.mean(
@@ -70,7 +563,7 @@
     return jnp.where(allowed[:, None], biased, MASKED)
 
 
-def local(
+def plain_local(
     block_input,
     segments,
     variates,
@@ -153,7 +646,7 @@
         ).astype(jnp.bfloat16),
         "tensor",
     ).astype(jnp.float32)
-    norm_grad_mid, grad_ffn_gain = norm_back(mid_rows, ffn_inverse, ffn_gain, grad_ffn_normed)
+    norm_grad_mid, grad_ffn_gain = plain_norm_back(mid_rows, ffn_inverse, ffn_gain, grad_ffn_normed)
     grad_mid = cotangent.astype(jnp.float32) + norm_grad_mid
     grad_branch = grad_mid.astype(jnp.bfloat16)
     grad_w_out = jnp.einsum("tk,td->kd", attended, grad_branch, preferred_element_type=jnp.float32)
@@ -212,7 +705,7 @@
         ),
         "tensor",
     ).astype(jnp.float32)
-    norm_grad_input, grad_attn_gain = norm_back(
+    norm_grad_input, grad_attn_gain = plain_norm_back(
         input_rows, attn_inverse, attn_gain, grad_attn_normed
     )
     input_grad = grad_mid + norm_grad_input
@@ -243,35 +736,37 @@
     )
 
 
+def solution_local(*args):
+    block_output, input_grad, g_gain1, g_qkv, g_bias, g_out, g_gain2, g_gate, g_up, g_down = fast_local(*args)
+    g_gate, g_up, g_down = lax.psum((g_gate, g_up, g_down), "dp")
+    g_qkv, g_out = lax.psum((g_qkv, g_out), "dp")
+    g_gain1, g_bias, g_gain2 = lax.psum((g_gain1, g_bias, g_gain2), "dp")
+    return (
+        block_output,
+        input_grad,
+        g_gain1,
+        jnp.transpose(g_qkv, (1, 0, 2)).astype(F32),
+        g_bias,
+        g_out.astype(F32),
+        g_gain2,
+        jnp.stack([g_gate, g_up], axis=1).astype(F32),
+        g_down.astype(F32),
+    )
+
+
 def solution(mesh):
     placed = (
-        P("dp", None),
-        P("dp"),
-        P("dp"),
-        P("dp"),
-        P(),
-        P(None, None, "tensor"),
-        P(None, "tensor"),
-        P("tensor", None),
-        P(),
-        P(None, None, "tensor"),
-        P("tensor", None),
-        P("dp", None),
-    )
+        P("dp", None), P("dp"), P("dp"), P("dp"), P(), P(None, None, "tensor"), P(None, "tensor"),
+        P("tensor", None), P(), P(None, None, "tensor"), P("tensor", None), P("dp", None),
+    )
+    fast = mesh.shape["tensor"] == 2
     return jax.shard_map(
-        local,
+        solution_local if fast else plain_local,
         mesh=mesh,
         in_specs=placed,
         out_specs=(
-            P("dp", None),
-            P("dp", None),
-            P(),
-            P(None, None, "tensor"),
-            P(None, "tensor"),
-            P("tensor", None),
-            P(),
-            P(None, None, "tensor"),
-            P("tensor", None),
+            P("dp", None), P("dp", None), P(), P(None, None, "tensor"), P(None, "tensor"), P("tensor", None), P(),
+            P(None, None, "tensor"), P("tensor", None),
         ),
         check_vma=False,
     )

time: 1270 us -> 719 us (0.57)
  waiting for transfers between devices: 843 us -> 418 us
  matrix products: 233 us -> 0 us
  Pallas kernels: 0 us -> 145 us
  other arithmetic: 77 us -> 24.1 us
    psum x4 -> x1, waiting for transfers between devices: 843 us -> 418 us  [solution_local(): g_qkv, g_out = lax.psum((g_qkv, g_out), 'dp')]
    dot_general x20 -> x0, matrix products: 233 us -> none  [the longest x1 22.5 us: local(): jnp.einsum('sqhd,skhd->shqk', grad_attended, values, preferred_element_ty...]
    pallas_call x0 -> x7, Pallas kernels: none -> 145 us  [the longest x1 50.2 us: ffn_call(): pl.pallas_call(ffn_body, grid=(hidden // blk,), out_shape=[jax.ShapeDtype...]
    reduce_sum x5 -> x1, other arithmetic: 27.7 us -> 0.11 us  [fast_local(): g_bias = jnp.sum(gb, axis=(3, 4)).reshape(-1, 2).T]
    slice x2 -> x1, local copies, waits for them, and re-layouts: 0.47 us -> 16.2 us  [fast_local(): w_gate_up[:, 1]]
    unnamed x92 -> x25, local copies, waits for them, and re-layouts: 41.1 us -> 33.8 us
    convert_element_type x2 -> x6, other arithmetic: 28.1 us -> 22 us  [the longest x1 10.3 us: solution_local(): jnp.stack([g_gate, g_up], axis=1).astype(F32)]
  transfers between devices with their start and end apart: 4 -> 1, of which waited for: 3 -> 1; matrix products, arithmetic and copies ran while one was open for 7% -> 0% of each run, Pallas kernels for 0% -> 0%
where the time goes in v1:
time: 719 us; the launch traced here: 710 us
  waiting for transfers between devices  418 us (58%)
  Pallas kernels  145 us (20%)
  local copies, waits for them, and re-layouts  60 us (8%)
  blocking collectives  48.3 us (7%)
  other arithmetic  24.1 us (3%)
  between operations  14.7 us (2%)
    psum x1, waiting for transfers between devices, solution_local(): g_qkv, g_out = lax.psum((g_qkv, g_out), 'dp')  418 us
    pallas_call x1, Pallas kernels, ffn_call(): pl.pallas_call(ffn_body, grid=(hidden // blk,), out_shape=[jax.ShapeDtype...  50.2 us
    psum x1, blocking collectives, solution_local(): g_gain1, g_bias, g_gain2 = lax.psum((g_gain1, g_bias, g_gain2), 'dp')  48.3 us
    unnamed x25, local copies, waits for them, and re-layouts  33.8 us
    pallas_call x1, Pallas kernels, attn_bwd_call(): pl.pallas_call(attn_bwd_body, grid=(pairs,), out_shape=[jax.ShapeDtypeStr...  27.4 us
    pallas_call x1, Pallas kernels, qkv_back_call(): pl.pallas_call(qkv_back_body, out_shape=[jax.ShapeDtypeStruct((rows, dim)...  18.7 us
    slice x1, local copies, waits for them, and re-layouts, fast_local(): w_gate_up[:, 1]  16.2 us
    pallas_call x1, Pallas kernels, ffn_back_call(): pl.pallas_call(ffn_back_body, out_shape=[jax.ShapeDtypeStruct((rows, dim)...  15.5 us
  transfers between devices with their start and end apart: 1, of which 1 were waited for; matrix products, arithmetic and copies ran while one was open for 0% of the time, Pallas kernels for 0%

profile of v1, /device:TPU:0, one launch (start us, length us, event | category | flops | bytes accessed | tf_op | source)
XLA Modules:
  0.0 710.2 jit_solution(5460525127112552180)
XLA Ops:
  7.3 0.7 convert_element_type.21
  8.6 1.0 copy.32.sin_ref
  9.7 1.0 copy.31.cos_ref
  10.9 16.2 %fusion.7 = (bf16[1024,1,2048]{2,1,0:T(2,128)(2,1)S(1)}, bf16[1024,1,2048]{2,1,0:T(2,128)(2,1)S(1)}) fusion(bf16[1024,2,2048]{2,1,0:T(2,128)(2,1)} %param.21), kind=kLoop, calls=%fused_computation.38 | loop fusion | bytes 16777216 | tf_op jit(solution)/shard_map/slice | solution.py:500
  27.1 7.7 %copy_bitcast_fusion = (bf16[1024,2048]{1,0:T(8,128)(2,1)}, bf16[1024,2048]{1,0:T(8,128)(2,1)}) fusion(bf16[1024,1,2048]{2,1,0:T(2,128)(2,1)S(1)} %get-tuple-element.96, bf16[1024,1,2048]{2,1,0:T(2,128)(2,1)S(1)} %get-tuple-element.97), kind=kLoop, calls=%fused_computation.1 | loop fusion | bytes 16777216 | tf_op jit(solution)/shard_map/squeeze | solution.py:500
  35.5 7.9 %qkv.1 = (bf16[1024,1024]{1,0:T(8,128)(2,1)}, bf16[1024,512]{1,0:T(8,128)(2,1)}, bf16[1024,512]{1,0:T(8,128)(2,1)}, bf16[1024,512]{1,0:T(8,128)(2,1)}) custom-call(bf16[1024,1024]{1,0:T(8,128)(2,1)} %x_ref.5, f32[1,1024]{1,0:T(1,128)} %bitcast.26, bf16[3,1024,512]{2,1,0:T(8,128)(2,1)} %bitcast.16, f32[1024,128]{1,0:T(8,128)} %copy.31.cos_ref, ...), custom_call_target="tpu_custom_call" | custom-call | tf_op jit(solution)/shard_map/qkv/pallas_call | solution.py:75
  44.1 1.4 select_convert_fusion
  45.5 15.5 %attn_fwd.1 = (bf16[1024,512]{1,0:T(8,128)(2,1)}, f32[1024,512]{1,0:T(8,128)}, bf16[4,2,1024,128]{3,2,1,0:T(8,128)(2,1)}) custom-call(bf16[1024,512]{1,0:T(8,128)(2,1)} %get-tuple-element.35.q_ref, bf16[1024,512]{1,0:T(8,128)(2,1)} %get-tuple-element.36.k_ref, bf16[1024,512]{1,0:T(8,128)(2,1)} %get-tuple-element.37.v_ref, ...), custom_call_target="tpu_custom_call" | custom-call | tf_op jit(solution)/shard_map/attn_fwd/pallas_call | solution.py:131
  60.9 9.8 %attn_out.1 = (f32[1024,1024]{1,0:T(8,128)}, bf16[1024,1024]{1,0:T(8,128)(2,1)}) custom-call(bf16[1024,1024]{1,0:T(8,128)(2,1)} %x_ref.5, bf16[1024,512]{1,0:T(8,128)(2,1)} %get-tuple-element.38.o_ref.at_ref, bf16[512,1024]{1,0:T(8,128)(2,1)} %w_ref.3, f32[1,1024]{1,0:T(1,128)} %bitcast.23), custom_call_target="tpu_custom_call" | custom-call | tf_op jit(solution)/shard_map/attn_out/pallas_call | solution.py:258
  70.8 50.2 %ffn.1 = (bf16[1024,1024]{1,0:T(8,128)(2,1)}, bf16[1024,1024]{1,0:T(8,128)(2,1)}, bf16[2048,1024]{1,0:T(8,128)(2,1)}, bf16[1024,2048]{1,0:T(8,128)(2,1)}, bf16[1024,2048]{1,0:T(8,128)(2,1)}) custom-call(bf16[1024,1024]{1,0:T(8,128)(2,1)} %get-tuple-element.39.xn_ref, bf16[1024,1024]{1,0:T(8,128)(2,1)} %ct_ref.3, ...), custom_call_target="tpu_custom_call" | custom-call | tf_op jit(solution)/shard_map/ffn/pallas_call | solution.py:320
  120.9 15.5 %ffn_back.1 = (bf16[1024,1024]{1,0:T(8,128)(2,1)}, f32[1024,1024]{1,0:T(8,128)}, bf16[1024,512]{1,0:T(8,128)(2,1)}, bf16[512,1024]{1,0:T(8,128)(2,1)}, f32[1,1024]{1,0:T(1,128)}) custom-call(bf16[1024,1024]{1,0:T(8,128)(2,1)} %get-tuple-element.40.gx_ref, bf16[1024,1024]{1,0:T(8,128)(2,1)} %get-tuple-element.41.fo_ref, ...), custom_call_target="tpu_custom_call" | custom-call | tf_op jit(solution)/shard_map/ffn_back/pallas_call | solution.py:384
  136.5 27.4 %attn_bwd.1 = (bf16[1024,512]{1,0:T(8,128)(2,1)}, bf16[1024,512]{1,0:T(8,128)(2,1)}, bf16[1024,512]{1,0:T(8,128)(2,1)}, f32[4,2,2,8,256]{4,3,2,1,0:T(8,128)}) custom-call(bf16[1024,512]{1,0:T(8,128)(2,1)} %get-tuple-element.35.q_ref, bf16[1024,512]{1,0:T(8,128)(2,1)} %get-tuple-element.36.k_ref, bf16[1024,512]{1,0:T(8,128)(2,1)} %get-tuple-element.37.v_ref, ...), custom_call_target="tpu_custom_call" | custom-call | tf_op jit(solution)/shard_map/attn_bwd/pallas_call | solution.py:198
  163.8 18.7 %qkv_back.1 = (f32[1024,1024]{1,0:T(8,128)}, bf16[3,1024,512]{2,1,0:T(8,128)(2,1)}, f32[1,1024]{1,0:T(1,128)}) custom-call(bf16[1024,512]{1,0:T(8,128)(2,1)} %get-tuple-element.47.dq_ref, bf16[1024,512]{1,0:T(8,128)(2,1)} %get-tuple-element.48.dk_ref, bf16[1024,512]{1,0:T(8,128)(2,1)} %get-tuple-element.49.dv_ref, bf16[3,1024,512]{2,1,0:T(8,128)(2,1)} %bitcast.17, ...), custom_call_target="tpu_custom_call" | custom-call | tf_op jit(solution)/shard_map/qkv_back/pallas_call | solution.py:439
  182.6 0.9 copy-done.5
  183.7 48.3 %all-reduce = (f32[1024]{0:T(1024)}, f32[2,8]{1,0:T(2,128)}, f32[1024]{0:T(1024)}) all-reduce(f32[1024]{0:T(1024)S(1)} %bitcast.30, f32[2,8]{1,0:T(2,128)S(1)} %bitcast.28, f32[1024]{0:T(1024)S(1)} %bitcast.29), channel_id=1, replica_groups=mesh['dp'=16,'tensor'=2] {'dp'}, use_global_device_ids=true, to_apply=%region_0.1 | all-reduce | flops 2064 | bytes 16512 | tf_op jit(solution)/shard_map/psum | solution.py:743
  232.0 418.1 %all-reduce.4.cloned.1.call-done = (bf16[1024,3,512]{2,0,1:T(8,128)(2,1)}, bf16[512,1024]{1,0:T(8,128)(2,1)}, bf16[1024,1,2048]{2,0,1:T(8,128)(2,1)}, bf16[1024,1,2048]{2,0,1:T(8,128)(2,1)}, bf16[2048,1024]{1,0:T(8,128)(2,1)}) async-done(((bf16[1024,3,512]{2,0,1:T(8,128)(2,1)}, bf16[512,1024]{1,0:T(8,128)(2,1)}, bf16[1024,1,2048]{2,0,1:T(8,128)(2,1)}, bf16[1024,1,2048]{2,0,1:T(8,128)(2,1)}, ...) | async-done | bytes 16777232 | tf_op jit(solution)/shard_map/psum | solution.py:742
  650.1 10.3 %maximum_convert_fusion = f32[1024,2,2048]{2,0,1:T(8,128)} fusion(bf16[1024,1,2048]{2,0,1:T(8,128)(2,1)} %get-tuple-element.93, bf16[1024,1,2048]{2,0,1:T(8,128)(2,1)} %get-tuple-element.94), kind=kLoop, calls=%fused_computation | loop fusion | flops 8388608 | bytes 25165824 | tf_op jit(solution)/shard_map/convert_element_type | solution.py:752
  660.4 28.7 %copy.38 = f32[1024,2,2048]{2,1,0:T(2,128)} copy(f32[1024,2,2048]{2,0,1:T(8,128)} %maximum_convert_fusion) | data formatting | bytes 33554432
  689.1 4.4 convert_element_type.27
  693.6 3.6 convert_element_type.24
  697.2 1.6 convert_element_type.25
  698.7 1.3 copy.51
  700.1 0.8 copy-done.1
  700.9 2.0 copy.52
  (42 shorter events, 2.5 us)
Async XLA Ops:
  7.2 3.6 copy-start.10
  7.2 642.9 %all-reduce.4.cloned.1.call-start = ((), (), s32[]{:S(2)}) async-start(), calls=%async_computation | async-start | bytes 33554432 | tf_op jit(solution)/shard_map/psum | solution.py:742
  27.1 7.7 %copy-start.6 = (s32[1024]{0:T(1024)S(1)}, s32[1024]{0:T(1024)}, u32[]{:S(2)}) copy-start(s32[1024]{0:T(1024)} %param.14) | copy-start | bytes 12292
  34.8 9.3 %copy-start.7 = (s32[1024]{0:T(1024)S(1)}, s32[1024]{0:T(1024)}, u32[]{:S(2)}) copy-start(s32[1024]{0:T(1024)} %param.13) | copy-start | bytes 12292
  182.6 0.9 copy-start.5
  182.6 1.1 copy-start.8
  182.6 1.1 copy-start.9
  660.4 28.7 %copy-start = (bf16[2048,1024]{1,0:T(8,128)(2,1)S(1)}, bf16[2048,1024]{1,0:T(8,128)(2,1)}, u32[]{:S(2)}) copy-start(bf16[2048,1024]{1,0:T(8,128)(2,1)} %get-tuple-element.95) | copy-start | bytes 12582916
  689.1 4.5 copy-start.2
  693.6 3.6 copy-start.4
  693.6 5.2 copy-start.3
  697.2 3.7 copy-start.1
Sparse Core Ops, SparseCore 0:
  182.7 467.2 all-reduce.3

commit v2 on v1

--- a/solution.py
+++ b/solution.py
@@ -20,6 +20,12 @@
 VAR_COLS = 4
 SEG_COL = 12
 ONE_COL = 20
+ROWS = 32
+LAG = 2
+HALF_ROWS = 512
+GROUP_ROWS = 4 * HALF_ROWS
+WIDE = 1024
+SMALL = 8
 
 
 def dot_nn(a, b):
@@ -271,7 +277,10 @@
     )(x, o, w, gain)
 
 
-def ffn_body(xn_ref, ct_ref, wg_ref, wu_ref, wd_ref, out_ref, gx_ref, gd_ref, gg_ref, gu_ref, acc_o, acc_g, hid, dg, du):
+def ffn_body(
+    bits, xn_ref, ct_ref, wg_ref, wu_ref, wd_ref,
+    out_ref, gx_ref, gd_ref, gk_ref, gs_ref, uk_ref, us_ref, acc_o, acc_g, hid, dg, du,
+):
     j = pl.program_id(0)
     rows = xn_ref.shape[0]
     blk = 256
@@ -300,9 +309,19 @@
         du[sl, :] = dup
         acc_o[sl, :] += dot_nn(hidden, wd)
         acc_g[sl, :] += dot_nt(dgate, wg) + dot_nt(dup, wu)
-    gd_ref[...] = dot_tn(hid[...], ct_ref[...]).astype(BF)
-    gg_ref[...] = dot_tn(xn_ref[...], dg[...]).astype(BF)
-    gu_ref[...] = dot_tn(xn_ref[...], du[...]).astype(BF)
+    gd_ref[0, 0] = dot_tn(hid[...], ct_ref[...]).astype(BF)
+    for part, keep, send, bit in ((dg, gk_ref, gs_ref, bits[0]), (du, uk_ref, us_ref, bits[1])):
+        grad = dot_tn(xn_ref[...], part[...]).astype(BF)
+
+        @pl.when(bit == 0)
+        def _():
+            keep[0] = grad[:HALF_ROWS]
+            send[0] = grad[HALF_ROWS:]
+
+        @pl.when(bit == 1)
+        def _():
+            keep[0] = grad[HALF_ROWS:]
+            send[0] = grad[:HALF_ROWS]
 
     @pl.when(j == pl.num_programs(0) - 1)
     def _():
@@ -310,29 +329,96 @@
         gx_ref[...] = acc_g[...].astype(BF)
 
 
-def ffn_call(xn, ct, wg, wu, wd):
+def ffn_call(xn, ct, wg, wu, wd, bits):
     rows, dim = xn.shape
     hidden = wd.shape[0]
     blk = 256
-    full = pl.BlockSpec((rows, dim), lambda j: (0, 0))
-    colw = pl.BlockSpec((dim, blk), lambda j: (0, j))
-    roww = pl.BlockSpec((blk, dim), lambda j: (j, 0))
+    full = pl.BlockSpec((rows, dim), lambda j, b: (0, 0))
+    colw = pl.BlockSpec((dim, blk), lambda j, b: (0, j))
+    roww = pl.BlockSpec((blk, dim), lambda j, b: (j, 0))
+    grad = pl.BlockSpec((1, HALF_ROWS, blk), lambda j, b: (j // 4, 0, lax.rem(j, 4)))
+
+    def down_at(j, b):
+        group = j // 4
+        half = lax.rem(j, 4) // 2
+        bit = jnp.where(group == 0, b[0], b[1])
+        return (jnp.where(half == bit, 0, 1), group, lax.rem(j, 2), 0)
+
     return pl.pallas_call(
         ffn_body,
-        grid=(hidden // blk,),
+        grid_spec=pltpu.PrefetchScalarGridSpec(
+            num_scalar_prefetch=1,
+            grid=(hidden // blk,),
+            in_specs=[full, full, colw, colw, roww],
+            out_specs=[full, full, pl.BlockSpec((1, 1, blk, dim), down_at), grad, grad, grad, grad],
+            scratch_shapes=[pltpu.VMEM((rows, dim), F32)] * 2 + [pltpu.VMEM((rows, blk), BF)] * 3,
+        ),
         out_shape=[
             jax.ShapeDtypeStruct((rows, dim), BF),
             jax.ShapeDtypeStruct((rows, dim), BF),
-            jax.ShapeDtypeStruct((hidden, dim), BF),
-            jax.ShapeDtypeStruct((dim, hidden), BF),
-            jax.ShapeDtypeStruct((dim, hidden), BF),
-        ],
-        in_specs=[full, full, colw, colw, roww],
-        out_specs=[full, full, roww, colw, colw],
-        scratch_shapes=[pltpu.VMEM((rows, dim), F32)] * 2 + [pltpu.VMEM((rows, blk), BF)] * 3,
+            jax.ShapeDtypeStruct((2, 2, HALF_ROWS, dim), BF),
+        ]
+        + [jax.ShapeDtypeStruct((2, HALF_ROWS, dim), BF)] * 4,
         compiler_params=pltpu.CompilerParams(vmem_limit_bytes=VMEM_LIMIT),
         name="ffn",
-    )(xn, ct, wg, wu, wd)
+    )(bits, xn, ct, wg, wu, wd)
+
+
+def pair_rows(w):
+    dim, two, width = w.shape
+    return jnp.transpose(w.reshape(dim, two, width // LANES, LANES), (0, 2, 1, 3)).reshape(-1, LANES)
+
+
+def split_body(w_ref, wg_ref, wu_ref, wide):
+    rows = wg_ref.shape[0]
+    tiles = wg_ref.shape[1] // LANES
+    wide[...] = w_ref[...].astype(F32)
+    for c, out in ((0, wg_ref), (1, wu_ref)):
+        for s in range(tiles):
+            out[:, s * LANES : (s + 1) * LANES] = wide[pl.ds(2 * s + c, rows, stride=2 * tiles), :].astype(BF)
+
+
+def split_call(w):
+    dim, _, width = w.shape
+    blk = 64
+    flat = blk * 2 * width // LANES
+    return pl.pallas_call(
+        split_body,
+        grid=(dim // blk,),
+        out_shape=[jax.ShapeDtypeStruct((dim, width), BF)] * 2,
+        in_specs=[pl.BlockSpec((flat, LANES), lambda i: (i, 0))],
+        out_specs=[pl.BlockSpec((blk, width), lambda i: (i, 0))] * 2,
+        scratch_shapes=[pltpu.VMEM((flat, LANES), F32)],
+        compiler_params=pltpu.CompilerParams(vmem_limit_bytes=VMEM_LIMIT),
+        name="split_gate_up",
+    )(pair_rows(w))
+
+
+def join_body(a_ref, b_ref, out_ref):
+    rows = a_ref.shape[2]
+    tiles = WIDE // LANES
+    for f in range(2):
+        for s in range(tiles):
+            for c, src in ((0, a_ref), (1, b_ref)):
+                at = (f * tiles + s) * 2 + c
+                out_ref[pl.ds(at, rows, stride=4 * tiles), :] = src[0, f, :, s * LANES : (s + 1) * LANES].astype(F32)
+
+
+def join_call(a, b):
+    blk = 64
+    tiles = 4 * WIDE // LANES
+    half = pl.BlockSpec((1, 2, blk, WIDE), lambda i: (i // (HALF_ROWS // blk), 0, lax.rem(i, HALF_ROWS // blk), 0))
+    flat = pl.pallas_call(
+        join_body,
+        grid=(2 * HALF_ROWS // blk,),
+        out_shape=jax.ShapeDtypeStruct((2 * HALF_ROWS * tiles, LANES), F32),
+        in_specs=[half, half],
+        out_specs=pl.BlockSpec((blk * tiles, LANES), lambda i: (i, 0)),
+        compiler_params=pltpu.CompilerParams(vmem_limit_bytes=VMEM_LIMIT),
+        name="join_gate_up",
+    )(a, b)
+    split = flat.reshape(2 * HALF_ROWS, tiles // 2, 2, LANES)
+    return jnp.transpose(split, (0, 2, 1, 3)).reshape(2 * HALF_ROWS, 2, 2 * WIDE)
 
 
 def norm_back(rows_now, gain, grads):
@@ -344,8 +430,7 @@
 
 
 def ffn_back_body(
-    gx_ref, fo_ref, mid_ref, ct_ref, gain_ref, w_ref, at_ref,
-    out_ref, gm_ref, do_ref, gw_ref, gg_ref, gx_in, fo_in, gb, ssem, rsem,
+    gx_ref, fo_ref, mid_ref, ct_ref, gain_ref, w_ref, out_ref, gm_ref, do_ref, gg_ref, gx_in, fo_in, ssem, rsem
 ):
     peer = partner_barrier()
     rows = mid_ref.shape[0]
@@ -366,10 +451,8 @@
         gain_sum = gain_sum + gain_grad
         gm = ct_ref[sl, :].astype(F32) + back
         gm_ref[sl, :] = gm
-        gb[sl, :] = gm.astype(BF)
-        do_ref[sl, :] = dot_nt(gb[sl, :], w_ref[...]).astype(BF)
+        do_ref[sl, :] = dot_nt(gm.astype(BF), w_ref[...]).astype(BF)
     gg_ref[...] = gain_sum
-    gw_ref[...] = dot_tn(at_ref[...], gb[...]).astype(BF)
     for c in range(CHUNKS):
         sl = slice(c * blk, (c + 1) * blk)
         copies[CHUNKS + c].wait_recv()
@@ -378,7 +461,7 @@
         copy.wait_send()
 
 
-def ffn_back_call(gx, fo, mid, ct, gain, w, at):
+def ffn_back_call(gx, fo, mid, ct, gain, w):
     rows, dim = mid.shape
     width = w.shape[0]
     return pl.pallas_call(
@@ -387,13 +470,11 @@
             jax.ShapeDtypeStruct((rows, dim), BF),
             jax.ShapeDtypeStruct((rows, dim), F32),
             jax.ShapeDtypeStruct((rows, width), BF),
-            jax.ShapeDtypeStruct((width, dim), BF),
             jax.ShapeDtypeStruct((1, dim), F32),
         ],
-        in_specs=[whole_spec()] * 7,
-        out_specs=[whole_spec()] * 5,
+        in_specs=[whole_spec()] * 6,
+        out_specs=[whole_spec()] * 4,
         scratch_shapes=[
-            pltpu.VMEM((rows, dim), BF),
             pltpu.VMEM((rows, dim), BF),
             pltpu.VMEM((rows, dim), BF),
             pltpu.SemaphoreType.DMA((2 * CHUNKS,)),
@@ -401,14 +482,17 @@
         ],
         compiler_params=pltpu.CompilerParams(collective_id=2, has_side_effects=True, vmem_limit_bytes=VMEM_LIMIT),
         name="ffn_back",
-    )(gx, fo, mid, ct, gain, w, at)
-
-
-def qkv_back_body(dq_ref, dk_ref, dv_ref, w_ref, xn_ref, x_ref, gain_ref, gm_ref, ig_ref, gw_ref, gg_ref, mine, theirs, ssem, rsem):
+    )(gx, fo, mid, ct, gain, w)
+
+
+def qkv_back_body(
+    dq_ref, dk_ref, dv_ref, w_ref, xn_ref, x_ref, gain_ref, gm_ref, at_ref,
+    ig_ref, qk_ref, vo_ref, gg_ref, mine, theirs, ssem, rsem,
+):
     peer = partner_barrier()
     rows = x_ref.shape[0]
     blk = rows // CHUNKS
-    parts = (dq_ref, dk_ref, dv_ref)
+    width = dq_ref.shape[1]
     copies = []
     for c in range(CHUNKS):
         sl = slice(c * blk, (c + 1) * blk)
@@ -419,8 +503,12 @@
         copy = send_rows(mine, theirs, pl.ds(c * blk, blk), ssem.at[c], rsem.at[c], peer)
         copy.start()
         copies.append(copy)
-    for n in range(3):
-        gw_ref[n] = dot_tn(xn_ref[...], parts[n][...]).astype(BF)
+    qk_ref[:, :width] = dot_tn(xn_ref[...], dq_ref[...]).astype(BF)
+    qk_ref[:, width:] = dot_tn(xn_ref[...], dk_ref[...]).astype(BF)
+    grad_v = dot_tn(xn_ref[...], dv_ref[...]).astype(BF)
+    vo_ref[:HALF_ROWS, :width] = grad_v[:HALF_ROWS]
+    vo_ref[:HALF_ROWS, width:] = grad_v[HALF_ROWS:]
+    vo_ref[HALF_ROWS:, :] = dot_tn(at_ref[...], gm_ref[...].astype(BF)).astype(BF)
     gain_sum = jnp.zeros((1, x_ref.shape[1]), F32)
     for c in range(CHUNKS):
         sl = slice(c * blk, (c + 1) * blk)
@@ -434,17 +522,18 @@
         copy.wait_send()
 
 
-def qkv_back_call(dq, dk, dv, w, xn, x, gain, gm):
+def qkv_back_call(dq, dk, dv, w, xn, x, gain, gm, at):
     rows, dim = x.shape
     return pl.pallas_call(
         qkv_back_body,
         out_shape=[
             jax.ShapeDtypeStruct((rows, dim), F32),
-            jax.ShapeDtypeStruct(w.shape, BF),
+            jax.ShapeDtypeStruct((dim, dim), BF),
+            jax.ShapeDtypeStruct((dim, dim), BF),
             jax.ShapeDtypeStruct((1, dim), F32),
         ],
-        in_specs=[whole_spec()] * 8,
-        out_specs=[whole_spec()] * 3,
+        in_specs=[whole_spec()] * 9,
+        out_specs=[whole_spec()] * 4,
         scratch_shapes=[
             pltpu.VMEM((rows, dim), BF),
             pltpu.VMEM((rows, dim), BF),
@@ -453,7 +542,249 @@
         ],
         compiler_params=pltpu.CompilerParams(collective_id=3, has_side_effects=True, vmem_limit_bytes=VMEM_LIMIT),
         name="qkv_back",
-    )(dq, dk, dv, w, xn, x, gain, gm)
+    )(dq, dk, dv, w, xn, x, gain, gm, at)
+
+
+def peers_of(dp):
+    z = dp // 4
+    y = (dp // 2) % 2
+    x = dp % 2
+    at = lambda zz, yy, xx: zz * 4 + yy * 2 + xx
+    return z, y, x, at(z, y, 1 - x), at(z, 1 - y, x), at(z + 1 - 2 * (z % 2), y, x), at(3 - z, y, x)
+
+
+def sum_body(
+    gk, rg, uk, ru, dk, rda, rdb, qk, vo, small_in, out_a, out_b, small_out,
+    L, S, Z, R, Y, F, sb, st, loc, s1s, s1r, sends, zr, rr, yr, ar, xr, lo, ss, sr,
+):
+    dp = lax.axis_index("dp")
+    t = lax.axis_index("tensor")
+    z, y, x, px, py, zn, mm = peers_of(dp)
+    is_mid = (z == 1) | (z == 2)
+    is_end = (z == 0) | (z == 3)
+    mine = jnp.where(z == 2, WIDE // 2, 0)
+    others = WIDE // 2 - mine
+    n = GROUP_ROWS // ROWS
+    first = (px, py)
+    last = (py, px)
+    outs = (out_a, out_b)
+    owner = (x, y)
+
+    def remote(src, dst, ssem, rsem, peer):
+        return pltpu.make_async_remote_copy(
+            src_ref=src, dst_ref=dst, send_sem=ssem, recv_sem=rsem, device_id=(peer, t), device_id_type=MESH
+        )
+
+    def loads(g, b):
+        rows = pl.ds(b * HALF_ROWS, HALF_ROWS)
+        if b < 2:
+            srcs = ((gk, uk)[g].at[b], (rg, ru)[g].at[b])
+        elif b == 2:
+            srcs = (dk.at[0, g], (rda, rdb)[g].at[...])
+        else:
+            srcs = ((qk, vo)[g].at[pl.ds(pl.multiple_of(owner[g] * HALF_ROWS, HALF_ROWS), HALF_ROWS)],)
+        return [
+            pltpu.make_async_copy(src, (L, S)[k].at[g, rows], loc.at[g, b, k]) for k, src in enumerate(srcs)
+        ]
+
+    for b in range(4):
+        for g in range(2):
+            for copy in loads(g, b):
+                copy.start()
+
+    barrier = pltpu.get_barrier_semaphore()
+    others_z = [lax.rem(z + k, 4) * 4 + y * 2 + x for k in range(1, 4)]
+    for peer in [px, py] + others_z:
+        pl.semaphore_signal(barrier, inc=1, device_id=(peer, t), device_id_type=MESH)
+    pl.semaphore_wait(barrier, 5)
+
+    def first_exchange(g):
+        away = pl.ds(pl.multiple_of((1 - owner[g]) * HALF_ROWS, HALF_ROWS), HALF_ROWS)
+        return remote(
+            (qk, vo)[g].at[away], S.at[g, pl.ds(3 * HALF_ROWS, HALF_ROWS)], s1s.at[g], s1r.at[g], first[g]
+        )
+
+    small_x = remote(small_in, sb.at[0], ss.at[0], sr.at[0], px)
+    small_y = remote(st.at[0], sb.at[1], ss.at[1], sr.at[1], py)
+    small_z = [remote(st.at[1], sb.at[2 + z], ss.at[2 + k], sr.at[2 + z], others_z[k]) for k in range(3)]
+    small_x.start()
+    for g in range(2):
+        first_exchange(g).start()
+
+    def rows_of(i):
+        return pl.ds(pl.multiple_of(i * ROWS, ROWS), ROWS)
+
+    def cols_of(at):
+        return pl.ds(pl.multiple_of(at, WIDE // 2), WIDE // 2)
+
+    def z_copy(g, i):
+        return remote(L.at[g, rows_of(i)], Z.at[g, rows_of(i)], sends.at[g, 0], zr.at[g, i], zn)
+
+    def r_copy(g, i):
+        return remote(L.at[g, rows_of(i), cols_of(others)], R.at[g, rows_of(i)], sends.at[g, 1], rr.at[g, i], mm)
+
+    def y_copy(g, i):
+        return remote(R.at[g, rows_of(i)], Y.at[g, rows_of(i)], sends.at[g, 2], yr.at[g, i], last[g])
+
+    def a_copy(g, i, at):
+        return remote(F.at[g, rows_of(i), cols_of(at)], F.at[g, rows_of(i), cols_of(at)], sends.at[g, 3], ar.at[g, i], mm)
+
+    def o_copy(g, i):
+        return remote(F.at[g, rows_of(i)], F.at[g, rows_of(i)], sends.at[g, 4], zr.at[g, i], zn)
+
+    def x_copy(g, i):
+        return remote(F.at[g, rows_of(i)], outs[g].at[owner[g], rows_of(i)], sends.at[g, 5], xr.at[g], first[g])
+
+    def l_copy(g, i):
+        return pltpu.make_async_copy(F.at[g, rows_of(i)], outs[g].at[owner[g], rows_of(i)], lo.at[g])
+
+    def body(i, carry):
+        @pl.when((i < n) & (lax.rem(i, n // 4) == 0))
+        def _():
+            for b in range(4):
+                @pl.when(i == b * (n // 4))
+                def _():
+                    for g in range(2):
+                        for copy in loads(g, b):
+                            copy.wait()
+                        if b == 3:
+                            first_exchange(g).wait_recv()
+
+        @pl.when(is_end & (i < n))
+        def _():
+            for g in range(2):
+                r = rows_of(i)
+                L[g, r, :] = (L[g, r, :].astype(F32) + S[g, r, :].astype(F32)).astype(BF)
+                z_copy(g, i).start()
+
+        @pl.when(is_mid)
+        def _():
+            j = i - 4 * LAG
+
+            @pl.when((j >= 0) & (j < n))
+            def _():
+                for g in range(2):
+                    a_copy(g, j, others).wait_recv()
+                    o_copy(g, j).start()
+                    x_copy(g, j).start()
+                    l_copy(g, j).start()
+
+            j3 = i - 3 * LAG
+
+            @pl.when((j3 >= 0) & (j3 < n))
+            def _():
+                for g in range(2):
+                    y_copy(g, j3).wait_recv()
+                    r = rows_of(j3)
+                    F[g, r, cols_of(mine)] = (R[g, r, :].astype(F32) + Y[g, r, :].astype(F32)).astype(BF)
+                    a_copy(g, j3, mine).start()
+
+            j2 = i - 2 * LAG
+
+            @pl.when((j2 >= 0) & (j2 < n))
+            def _():
+                for g in range(2):
+                    r_copy(g, j2).wait_recv()
+                    r = rows_of(j2)
+                    R[g, r, :] = (R[g, r, :].astype(F32) + L[g, r, cols_of(mine)].astype(F32)).astype(BF)
+                    y_copy(g, j2).start()
+
+            j1 = i - LAG
+
+            @pl.when((j1 >= 0) & (j1 < n))
+            def _():
+                for g in range(2):
+                    z_copy(g, j1).wait_recv()
+                    r = rows_of(j1)
+                    L[g, r, :] = (L[g, r, :].astype(F32) + S[g, r, :].astype(F32) + Z[g, r, :].astype(F32)).astype(BF)
+                    r_copy(g, j1).start()
+
+        @pl.when(is_end)
+        def _():
+            j = i - 5 * LAG
+
+            @pl.when((j >= 0) & (j < n))
+            def _():
+                for g in range(2):
+                    o_copy(g, j).wait_recv()
+                    x_copy(g, j).start()
+                    l_copy(g, j).start()
+
+        @pl.when(i == n // 8)
+        def _():
+            small_x.wait_recv()
+            st[0] = small_in[...] + sb[0]
+            small_y.start()
+
+        @pl.when(i == n // 4)
+        def _():
+            small_y.wait_recv()
+            st[1] = st[0] + sb[1]
+            for copy in small_z:
+                copy.start()
+
+        return carry
+
+    lax.fori_loop(0, n + 5 * LAG, body, 0)
+
+    for k in range(3):
+        remote(st.at[1], sb.at[2 + lax.rem(z + k + 1, 4)], ss.at[2 + k], sr.at[2 + lax.rem(z + k + 1, 4)], others_z[k]).wait_recv()
+    sb[2 + z] = st[1]
+    small_out[...] = (sb[2] + sb[3]) + (sb[4] + sb[5])
+
+    small_x.wait_send()
+    small_y.wait_send()
+    for copy in small_z:
+        copy.wait_send()
+    for g in range(2):
+        first_exchange(g).wait_send()
+        away = 1 - owner[g]
+
+        @pl.when(is_end)
+        def _():
+            remote(L.at[g], Z.at[g], sends.at[g, 0], zr.at[g, 0], zn).wait_send()
+
+        @pl.when(is_mid)
+        def _():
+            half = pl.ds(0, WIDE // 2)
+            remote(R.at[g], Y.at[g], sends.at[g, 1], rr.at[g, 0], mm).wait_send()
+            remote(R.at[g], Y.at[g], sends.at[g, 2], yr.at[g, 0], last[g]).wait_send()
+            remote(R.at[g], Y.at[g], sends.at[g, 3], ar.at[g, 0], mm).wait_send()
+            remote(F.at[g], F.at[g], sends.at[g, 4], zr.at[g, 0], zn).wait_send()
+
+        whole = remote(F.at[g], outs[g].at[away], sends.at[g, 5], xr.at[g], first[g])
+        whole.wait_send()
+        whole.wait_recv()
+        pltpu.make_async_copy(F.at[g], outs[g].at[owner[g]], lo.at[g]).wait()
+
+
+def sum_call(gk, rg, uk, ru, dk, rda, rdb, qk, vo, small):
+    any_spec = pl.BlockSpec(memory_space=pl.ANY)
+    n = GROUP_ROWS // ROWS
+    full = pltpu.VMEM((2, GROUP_ROWS, WIDE), BF)
+    half = pltpu.VMEM((2, GROUP_ROWS, WIDE // 2), BF)
+    dma = pltpu.SemaphoreType.DMA
+    return pl.pallas_call(
+        sum_body,
+        out_shape=[jax.ShapeDtypeStruct((2, GROUP_ROWS, WIDE), BF)] * 2 + [jax.ShapeDtypeStruct((SMALL, WIDE), F32)],
+        in_specs=[any_spec] * 9 + [whole_spec()],
+        out_specs=[any_spec] * 2 + [whole_spec()],
+        scratch_shapes=[
+            full, full, full, half, half, full,
+            pltpu.VMEM((6, SMALL, WIDE), F32),
+            pltpu.VMEM((2, SMALL, WIDE), F32),
+            dma((2, 4, 2)), dma((2,)), dma((2,)), dma((2, 6)),
+            dma((2, n)), dma((2, n)), dma((2, n)), dma((2, n)),
+            dma((2,)), dma((2,)), dma((5,)), dma((6,)),
+        ],
+        compiler_params=pltpu.CompilerParams(collective_id=4, has_side_effects=True, vmem_limit_bytes=VMEM_LIMIT),
+        name="grad_sum",
+    )(gk, rg, uk, ru, dk, rda, rdb, qk, vo, small)
+
+
+def first_swap(sends, bit):
+    pairs = [(d, d ^ bit) for d in range(16)]
+    return [lax.ppermute(s, "dp", pairs) for s in sends]
 
 
 def tables(time_ids):
@@ -489,20 +820,42 @@
 def fast_local(
     block_input, segments, variates, time_ids, attn_gain, w_qkv, head_bias, w_out, ffn_gain, w_gate_up, w_down, cotangent
 ):
+    dp = lax.axis_index("dp")
+    bits = jnp.stack([dp % 2, (dp // 2) % 2]).astype(jnp.int32)
     w3 = jnp.transpose(w_qkv, (1, 0, 2))
     cosine, sine = tables(time_ids)
     base, segq, extk, bias_rows, onehot = mask_tables(segments, variates, head_bias)
     gain1 = attn_gain[None, :]
     gain2 = ffn_gain[None, :]
+    wg, wu = split_call(w_gate_up)
     xn, q, k, v = qkv_call(block_input, gain1, w3, cosine, sine)
     attended, o32, extq = attn_fwd_call(q, k, v, base, segq, extk, bias_rows)
     mid, xn2 = attn_out_call(block_input, attended, w_out, gain2)
-    ffn_part, gx_part, g_down, g_gate, g_up = ffn_call(xn2, cotangent, w_gate_up[:, 0], w_gate_up[:, 1], w_down)
-    block_output, grad_mid, do, g_out, g_gain2 = ffn_back_call(gx_part, ffn_part, mid, cotangent, gain2, w_out, attended)
+    ffn_part, gx_part, down, gk, gs, uk, us = ffn_call(xn2, cotangent, wg, wu, w_down, bits)
+    rg, rda = first_swap([gs, down[1, 0]], 1)
+    ru, rdb = first_swap([us, down[1, 1]], 2)
+    block_output, grad_mid, do, g_gain2 = ffn_back_call(gx_part, ffn_part, mid, cotangent, gain2, w_out)
     dq, dk, dv, gb = attn_bwd_call(q, k, v, do, o32, extq, extk, onehot, cosine, sine)
-    input_grad, g_qkv, g_gain1 = qkv_back_call(dq, dk, dv, w3, xn, block_input, gain1, grad_mid)
+    input_grad, qk, vo, g_gain1 = qkv_back_call(dq, dk, dv, w3, xn, block_input, gain1, grad_mid, attended)
     g_bias = jnp.sum(gb, axis=(3, 4)).reshape(-1, 2).T
-    return block_output, input_grad, g_gain1[0], g_qkv, g_bias, g_out, g_gain2[0], g_gate, g_up, g_down
+    heads = g_bias.shape[1]
+    bias_row = jnp.pad(g_bias.reshape(1, -1), ((0, 0), (0, WIDE - 2 * heads)))
+    small = jnp.concatenate([g_gain1, g_gain2, bias_row, jnp.zeros((SMALL - 3, WIDE), F32)], axis=0)
+    sum_a, sum_b, small = sum_call(gk, rg, uk, ru, down, rda, rdb, qk, vo, small)
+    sum_a = sum_a.reshape(2, 4, HALF_ROWS, WIDE)
+    sum_b = sum_b.reshape(2, 4, HALF_ROWS, WIDE)
+    width = w_qkv.shape[2]
+    g_gate_up = join_call(sum_a, sum_b)
+    g_down = jnp.stack([sum_a[:, 2], sum_b[:, 2]]).astype(F32).reshape(w_down.shape)
+    qk = sum_a[:, 3].reshape(2 * HALF_ROWS, WIDE)
+    v_rows = sum_b[0, 3]
+    v_cols = jnp.concatenate([v_rows[:, :width], v_rows[:, width:]], axis=0)
+    g_qkv = jnp.stack([qk[:, :width], qk[:, width:], v_cols]).astype(F32)
+    g_out = sum_b[1, 3].astype(F32)
+    g_bias = small[2, : 2 * heads].reshape(2, heads)
+    return (
+        block_output, input_grad, small[0], jnp.transpose(g_qkv, (1, 0, 2)), g_bias, g_out, small[1], g_gate_up, g_down,
+    )
 
 
 def rope_tables(time_ids, head_dim):
@@ -736,32 +1089,14 @@
     )
 
 
-def solution_local(*args):
-    block_output, input_grad, g_gain1, g_qkv, g_bias, g_out, g_gain2, g_gate, g_up, g_down = fast_local(*args)
-    g_gate, g_up, g_down = lax.psum((g_gate, g_up, g_down), "dp")
-    g_qkv, g_out = lax.psum((g_qkv, g_out), "dp")
-    g_gain1, g_bias, g_gain2 = lax.psum((g_gain1, g_bias, g_gain2), "dp")
-    return (
-        block_output,
-        input_grad,
-        g_gain1,
-        jnp.transpose(g_qkv, (1, 0, 2)).astype(F32),
-        g_bias,
-        g_out.astype(F32),
-        g_gain2,
-        jnp.stack([g_gate, g_up], axis=1).astype(F32),
-        g_down.astype(F32),
-    )
-
-
 def solution(mesh):
     placed = (
         P("dp", None), P("dp"), P("dp"), P("dp"), P(), P(None, None, "tensor"), P(None, "tensor"),
         P("tensor", None), P(), P(None, None, "tensor"), P("tensor", None), P("dp", None),
     )
-    fast = mesh.shape["tensor"] == 2
+    fast = (mesh.shape["dp"], mesh.shape["tensor"]) == (16, 2)
     return jax.shard_map(
-        solution_local if fast else plain_local,
+        fast_local if fast else plain_local,
         mesh=mesh,
         in_specs=placed,
         out_specs=(

time: 719 us -> 484 us (0.67)
  waiting for transfers between devices: 418 us -> 0.01 us
  Pallas kernels: 145 us -> 434 us
  blocking collectives: 48.3 us -> 0 us
  local copies, waits for them, and re-layouts: 60 us -> 22.5 us
  between operations: 14.7 us -> 1.13 us
    psum x1 -> x0, waiting for transfers between devices: 418 us -> none  [solution_local(): g_qkv, g_out = lax.psum((g_qkv, g_out), 'dp')]
    pallas_call x1 -> x4, Pallas kernels: 50.2 us -> 327 us  [the longest x1 227 us: sum_call(): pl.pallas_call(sum_body, out_shape=[jax.ShapeDtypeStruct((2, GROUP_ROWS,...]
    psum x1 -> x0, blocking collectives: 48.3 us -> none  [solution_local(): g_gain1, g_bias, g_gain2 = lax.psum((g_gain1, g_bias, g_gain2), 'dp')]
    unnamed x25 -> x24, local copies, waits for them, and re-layouts: 33.8 us -> 9.54 us
    slice x1 -> x3, local copies, waits for them, and re-layouts: 16.2 us -> 2.19 us  [the longest x1 1.44 us: fast_local(): small[1]]
    pallas_call x1, Pallas kernels: 27.4 us -> 39.1 us  [attn_bwd_call(): pl.pallas_call(attn_bwd_body, grid=(pairs,), out_shape=[jax.ShapeDtypeStr...]
    convert_element_type x4 -> x2, other arithmetic: 19.9 us -> 8.22 us  [the longest x1 4.72 us: fast_local(): jnp.stack([sum_a[:, 2], sum_b[:, 2]]).astype(F32).reshape(w_down.shape)]
  transfers between devices with their start and end apart: 1 -> 4, of which waited for: 1 -> 0; matrix products, arithmetic and copies ran while one was open for 0% -> 1% of each run, Pallas kernels for 0% -> 15%
where the time goes in v2:
time: 484 us; the launch traced here: 482 us
  Pallas kernels  434 us (90%)
  local copies, waits for them, and re-layouts  22.5 us (5%)
  other arithmetic  18.8 us (4%)
  starting transfers between devices  5.06 us (1%)
    pallas_call x1, Pallas kernels, sum_call(): pl.pallas_call(sum_body, out_shape=[jax.ShapeDtypeStruct((2, GROUP_ROWS,...  227 us
    pallas_call x1, Pallas kernels, ffn_call(): pl.pallas_call(ffn_body, grid_spec=pltpu.PrefetchScalarGridSpec(num_scala...  62.1 us
    pallas_call x1, Pallas kernels, attn_bwd_call(): pl.pallas_call(attn_bwd_body, grid=(pairs,), out_shape=[jax.ShapeDtypeStr...  39.1 us
    pallas_call x1, Pallas kernels, join_call(): pl.pallas_call(join_body, grid=(2 * HALF_ROWS // blk,), out_shape=jax.Sha...  21.6 us
    pallas_call x1, Pallas kernels, qkv_back_call(): pl.pallas_call(qkv_back_body, out_shape=[jax.ShapeDtypeStruct((rows, dim)...  19.9 us
    pallas_call x1, Pallas kernels, split_call(): pl.pallas_call(split_body, grid=(dim // blk,), out_shape=[jax.ShapeDtypeS...  16.8 us
    pallas_call x1, Pallas kernels, attn_fwd_call(): pl.pallas_call(attn_fwd_body, grid=(pairs,), out_shape=[jax.ShapeDtypeStr...  15.4 us
    pallas_call x1, Pallas kernels, ffn_back_call(): pl.pallas_call(ffn_back_body, out_shape=[jax.ShapeDtypeStruct((rows, dim)...  14.8 us
  transfers between devices with their start and end apart: 4, of which 0 were waited for; matrix products, arithmetic and copies ran while one was open for 1% of the time, Pallas kernels for 15%

profile of v2, /device:TPU:0, one launch (start us, length us, event | category | flops | bytes accessed | tf_op | source)
XLA Modules:
  0.0 481.5 jit_solution(18375231840201489927)
XLA Ops:
  5.0 16.8 %split_gate_up.1 = (bf16[1024,2048]{1,0:T(8,128)(2,1)}, bf16[1024,2048]{1,0:T(8,128)(2,1)}) custom-call(bf16[32768,128]{1,0:T(8,128)(2,1)} %bitcast.60), custom_call_target="tpu_custom_call" | custom-call | tf_op jit(solution)/shard_map/split_gate_up/pallas_call | solution.py:385
  22.4 7.9 %qkv.1 = (bf16[1024,1024]{1,0:T(8,128)(2,1)}, bf16[1024,512]{1,0:T(8,128)(2,1)}, bf16[1024,512]{1,0:T(8,128)(2,1)}, bf16[1024,512]{1,0:T(8,128)(2,1)}) custom-call(bf16[1024,1024]{1,0:T(8,128)(2,1)} %x_ref.5, f32[1,1024]{1,0:T(1,128)} %bitcast.67, bf16[3,1024,512]{2,1,0:T(8,128)(2,1)} %bitcast.58, f32[1024,128]{1,0:T(8,128)} %copy.31.cos_ref, ...), custom_call_target="tpu_custom_call" | custom-call | tf_op jit(solution)/shard_map/qkv/pallas_call | solution.py:81
  31.0 1.4 select_convert_fusion
  32.4 15.4 %attn_fwd.1 = (bf16[1024,512]{1,0:T(8,128)(2,1)}, f32[1024,512]{1,0:T(8,128)}, bf16[4,2,1024,128]{3,2,1,0:T(8,128)(2,1)}) custom-call(bf16[1024,512]{1,0:T(8,128)(2,1)} %get-tuple-element.42.q_ref, bf16[1024,512]{1,0:T(8,128)(2,1)} %get-tuple-element.43.k_ref, bf16[1024,512]{1,0:T(8,128)(2,1)} %get-tuple-element.44.v_ref, ...), custom_call_target="tpu_custom_call" | custom-call | tf_op jit(solution)/shard_map/attn_fwd/pallas_call | solution.py:137
  47.9 9.8 %attn_out.1 = (f32[1024,1024]{1,0:T(8,128)}, bf16[1024,1024]{1,0:T(8,128)(2,1)}) custom-call(bf16[1024,1024]{1,0:T(8,128)(2,1)} %x_ref.5, bf16[1024,512]{1,0:T(8,128)(2,1)} %get-tuple-element.45.o_ref.at_ref, bf16[512,1024]{1,0:T(8,128)(2,1)} %w_ref.3, f32[1,1024]{1,0:T(1,128)} %bitcast.64), custom_call_target="tpu_custom_call" | custom-call | tf_op jit(solution)/shard_map/attn_out/pallas_call | solution.py:264
  57.7 62.1 %ffn.1 = (bf16[1024,1024]{1,0:T(8,128)(2,1)}, bf16[1024,1024]{1,0:T(8,128)(2,1)}, bf16[2,2,512,1024]{3,2,1,0:T(8,128)(2,1)}, bf16[2,512,1024]{2,1,0:T(8,128)(2,1...) custom-call(s32[2]{0:T(128)} %pad_add_fusion.bits, ...), custom_call_target="tpu_custom_call" | custom-call | tf_op jit(solution)/shard_map/ffn/pallas_call | solution.py:347
  119.8 3.0 collective-permute-start
  122.8 1.5 collective-permute-start.1
  124.3 3.1 slice_bitcast_fusion.6
  128.0 14.8 %ffn_back.1 = (bf16[1024,1024]{1,0:T(8,128)(2,1)}, f32[1024,1024]{1,0:T(8,128)}, bf16[1024,512]{1,0:T(8,128)(2,1)}, f32[1,1024]{1,0:T(1,128)}) custom-call(bf16[1024,1024]{1,0:T(8,128)(2,1)} %get-tuple-element.49.gx_ref, bf16[1024,1024]{1,0:T(8,128)(2,1)} %get-tuple-element.50.fo_ref, f32[1024,1024]{1,0:T(8,128)} %get-tuple-element.51.mid_ref, ...), custom_call_target="tpu_custom_call" | custom-call | tf_op jit(solution)/shard_map/ffn_back/pallas_call | solution.py:467
  143.5 39.1 %attn_bwd.1 = (bf16[1024,512]{1,0:T(8,128)(2,1)}, bf16[1024,512]{1,0:T(8,128)(2,1)}, bf16[1024,512]{1,0:T(8,128)(2,1)}, f32[4,2,2,8,256]{4,3,2,1,0:T(8,128)}) custom-call(bf16[1024,512]{1,0:T(8,128)(2,1)} %get-tuple-element.42.q_ref, bf16[1024,512]{1,0:T(8,128)(2,1)} %get-tuple-element.43.k_ref, bf16[1024,512]{1,0:T(8,128)(2,1)} %get-tuple-element.44.v_ref, ...), custom_call_target="tpu_custom_call" | custom-call | tf_op jit(solution)/shard_map/attn_bwd/pallas_call | solution.py:204
  182.6 19.9 %qkv_back.1 = (f32[1024,1024]{1,0:T(8,128)}, bf16[1024,1024]{1,0:T(8,128)(2,1)}, bf16[1024,1024]{1,0:T(8,128)(2,1)}, f32[1,1024]{1,0:T(1,128)}) custom-call(bf16[1024,512]{1,0:T(8,128)(2,1)} %get-tuple-element.56.dq_ref, bf16[1024,512]{1,0:T(8,128)(2,1)} %get-tuple-element.57.dk_ref, bf16[1024,512]{1,0:T(8,128)(2,1)} %get-tuple-element.58.dv_ref, ...), custom_call_target="tpu_custom_call" | custom-call | tf_op jit(solution)/shard_map/qkv_back/pallas_call | solution.py:527
  206.0 226.5 %grad_sum.1 = (bf16[2,2048,1024]{2,1,0:T(8,128)(2,1)}, bf16[2,2048,1024]{2,1,0:T(8,128)(2,1)}, f32[8,1024]{1,0:T(8,128)}) custom-call(bf16[2,512,1024]{2,1,0:T(8,128)(2,1)} %get-tuple-element.62.gk, bf16[2,512,1024]{2,1,0:T(8,128)(2,1)} %copy-done.4, bf16[2,512,1024]{2,1,0:T(8,128)(2,1)} %get-tuple-element.64.uk, ...), custom_call_target="tpu_custom_call" | custom-call | tf_op jit(solution)/shard_map/grad_sum/pallas_call | solution.py:767
  433.2 1.4 fusion.11
  434.6 1.9 slice_bitcast_fusion
  436.5 3.5 fusion
  440.0 2.5 slice_bitcast_fusion.1
  442.5 21.6 %join_gate_up.1 = f32[32768,128]{1,0:T(8,128)} custom-call(bf16[2,4,512,1024]{3,2,1,0:T(8,128)(2,1)} %bitcast.52, bf16[2,4,512,1024]{3,2,1,0:T(8,128)(2,1)} %bitcast.56), custom_call_target="tpu_custom_call" | custom-call | tf_op jit(solution)/shard_map/join_gate_up/pallas_call | solution.py:411
  464.9 1.5 copy-done.1
  466.5 1.4 copy-done.2
  468.4 4.7 bitcast_convert_fusion
  473.2 3.2 convert_bitcast_fusion
  477.7 1.6 copy-done.3
  479.3 2.0 copy.44
  (60 shorter events, 13.6 us)
Async XLA Ops:
  22.4 8.6 %copy-start.8 = (s32[1024]{0:T(1024)S(1)}, s32[1024]{0:T(1024)}, u32[]{:S(2)}) copy-start(s32[1024]{0:T(1024)} %param.14) | copy-start | bytes 12292
  22.4 8.6 %copy-start.9 = (s32[1024]{0:T(1024)S(1)}, s32[1024]{0:T(1024)}, u32[]{:S(2)}) copy-start(s32[1024]{0:T(1024)} %param.13) | copy-start | bytes 12292
  119.8 84.5 %collective-permute-start = (bf16[2,512,1024]{2,1,0:T(8,128)(2,1)}, bf16[2,512,1024]{2,1,0:T(8,128)(2,1)S(1)}, u32[]{:S(2)}, u32[]{:S(2)}) collective-permute-start(bf16[2,512,1024]{2,1,0:T(8,128)(2,1)} %get-tuple-element.63), channel_id=1, source_target_pairs={{0,2},{2,0},{4,6},{6,4},{8,10},{10,8},{12,14},{14,12},{16,18},{18,... | collective-permute-start | bytes 6291464 | tf_op jit(solution)/shard_map/ppermute | solution.py:787
  122.8 81.5 %collective-permute-start.1 = (bf16[2,512,1024]{2,1,0:T(8,128)(2,1)}, bf16[2,512,1024]{2,1,0:T(8,128)(2,1)}, u32[]{:S(2)}, u32[]{:S(2)}) collective-permute-start(bf16[2,512,1024]{2,1,0:T(8,128)(2,1)} %get-tuple-element.65), channel_id=1, source_target_pairs={{0,4},{2,6},{4,0},{6,2},{8,12},{10,14},{12,8},{14,10},{16,20},{18,... | collective-permute-start | bytes 6291464 | tf_op jit(solution)/shard_map/ppermute | solution.py:787
  127.4 76.9 %collective-permute-start.3 = (bf16[512,1024]{1,0:T(8,128)(2,1)}, bf16[512,1024]{1,0:T(8,128)(2,1)S(1)}, u32[]{:S(2)}, u32[]{:S(2)}) collective-permute-start(bf16[512,1024]{1,0:T(8,128)(2,1)} %get-tuple-element.79), channel_id=1, source_target_pairs={{0,4},{2,6},{4,0},{6,2},{8,12},{10,14},{12,8},{14,10},{16,20},{18,... | collective-permute-start | bytes 3145736 | tf_op jit(solution)/shard_map/ppermute | solution.py:787
  127.9 76.4 %collective-permute-start.2 = (bf16[512,1024]{1,0:T(8,128)(2,1)}, bf16[512,1024]{1,0:T(8,128)(2,1)}, u32[]{:S(2)}, u32[]{:S(2)}) collective-permute-start(bf16[512,1024]{1,0:T(8,128)(2,1)} %get-tuple-element.80), channel_id=1, source_target_pairs={{0,2},{2,0},{4,6},{6,4},{8,10},{10,8},{12,14},{14,12},{16,18},{18,... | collective-permute-start | bytes 3145736 | tf_op jit(solution)/shard_map/ppermute | solution.py:787
  182.6 19.9 %copy-start.7 = (f32[4,2,2,8,256]{4,3,2,1,0:T(8,128)S(1)}, f32[4,2,2,8,256]{4,3,2,1,0:T(8,128)}, u32[]{:S(2)}) copy-start(f32[4,2,2,8,256]{4,3,2,1,0:T(8,128)} %get-tuple-element.71) | copy-start | bytes 393220
  182.6 20.3 %copy-start.10 = (f32[1,1024]{1,0:T(1,128)S(1)}, f32[1,1024]{1,0:T(1,128)}, u32[]{:S(2)}) copy-start(f32[1,1024]{1,0:T(1,128)} %get-tuple-element.70) | copy-start | bytes 12292
  204.3 1.0 copy-start.6
  204.3 1.6 copy-start.4
  434.6 5.4 %copy-start = (bf16[2,2048,1024]{2,1,0:T(8,128)(2,1)S(1)}, bf16[2,2048,1024]{2,1,0:T(8,128)(2,1)}, u32[]{:S(2)}) copy-start(bf16[2,2048,1024]{2,1,0:T(8,128)(2,1)} %get-tuple-element.73) | copy-start | bytes 25165828
  464.8 1.6 copy-start.1
  466.4 1.6 copy-start.2
  473.1 3.2 copy-start.5
  476.3 2.9 copy-start.3

commit v3 on v2

--- a/solution.py
+++ b/solution.py
@@ -20,12 +20,14 @@
 VAR_COLS = 4
 SEG_COL = 12
 ONE_COL = 20
-ROWS = 32
-LAG = 2
+ROWS = 16
+LAG = 3
 HALF_ROWS = 512
 GROUP_ROWS = 4 * HALF_ROWS
 WIDE = 1024
 SMALL = 8
+FFN_ROWS = 256
+FFN_COLS = 512
 
 
 def dot_nn(a, b):
@@ -95,8 +97,15 @@
     )(x, gain, w, cosine, sine)
 
 
-def attn_fwd_body(q_ref, k_ref, v_ref, base_ref, segq_ref, extk_ref, bias_ref, o_ref, o32_ref, extq_ref):
+def attn_fwd_body(
+    q_ref, k_ref, v_ref, base_ref, segq_ref, extk_ref, bias_ref, w_ref, o_ref, o32_ref, extq_ref, wg_ref, wu_ref
+):
     rows = q_ref.shape[0]
+    for t in range(w_ref.shape[1] // 8):
+        turned = jnp.swapaxes(w_ref[:, t * 8 : (t + 1) * 8, :].astype(F32), 0, 1)
+        for k in range(8):
+            s = t * 4 + k // 2
+            (wg_ref, wu_ref)[k % 2][:, s * LANES : (s + 1) * LANES] = turned[k].astype(BF)
     blk = 256
     lane = lax.broadcasted_iota(jnp.int32, (blk, LANES), 1)
     kx = jnp.concatenate([k_ref[...], extk_ref[...]], axis=1)
@@ -129,9 +138,12 @@
         o_ref[sl, :] = o.astype(BF)
 
 
-def attn_fwd_call(q, k, v, base, segq, extk, bias_rows):
+def attn_fwd_call(q, k, v, base, segq, extk, bias_rows, w_pairs):
     rows, width = q.shape
     pairs = width // LANES
+    dim, tiles, _ = w_pairs.shape
+    share = dim // pairs
+    half_w = pl.BlockSpec((share, tiles * LANES // 2), lambda p: (p, 0))
     col = pl.BlockSpec((rows, LANES), lambda p: (0, p))
     full = pl.BlockSpec((rows, LANES), lambda p: (0, 0))
     return pl.pallas_call(
@@ -141,12 +153,18 @@
             jax.ShapeDtypeStruct((rows, width), BF),
             jax.ShapeDtypeStruct((rows, width), F32),
             jax.ShapeDtypeStruct((pairs, 2, rows, LANES), BF),
-        ],
-        in_specs=[col, col, col, full, full, full, pl.BlockSpec((1, 2, LANES), lambda p: (p, 0, 0))],
-        out_specs=[col, col, pl.BlockSpec((1, 2, rows, LANES), lambda p: (p, 0, 0, 0))],
+            jax.ShapeDtypeStruct((dim, tiles * LANES // 2), BF),
+            jax.ShapeDtypeStruct((dim, tiles * LANES // 2), BF),
+        ],
+        in_specs=[
+            col, col, col, full, full, full,
+            pl.BlockSpec((1, 2, LANES), lambda p: (p, 0, 0)),
+            pl.BlockSpec((share, tiles, LANES), lambda p: (p, 0, 0)),
+        ],
+        out_specs=[col, col, pl.BlockSpec((1, 2, rows, LANES), lambda p: (p, 0, 0, 0)), half_w, half_w],
         compiler_params=pltpu.CompilerParams(vmem_limit_bytes=VMEM_LIMIT),
         name="attn_fwd",
-    )(q, k, v, base, segq, extk, bias_rows)
+    )(q, k, v, base, segq, extk, bias_rows, w_pairs)
 
 
 def attn_bwd_body(
@@ -279,16 +297,17 @@
 
 def ffn_body(
     bits, xn_ref, ct_ref, wg_ref, wu_ref, wd_ref,
-    out_ref, gx_ref, gd_ref, gk_ref, gs_ref, uk_ref, us_ref, acc_o, acc_g, hid, dg, du,
+    out_ref, gx_ref, gd_ref, gk_ref, gs_ref, uk_ref, us_ref, acc_o, acc_g, hid, dg, du, xt,
 ):
     j = pl.program_id(0)
     rows = xn_ref.shape[0]
-    blk = 256
+    blk = FFN_ROWS
 
     @pl.when(j == 0)
     def _():
         acc_o[...] = jnp.zeros_like(acc_o)
         acc_g[...] = jnp.zeros_like(acc_g)
+        xt[...] = xn_ref[...].T
 
     wg = wg_ref[...]
     wu = wu_ref[...]
@@ -311,17 +330,9 @@
         acc_g[sl, :] += dot_nt(dgate, wg) + dot_nt(dup, wu)
     gd_ref[0, 0] = dot_tn(hid[...], ct_ref[...]).astype(BF)
     for part, keep, send, bit in ((dg, gk_ref, gs_ref, bits[0]), (du, uk_ref, us_ref, bits[1])):
-        grad = dot_tn(xn_ref[...], part[...]).astype(BF)
-
-        @pl.when(bit == 0)
-        def _():
-            keep[0] = grad[:HALF_ROWS]
-            send[0] = grad[HALF_ROWS:]
-
-        @pl.when(bit == 1)
-        def _():
-            keep[0] = grad[HALF_ROWS:]
-            send[0] = grad[:HALF_ROWS]
+        for out, half in ((keep, bit), (send, 1 - bit)):
+            rows_at = pl.ds(pl.multiple_of(half * HALF_ROWS, HALF_ROWS), HALF_ROWS)
+            out[0] = dot_nn(xt[rows_at, :], part[...]).astype(BF)
 
     @pl.when(j == pl.num_programs(0) - 1)
     def _():
@@ -332,17 +343,18 @@
 def ffn_call(xn, ct, wg, wu, wd, bits):
     rows, dim = xn.shape
     hidden = wd.shape[0]
-    blk = 256
+    blk = FFN_COLS
+    per = WIDE // blk
     full = pl.BlockSpec((rows, dim), lambda j, b: (0, 0))
     colw = pl.BlockSpec((dim, blk), lambda j, b: (0, j))
     roww = pl.BlockSpec((blk, dim), lambda j, b: (j, 0))
-    grad = pl.BlockSpec((1, HALF_ROWS, blk), lambda j, b: (j // 4, 0, lax.rem(j, 4)))
+    grad = pl.BlockSpec((1, HALF_ROWS, blk), lambda j, b: (j // per, 0, lax.rem(j, per)))
 
     def down_at(j, b):
-        group = j // 4
-        half = lax.rem(j, 4) // 2
+        group = j // per
+        half = lax.rem(j, per) // (per // 2)
         bit = jnp.where(group == 0, b[0], b[1])
-        return (jnp.where(half == bit, 0, 1), group, lax.rem(j, 2), 0)
+        return (jnp.where(half == bit, 0, 1), group, lax.rem(j, per // 2), 0)
 
     return pl.pallas_call(
         ffn_body,
@@ -351,7 +363,8 @@
             grid=(hidden // blk,),
             in_specs=[full, full, colw, colw, roww],
             out_specs=[full, full, pl.BlockSpec((1, 1, blk, dim), down_at), grad, grad, grad, grad],
-            scratch_shapes=[pltpu.VMEM((rows, dim), F32)] * 2 + [pltpu.VMEM((rows, blk), BF)] * 3,
+            scratch_shapes=[pltpu.VMEM((rows, dim), F32)] * 2 + [pltpu.VMEM((rows, blk), BF)] * 3
+            + [pltpu.VMEM((dim, rows), BF)],
         ),
         out_shape=[
             jax.ShapeDtypeStruct((rows, dim), BF),
@@ -366,59 +379,61 @@
 
 def pair_rows(w):
     dim, two, width = w.shape
-    return jnp.transpose(w.reshape(dim, two, width // LANES, LANES), (0, 2, 1, 3)).reshape(-1, LANES)
-
-
-def split_body(w_ref, wg_ref, wu_ref, wide):
-    rows = wg_ref.shape[0]
-    tiles = wg_ref.shape[1] // LANES
-    wide[...] = w_ref[...].astype(F32)
-    for c, out in ((0, wg_ref), (1, wu_ref)):
-        for s in range(tiles):
-            out[:, s * LANES : (s + 1) * LANES] = wide[pl.ds(2 * s + c, rows, stride=2 * tiles), :].astype(BF)
-
-
-def split_call(w):
-    dim, _, width = w.shape
-    blk = 64
-    flat = blk * 2 * width // LANES
-    return pl.pallas_call(
-        split_body,
-        grid=(dim // blk,),
-        out_shape=[jax.ShapeDtypeStruct((dim, width), BF)] * 2,
-        in_specs=[pl.BlockSpec((flat, LANES), lambda i: (i, 0))],
-        out_specs=[pl.BlockSpec((blk, width), lambda i: (i, 0))] * 2,
-        scratch_shapes=[pltpu.VMEM((flat, LANES), F32)],
-        compiler_params=pltpu.CompilerParams(vmem_limit_bytes=VMEM_LIMIT),
-        name="split_gate_up",
-    )(pair_rows(w))
-
-
-def join_body(a_ref, b_ref, out_ref):
-    rows = a_ref.shape[2]
+    tiled = jnp.transpose(w.reshape(dim, two, width // LANES, LANES), (0, 2, 1, 3))
+    return tiled.reshape(dim, two * width // LANES, LANES)
+
+
+def widen_body(ga_ref, gb_ref, da_ref, db_ref, aa_ref, v_ref, o_ref, gu_ref, down_ref, qkv_ref, out_ref):
     tiles = WIDE // LANES
     for f in range(2):
-        for s in range(tiles):
-            for c, src in ((0, a_ref), (1, b_ref)):
-                at = (f * tiles + s) * 2 + c
-                out_ref[pl.ds(at, rows, stride=4 * tiles), :] = src[0, f, :, s * LANES : (s + 1) * LANES].astype(F32)
-
-
-def join_call(a, b):
-    blk = 64
+        for q in range(tiles // 4):
+            parts = []
+            for k in range(8):
+                s = q * 4 + k // 2
+                parts.append((ga_ref, gb_ref)[k % 2][0, f, :, s * LANES : (s + 1) * LANES].astype(F32))
+            at = (f * tiles + q * 4) * 2
+            gu_ref[:, at : at + 8, :] = jnp.swapaxes(jnp.stack(parts), 0, 1)
+    down_ref[0, 0] = da_ref[0, 0].astype(F32)
+    down_ref[1, 0] = db_ref[0, 0].astype(F32)
+    width = qkv_ref.shape[2]
+    qkv_ref[0] = aa_ref[0, 0, :, :width].astype(F32)
+    qkv_ref[1] = aa_ref[0, 0, :, width:].astype(F32)
+    qkv_ref[2] = v_ref[0, 0].astype(F32)
+    out_ref[...] = o_ref[0, 0].astype(F32)
+
+
+def widen_call(a, b):
+    blk = 256
+    half = HALF_ROWS // blk
     tiles = 4 * WIDE // LANES
-    half = pl.BlockSpec((1, 2, blk, WIDE), lambda i: (i // (HALF_ROWS // blk), 0, lax.rem(i, HALF_ROWS // blk), 0))
-    flat = pl.pallas_call(
-        join_body,
-        grid=(2 * HALF_ROWS // blk,),
-        out_shape=jax.ShapeDtypeStruct((2 * HALF_ROWS * tiles, LANES), F32),
-        in_specs=[half, half],
-        out_specs=pl.BlockSpec((blk * tiles, LANES), lambda i: (i, 0)),
+    width = WIDE // 2
+    gate = pl.BlockSpec((1, 2, blk, WIDE), lambda i: (i // half, 0, lax.rem(i, half), 0))
+    block = lambda n: pl.BlockSpec((1, 1, blk, WIDE), lambda i: (i // half, n, lax.rem(i, half), 0))
+    gu, down, qkv, out = pl.pallas_call(
+        widen_body,
+        grid=(2 * half,),
+        out_shape=[
+            jax.ShapeDtypeStruct((2 * HALF_ROWS, tiles, LANES), F32),
+            jax.ShapeDtypeStruct((2, 2, HALF_ROWS, WIDE), F32),
+            jax.ShapeDtypeStruct((3, 2 * HALF_ROWS, width), F32),
+            jax.ShapeDtypeStruct((HALF_ROWS, WIDE), F32),
+        ],
+        in_specs=[
+            gate, gate, block(2), block(2), block(3),
+            pl.BlockSpec((1, 1, blk, width), lambda i: (0, 3, lax.rem(i, half), i // half)),
+            pl.BlockSpec((1, 1, blk // 2, WIDE), lambda i: (1, 3, i, 0)),
+        ],
+        out_specs=[
+            pl.BlockSpec((blk, tiles, LANES), lambda i: (i, 0, 0)),
+            pl.BlockSpec((2, 1, blk, WIDE), lambda i: (0, i // half, lax.rem(i, half), 0)),
+            pl.BlockSpec((3, blk, width), lambda i: (0, i, 0)),
+            pl.BlockSpec((blk // 2, WIDE), lambda i: (i, 0)),
+        ],
         compiler_params=pltpu.CompilerParams(vmem_limit_bytes=VMEM_LIMIT),
-        name="join_gate_up",
-    )(a, b)
-    split = flat.reshape(2 * HALF_ROWS, tiles // 2, 2, LANES)
-    return jnp.transpose(split, (0, 2, 1, 3)).reshape(2 * HALF_ROWS, 2, 2 * WIDE)
+        name="widen",
+    )(a, b, a, b, a, b, b)
+    gu = jnp.transpose(gu.reshape(2 * HALF_ROWS, tiles // 2, 2, LANES), (0, 2, 1, 3)).reshape(2 * HALF_ROWS, 2, 2 * WIDE)
+    return gu, down.reshape(4 * HALF_ROWS, WIDE), qkv, out
 
 
 def norm_back(rows_now, gain, grads):
@@ -790,10 +805,9 @@
 def tables(time_ids):
     half = HEAD // 2
     freqs = jnp.exp(jnp.arange(half, dtype=F32) * (-2.0 * math.log(10000.0) / HEAD))
-    angles = time_ids.astype(F32)[:, None] * freqs[None, :]
-    cosine = jnp.cos(angles)
-    sine = jnp.sin(angles)
-    return jnp.tile(cosine, (1, 4)), jnp.tile(jnp.concatenate([-sine, sine], axis=1), (1, 2))
+    angles = time_ids.astype(F32)[:, None] * jnp.tile(freqs, LANES // half)[None, :]
+    sign = jnp.where(jnp.arange(LANES) % HEAD < half, -1.0, 1.0)
+    return jnp.cos(angles), jnp.sin(angles) * sign[None, :]
 
 
 def mask_tables(segments, variates, head_bias):
@@ -827,9 +841,8 @@
     base, segq, extk, bias_rows, onehot = mask_tables(segments, variates, head_bias)
     gain1 = attn_gain[None, :]
     gain2 = ffn_gain[None, :]
-    wg, wu = split_call(w_gate_up)
     xn, q, k, v = qkv_call(block_input, gain1, w3, cosine, sine)
-    attended, o32, extq = attn_fwd_call(q, k, v, base, segq, extk, bias_rows)
+    attended, o32, extq, wg, wu = attn_fwd_call(q, k, v, base, segq, extk, bias_rows, pair_rows(w_gate_up))
     mid, xn2 = attn_out_call(block_input, attended, w_out, gain2)
     ffn_part, gx_part, down, gk, gs, uk, us = ffn_call(xn2, cotangent, wg, wu, w_down, bits)
     rg, rda = first_swap([gs, down[1, 0]], 1)
@@ -844,14 +857,7 @@
     sum_a, sum_b, small = sum_call(gk, rg, uk, ru, down, rda, rdb, qk, vo, small)
     sum_a = sum_a.reshape(2, 4, HALF_ROWS, WIDE)
     sum_b = sum_b.reshape(2, 4, HALF_ROWS, WIDE)
-    width = w_qkv.shape[2]
-    g_gate_up = join_call(sum_a, sum_b)
-    g_down = jnp.stack([sum_a[:, 2], sum_b[:, 2]]).astype(F32).reshape(w_down.shape)
-    qk = sum_a[:, 3].reshape(2 * HALF_ROWS, WIDE)
-    v_rows = sum_b[0, 3]
-    v_cols = jnp.concatenate([v_rows[:, :width], v_rows[:, width:]], axis=0)
-    g_qkv = jnp.stack([qk[:, :width], qk[:, width:], v_cols]).astype(F32)
-    g_out = sum_b[1, 3].astype(F32)
+    g_gate_up, g_down, g_qkv, g_out = widen_call(sum_a, sum_b)
     g_bias = small[2, : 2 * heads].reshape(2, heads)
     return (
         block_output, input_grad, small[0], jnp.transpose(g_qkv, (1, 0, 2)), g_bias, g_out, small[1], g_gate_up, g_down,

time: 484 us -> 437 us (0.903)
  Pallas kernels: 434 us -> 401 us
  local copies, waits for them, and re-layouts: 22.5 us -> 12.9 us
  other arithmetic: 18.8 us -> 9.43 us
    pallas_call x2 -> x1, Pallas kernels: 38.4 us -> 17 us  [widen_call(): pl.pallas_call(widen_body, grid=(2 * half,), out_shape=[jax.ShapeDtypeStr...]
    pallas_call x1, Pallas kernels: 39.1 us -> 27.2 us  [attn_bwd_call(): pl.pallas_call(attn_bwd_body, grid=(pairs,), out_shape=[jax.ShapeDtypeStr...]
    pallas_call x1, Pallas kernels: 62.1 us -> 51.4 us  [ffn_call(): pl.pallas_call(ffn_body, grid_spec=pltpu.PrefetchScalarGridSpec(num_scala...]
    convert_element_type x3 -> x1, other arithmetic: 8.91 us -> 0.69 us  [tables(): time_ids.astype(F32)[:, None] * jnp.tile(freqs, LANES // half)[None, :]]
    pallas_call x1, Pallas kernels: 15.4 us -> 23.1 us  [attn_fwd_call(): pl.pallas_call(attn_fwd_body, grid=(pairs,), out_shape=[jax.ShapeDtypeStr...]
    another operation x7 -> x1, local copies, waits for them, and re-layouts: 6.68 us -> 0.01 us  [tables(): jnp.tile(freqs, LANES // half)[None, :]]
  transfers between devices with their start and end apart: 4 -> 4, of which waited for: 0 -> 1; matrix products, arithmetic and copies ran while one was open for 1% -> 1% of each run, Pallas kernels for 15% -> 14%
where the time goes in v3:
time: 437 us; the launch traced here: 430 us
  Pallas kernels  401 us (92%)
  local copies, waits for them, and re-layouts  12.9 us (3%)
  other arithmetic  9.43 us (2%)
  starting transfers between devices  5.1 us (1%)
    pallas_call x1, Pallas kernels, sum_call(): pl.pallas_call(sum_body, out_shape=[jax.ShapeDtypeStruct((2, GROUP_ROWS,...  230 us
    pallas_call x1, Pallas kernels, ffn_call(): pl.pallas_call(ffn_body, grid_spec=pltpu.PrefetchScalarGridSpec(num_scala...  51.4 us
    pallas_call x1, Pallas kernels, attn_bwd_call(): pl.pallas_call(attn_bwd_body, grid=(pairs,), out_shape=[jax.ShapeDtypeStr...  27.2 us
    pallas_call x1, Pallas kernels, attn_fwd_call(): pl.pallas_call(attn_fwd_body, grid=(pairs,), out_shape=[jax.ShapeDtypeStr...  23.1 us
    pallas_call x1, Pallas kernels, qkv_back_call(): pl.pallas_call(qkv_back_body, out_shape=[jax.ShapeDtypeStruct((rows, dim)...  19.9 us
    pallas_call x1, Pallas kernels, widen_call(): pl.pallas_call(widen_body, grid=(2 * half,), out_shape=[jax.ShapeDtypeStr...  17 us
    pallas_call x1, Pallas kernels, ffn_back_call(): pl.pallas_call(ffn_back_body, out_shape=[jax.ShapeDtypeStruct((rows, dim)...  14.9 us
    pallas_call x1, Pallas kernels, attn_out_call(): pl.pallas_call(attn_out_body, out_shape=[jax.ShapeDtypeStruct((rows, dim)...  9.8 us
  transfers between devices with their start and end apart: 4, of which 1 were waited for; matrix products, arithmetic and copies ran while one was open for 1% of the time, Pallas kernels for 14%

profile of v3, /device:TPU:0, one launch (start us, length us, event | category | flops | bytes accessed | tf_op | source)
XLA Modules:
  0.0 430.0 jit_solution(4701873881329241483)
XLA Ops:
  0.8 0.8 subtract_reduce_fusion
  1.7 0.7 convert_element_type.8
  3.0 3.1 fusion
  6.1 7.9 %qkv.1 = (bf16[1024,1024]{1,0:T(8,128)(2,1)}, bf16[1024,512]{1,0:T(8,128)(2,1)}, bf16[1024,512]{1,0:T(8,128)(2,1)}, bf16[1024,512]{1,0:T(8,128)(2,1)}) custom-call(bf16[1024,1024]{1,0:T(8,128)(2,1)} %x_ref.5, f32[1,1024]{1,0:T(1,128)} %bitcast.40, bf16[3,1024,512]{2,1,0:T(8,128)(2,1)} %bitcast.34, f32[1024,128]{1,0:T(8,128)} %get-tuple-element.91.cos_ref, ...), custom_call_target="tpu_custom_call" | custom-call | tf_op jit(solution)/shard_map/qkv/pallas_call | solution.py:83
  14.7 1.4 select_convert_fusion
  16.1 23.1 %attn_fwd.1 = (bf16[1024,512]{1,0:T(8,128)(2,1)}, f32[1024,512]{1,0:T(8,128)}, bf16[4,2,1024,128]{3,2,1,0:T(8,128)(2,1)}, bf16[1024,2048]{1,0:T(8,128)(2,1)}, bf16[1024,2048]{1,0:T(8,128)(2,1)}) custom-call(bf16[1024,512]{1,0:T(8,128)(2,1)} %get-tuple-element.46.q_ref, bf16[1024,512]{1,0:T(8,128)(2,1)} %get-tuple-element.47.k_ref, ...), custom_call_target="tpu_custom_call" | custom-call | tf_op jit(solution)/shard_map/attn_fwd/pallas_call | solution.py:149
  39.2 9.8 %attn_out.1 = (f32[1024,1024]{1,0:T(8,128)}, bf16[1024,1024]{1,0:T(8,128)(2,1)}) custom-call(bf16[1024,1024]{1,0:T(8,128)(2,1)} %x_ref.5, bf16[1024,512]{1,0:T(8,128)(2,1)} %get-tuple-element.49.o_ref.at_ref, bf16[512,1024]{1,0:T(8,128)(2,1)} %w_ref.3, f32[1,1024]{1,0:T(1,128)} %bitcast.37), custom_call_target="tpu_custom_call" | custom-call | tf_op jit(solution)/shard_map/attn_out/pallas_call | solution.py:282
  49.0 51.4 %ffn.1 = (bf16[1024,1024]{1,0:T(8,128)(2,1)}, bf16[1024,1024]{1,0:T(8,128)(2,1)}, bf16[2,2,512,1024]{3,2,1,0:T(8,128)(2,1)}, bf16[2,512,1024]{2,1,0:T(8,128)(2,1...) custom-call(s32[2]{0:T(128)} %pad_add_fusion.bits, ...), custom_call_target="tpu_custom_call" | custom-call | tf_op jit(solution)/shard_map/ffn/pallas_call | solution.py:359
  100.4 3.0 collective-permute-start
  103.4 1.5 collective-permute-start.1
  104.9 3.1 slice_bitcast_fusion
  108.6 14.9 %ffn_back.1 = (bf16[1024,1024]{1,0:T(8,128)(2,1)}, f32[1024,1024]{1,0:T(8,128)}, bf16[1024,512]{1,0:T(8,128)(2,1)}, f32[1,1024]{1,0:T(1,128)}) custom-call(bf16[1024,1024]{1,0:T(8,128)(2,1)} %get-tuple-element.53.gx_ref, bf16[1024,1024]{1,0:T(8,128)(2,1)} %get-tuple-element.54.fo_ref, f32[1024,1024]{1,0:T(8,128)} %get-tuple-element.55.mid_ref, ...), custom_call_target="tpu_custom_call" | custom-call | tf_op jit(solution)/shard_map/ffn_back/pallas_call | solution.py:482
  124.2 27.2 %attn_bwd.1 = (bf16[1024,512]{1,0:T(8,128)(2,1)}, bf16[1024,512]{1,0:T(8,128)(2,1)}, bf16[1024,512]{1,0:T(8,128)(2,1)}, f32[4,2,2,8,256]{4,3,2,1,0:T(8,128)}) custom-call(bf16[1024,512]{1,0:T(8,128)(2,1)} %get-tuple-element.46.q_ref, bf16[1024,512]{1,0:T(8,128)(2,1)} %get-tuple-element.47.k_ref, bf16[1024,512]{1,0:T(8,128)(2,1)} %get-tuple-element.48.v_ref, ...), custom_call_target="tpu_custom_call" | custom-call | tf_op jit(solution)/shard_map/attn_bwd/pallas_call | solution.py:222
  151.4 19.9 %qkv_back.1 = (f32[1024,1024]{1,0:T(8,128)}, bf16[1024,1024]{1,0:T(8,128)(2,1)}, bf16[1024,1024]{1,0:T(8,128)(2,1)}, f32[1,1024]{1,0:T(1,128)}) custom-call(bf16[1024,512]{1,0:T(8,128)(2,1)} %get-tuple-element.60.dq_ref, bf16[1024,512]{1,0:T(8,128)(2,1)} %get-tuple-element.61.dk_ref, bf16[1024,512]{1,0:T(8,128)(2,1)} %get-tuple-element.62.dv_ref, ...), custom_call_target="tpu_custom_call" | custom-call | tf_op jit(solution)/shard_map/qkv_back/pallas_call | solution.py:542
  171.7 1.4 fusion.2.small_in
  173.4 0.9 copy-done.3
  174.3 0.7 copy-done.1
  175.0 229.8 %grad_sum.1 = (bf16[2,2048,1024]{2,1,0:T(8,128)(2,1)}, bf16[2,2048,1024]{2,1,0:T(8,128)(2,1)}, f32[8,1024]{1,0:T(8,128)}) custom-call(bf16[2,512,1024]{2,1,0:T(8,128)(2,1)} %get-tuple-element.66.gk, bf16[2,512,1024]{2,1,0:T(8,128)(2,1)} %copy-done.1, bf16[2,512,1024]{2,1,0:T(8,128)(2,1)} %get-tuple-element.68.uk, ...), custom_call_target="tpu_custom_call" | custom-call | tf_op jit(solution)/shard_map/grad_sum/pallas_call | solution.py:782
  404.8 0.7 slice_reduce_fusion
  405.5 1.4 fusion.9
  407.6 17.0 %widen.1 = (f32[1024,32,128]{2,1,0:T(8,128)}, f32[2,2,512,1024]{3,2,1,0:T(8,128)}, f32[3,1024,512]{2,1,0:T(8,128)}, f32[512,1024]{1,0:T(8,128)}) custom-call(bf16[2,4,512,1024]{3,2,1,0:T(8,128)(2,1)} %bitcast.31, bf16[2,4,512,1024]{3,2,1,0:T(8,128)(2,1)} %bitcast.27, bf16[2,4,512,1024]{3,2,1,0:T(8,128)(2,1)} %bitcast.32, bf16[2,4,512,1024]{3,2,1,0:T(8,128)(2,1)} %bitcast.28, ...), custom_call_target="tpu_custom_call" | custom-call | tf_op jit(solution)/shard_map/widen/pallas_call | solution.py:412
  424.6 1.3 copy.31
  425.9 1.6 copy-done
  427.5 2.0 copy.32
  (42 shorter events, 4.1 us)
Async XLA Ops:
  6.1 8.6 %copy-start.5 = (s32[1024]{0:T(1024)S(1)}, s32[1024]{0:T(1024)}, u32[]{:S(2)}) copy-start(s32[1024]{0:T(1024)} %param.14) | copy-start | bytes 12292
  6.1 8.6 %copy-start.6 = (s32[1024]{0:T(1024)S(1)}, s32[1024]{0:T(1024)}, u32[]{:S(2)}) copy-start(s32[1024]{0:T(1024)} %param.13) | copy-start | bytes 12292
  100.4 72.9 %collective-permute-start = (bf16[2,512,1024]{2,1,0:T(8,128)(2,1)}, bf16[2,512,1024]{2,1,0:T(8,128)(2,1)S(1)}, u32[]{:S(2)}, u32[]{:S(2)}) collective-permute-start(bf16[2,512,1024]{2,1,0:T(8,128)(2,1)} %get-tuple-element.67), channel_id=1, source_target_pairs={{0,2},{2,0},{4,6},{6,4},{8,10},{10,8},{12,14},{14,12},{16,18},{18,... | collective-permute-start | bytes 6291464 | tf_op jit(solution)/shard_map/ppermute | solution.py:802
  103.4 70.0 %collective-permute-start.1 = (bf16[2,512,1024]{2,1,0:T(8,128)(2,1)}, bf16[2,512,1024]{2,1,0:T(8,128)(2,1)}, u32[]{:S(2)}, u32[]{:S(2)}) collective-permute-start(bf16[2,512,1024]{2,1,0:T(8,128)(2,1)} %get-tuple-element.69), channel_id=1, source_target_pairs={{0,4},{2,6},{4,0},{6,2},{8,12},{10,14},{12,8},{14,10},{16,20},{18,... | collective-permute-start | bytes 6291464 | tf_op jit(solution)/shard_map/ppermute | solution.py:802
  108.0 65.3 %collective-permute-start.3 = (bf16[512,1024]{1,0:T(8,128)(2,1)}, bf16[512,1024]{1,0:T(8,128)(2,1)S(1)}, u32[]{:S(2)}, u32[]{:S(2)}) collective-permute-start(bf16[512,1024]{1,0:T(8,128)(2,1)} %get-tuple-element.83), channel_id=1, source_target_pairs={{0,4},{2,6},{4,0},{6,2},{8,12},{10,14},{12,8},{14,10},{16,20},{18,... | collective-permute-start | bytes 3145736 | tf_op jit(solution)/shard_map/ppermute | solution.py:802
  108.5 64.8 %collective-permute-start.2 = (bf16[512,1024]{1,0:T(8,128)(2,1)}, bf16[512,1024]{1,0:T(8,128)(2,1)}, u32[]{:S(2)}, u32[]{:S(2)}) collective-permute-start(bf16[512,1024]{1,0:T(8,128)(2,1)} %get-tuple-element.84), channel_id=1, source_target_pairs={{0,2},{2,0},{4,6},{6,4},{8,10},{10,8},{12,14},{14,12},{16,18},{18,... | collective-permute-start | bytes 3145736 | tf_op jit(solution)/shard_map/ppermute | solution.py:802
  151.4 20.0 %copy-start.4 = (f32[4,2,2,8,256]{4,3,2,1,0:T(8,128)S(1)}, f32[4,2,2,8,256]{4,3,2,1,0:T(8,128)}, u32[]{:S(2)}) copy-start(f32[4,2,2,8,256]{4,3,2,1,0:T(8,128)} %get-tuple-element.75) | copy-start | bytes 393220
  151.4 20.3 %copy-start.7 = (f32[1,1024]{1,0:T(1,128)S(1)}, f32[1,1024]{1,0:T(1,128)}, u32[]{:S(2)}) copy-start(f32[1,1024]{1,0:T(1,128)} %get-tuple-element.74) | copy-start | bytes 12292
  173.3 1.0 copy-start.3
  173.3 1.7 copy-start.1
  407.6 17.0 %copy-start.2 = (bf16[1024,1024]{1,0:T(8,128)(2,1)S(1)}, bf16[1024,1024]{1,0:T(8,128)(2,1)}, u32[]{:S(2)}) copy-start(bf16[1024,1024]{1,0:T(8,128)(2,1)} %get-tuple-element.114) | copy-start | bytes 6291460
  424.6 2.9 copy-start

commit v4 on v3

--- a/solution.py
+++ b/solution.py
@@ -20,14 +20,17 @@
 VAR_COLS = 4
 SEG_COL = 12
 ONE_COL = 20
-ROWS = 16
-LAG = 3
+ROWS = 32
+LAGS = (2, 4, 6, 8, 10)
+SPACE = 1
+SWAP_ROWS = 64
+SWAP_STEP = 2
 HALF_ROWS = 512
 GROUP_ROWS = 4 * HALF_ROWS
 WIDE = 1024
 SMALL = 8
-FFN_ROWS = 256
-FFN_COLS = 512
+FFN_ROWS = 512
+FFN_COLS = 256
 
 
 def dot_nn(a, b):
@@ -168,7 +171,7 @@
 
 
 def attn_bwd_body(
-    q_ref, k_ref, v_ref, do_ref, o32_ref, extq_ref, extk_ref, oh_ref, cos_ref, sin_ref, dq_ref, dk_ref, dv_ref, gb_ref, dqt_ref
+    q_ref, k_ref, v_ref, do_ref, o32_ref, extq_ref, extk_ref, oh_ref, cos_ref, sin_ref, d_ref, gb_ref, dqt_ref
 ):
     rows = q_ref.shape[0]
     blk = 256
@@ -208,9 +211,9 @@
     cosine = cos_ref[...]
     sine = sin_ref[...]
     dq = dqt_ref[...].T * HEAD**-0.5
-    dq_ref[...] = (dq * cosine - half_swap(dq) * sine).astype(BF)
-    dk_ref[...] = (dk * cosine - half_swap(dk) * sine).astype(BF)
-    dv_ref[...] = dv.astype(BF)
+    d_ref[0] = (dq * cosine - half_swap(dq) * sine).astype(BF)
+    d_ref[1] = (dk * cosine - half_swap(dk) * sine).astype(BF)
+    d_ref[2] = dv.astype(BF)
 
 
 def attn_bwd_call(q, k, v, do, o32, extq, extk, onehot, cosine, sine):
@@ -222,7 +225,7 @@
     return pl.pallas_call(
         attn_bwd_body,
         grid=(pairs,),
-        out_shape=[jax.ShapeDtypeStruct((rows, width), BF)] * 3 + [jax.ShapeDtypeStruct((pairs, 2, 2, 8, blk), F32)],
+        out_shape=[jax.ShapeDtypeStruct((3, rows, width), BF), jax.ShapeDtypeStruct((pairs, 2, 2, 8, blk), F32)],
         in_specs=[
             col, col, col, col, col,
             pl.BlockSpec((1, 2, rows, LANES), lambda p: (p, 0, 0, 0)),
@@ -230,7 +233,7 @@
             pl.BlockSpec((2, 8, rows), lambda p: (0, 0, 0)),
             full, full,
         ],
-        out_specs=[col, col, col, pl.BlockSpec((1, 2, 2, 8, blk), lambda p: (p, 0, 0, 0, 0))],
+        out_specs=[pl.BlockSpec((3, rows, LANES), lambda p: (0, 0, p)), pl.BlockSpec((1, 2, 2, 8, blk), lambda p: (p, 0, 0, 0, 0))],
         scratch_shapes=[pltpu.VMEM((LANES, rows), F32)],
         compiler_params=pltpu.CompilerParams(vmem_limit_bytes=VMEM_LIMIT),
         name="attn_bwd",
@@ -295,16 +298,103 @@
     )(x, o, w, gain)
 
 
+LATE = 4
+SLOTS = 4
+PART = FFN_COLS // 4
+
+
+def sent(copy):
+    copy.wait_send() if copy.is_remote else copy.wait()
+
+
+def grid_bits():
+    dp = lax.axis_index("dp")
+    return dp, dp % 2, (dp // 2) % 2, peers_of(dp)[3], peers_of(dp)[4]
+
+
 def ffn_body(
-    bits, xn_ref, ct_ref, wg_ref, wu_ref, wd_ref,
-    out_ref, gx_ref, gd_ref, gk_ref, gs_ref, uk_ref, us_ref, acc_o, acc_g, hid, dg, du, xt,
+    xn_ref, ct_ref, wg_ref, wu_ref, wd_ref,
+    out_ref, gx_ref, gk_ref, uk_ref, rg, ru, dk, rd, late_x, late_y,
+    acc_o, acc_g, hid, dg, du, xt, away_w, away_d, ws, wr, ds, dr,
 ):
     j = pl.program_id(0)
+    t = lax.axis_index("tensor")
+    dp, x, y, px, py = grid_bits()
+    steps = pl.num_programs(0)
     rows = xn_ref.shape[0]
-    blk = FFN_ROWS
+    blk = wd_ref.shape[0]
+    per = WIDE // blk
+    early = 2 * per - LATE
+    slot = lax.rem(j, SLOTS)
+    near = (px, py)
+    bits = (x, y)
+    arrays = ((rg, late_x), (ru, late_y))
+
+    def remote(src, dst, ssem, rsem, peer):
+        return pltpu.make_async_remote_copy(
+            src_ref=src, dst_ref=dst, send_sem=ssem, recv_sem=rsem, device_id=(peer, t), device_id_type=MESH
+        )
+
+    def wide_early(k, at):
+        cols = pl.ds(pl.multiple_of(lax.rem(at, per) * blk, blk), blk)
+        s = lax.rem(at, SLOTS)
+        return remote(away_w.at[k, s], arrays[k][0].at[:, cols], ws.at[k, s], wr.at[k], near[k])
+
+    def wide_late(k, at):
+        cols = pl.ds(pl.multiple_of((at - early) * blk, blk), blk)
+        s = lax.rem(at, SLOTS)
+        return pltpu.make_async_copy(away_w.at[k, s], arrays[k][1].at[pl.ds(0, HALF_ROWS), cols], ws.at[k, s])
+
+    def wide_do(at, act):
+        for k in range(2):
+
+            @pl.when(at < early)
+            def _():
+                act(wide_early(k, at))
+
+            @pl.when(at >= early)
+            def _():
+                act(wide_late(k, at))
+
+    def down_rows(g, half):
+        return pl.ds(pl.multiple_of(g * 2 * PART + half * PART, PART), PART)
+
+    def down_keep(g, at):
+        s = lax.rem(at, SLOTS)
+        return pltpu.make_async_copy(
+            away_d.at[s, down_rows(g, bits[g])], dk.at[g, pl.ds(pl.multiple_of(at * PART, PART), PART)], ds.at[g, s]
+        )
+
+    def down_send(g, at):
+        s = lax.rem(at, SLOTS)
+        rows_at = pl.ds(pl.multiple_of(at * PART, PART), PART)
+        return remote(away_d.at[s, down_rows(g, 1 - bits[g])], rd.at[g, rows_at], ds.at[2 + g, s], dr.at[g], near[g])
+
+    def down_late(g, at):
+        s = lax.rem(at, SLOTS)
+        rows_at = pl.ds(pl.multiple_of(HALF_ROWS + (at - early) * PART, PART), PART)
+        return pltpu.make_async_copy(
+            away_d.at[s, down_rows(g, 1 - bits[g])], arrays[g][1].at[rows_at], ds.at[2 + g, s]
+        )
+
+    def down_do(at, act):
+        for g in range(2):
+            act(down_keep(g, at))
+
+            @pl.when(at < early)
+            def _():
+                act(down_send(g, at))
+
+            @pl.when(at >= early)
+            def _():
+                act(down_late(g, at))
 
     @pl.when(j == 0)
     def _():
+        barrier = pltpu.get_barrier_semaphore()
+        for peer in near:
+            pl.semaphore_signal(barrier, inc=1, device_id=(peer, t), device_id_type=MESH)
+        pl.semaphore_wait(barrier, 2)
         acc_o[...] = jnp.zeros_like(acc_o)
         acc_g[...] = jnp.zeros_like(acc_g)
         xt[...] = xn_ref[...].T
@@ -312,8 +402,8 @@
     wg = wg_ref[...]
     wu = wu_ref[...]
     wd = wd_ref[...]
-    for i in range(rows // blk):
-        sl = slice(i * blk, (i + 1) * blk)
+    for i in range(rows // FFN_ROWS):
+        sl = slice(i * FFN_ROWS, (i + 1) * FFN_ROWS)
         xn = xn_ref[sl, :]
         gate = dot_nn(xn, wg)
         up = dot_nn(xn, wu)
@@ -328,53 +418,68 @@
         du[sl, :] = dup
         acc_o[sl, :] += dot_nn(hidden, wd)
         acc_g[sl, :] += dot_nt(dgate, wg) + dot_nt(dup, wu)
-    gd_ref[0, 0] = dot_tn(hid[...], ct_ref[...]).astype(BF)
-    for part, keep, send, bit in ((dg, gk_ref, gs_ref, bits[0]), (du, uk_ref, us_ref, bits[1])):
-        for out, half in ((keep, bit), (send, 1 - bit)):
-            rows_at = pl.ds(pl.multiple_of(half * HALF_ROWS, HALF_ROWS), HALF_ROWS)
-            out[0] = dot_nn(xt[rows_at, :], part[...]).astype(BF)
-
-    @pl.when(j == pl.num_programs(0) - 1)
+
+    @pl.when(j >= SLOTS)
+    def _():
+        wide_do(j - SLOTS, sent)
+        down_do(j - SLOTS, sent)
+
+    away_d[slot] = dot_tn(hid[...], ct_ref[...]).astype(BF)
+    down_do(j, lambda copy: copy.start())
+    for k, (part, keep, bit) in enumerate(((dg, gk_ref, x), (du, uk_ref, y))):
+        rows_at = lambda half: pl.ds(pl.multiple_of(half * HALF_ROWS, HALF_ROWS), HALF_ROWS)
+        away_w[k, slot] = dot_nn(xt[rows_at(1 - bit), :], part[...]).astype(BF)
+        keep[0] = dot_nn(xt[rows_at(bit), :], part[...]).astype(BF)
+    wide_do(j, lambda copy: copy.start())
+
+    @pl.when(j == steps - 1)
     def _():
         out_ref[...] = acc_o[...].astype(BF)
         gx_ref[...] = acc_g[...].astype(BF)
-
-
-def ffn_call(xn, ct, wg, wu, wd, bits):
+        for back in range(SLOTS, 0, -1):
+            wide_do(steps - back, sent)
+            down_do(steps - back, sent)
+        for k in range(2):
+            part = arrays[k][0].at[:, pl.ds(0, early * blk)]
+            remote(part, part, ws.at[k, 0], wr.at[k], near[k]).wait_recv()
+        for g in range(2):
+            part = rd.at[g, pl.ds(0, early * PART)]
+            remote(part, part, ds.at[g, 0], dr.at[g], near[g]).wait_recv()
+
+
+def ffn_call(xn, ct, wg, wu, wd):
     rows, dim = xn.shape
     hidden = wd.shape[0]
     blk = FFN_COLS
     per = WIDE // blk
-    full = pl.BlockSpec((rows, dim), lambda j, b: (0, 0))
-    colw = pl.BlockSpec((dim, blk), lambda j, b: (0, j))
-    roww = pl.BlockSpec((blk, dim), lambda j, b: (j, 0))
-    grad = pl.BlockSpec((1, HALF_ROWS, blk), lambda j, b: (j // per, 0, lax.rem(j, per)))
-
-    def down_at(j, b):
-        group = j // per
-        half = lax.rem(j, per) // (per // 2)
-        bit = jnp.where(group == 0, b[0], b[1])
-        return (jnp.where(half == bit, 0, 1), group, lax.rem(j, per // 2), 0)
-
+    full = pl.BlockSpec((rows, dim), lambda j: (0, 0))
+    colw = pl.BlockSpec((dim, blk), lambda j: (0, j))
+    roww = pl.BlockSpec((blk, dim), lambda j: (j, 0))
+    grad = pl.BlockSpec((1, HALF_ROWS, blk), lambda j: (j // per, 0, lax.rem(j, per)))
+    any_spec = pl.BlockSpec(memory_space=pl.ANY)
+    wide = jax.ShapeDtypeStruct((2, HALF_ROWS, dim), BF)
+    early = hidden // blk - LATE
+    come = jax.ShapeDtypeStruct((HALF_ROWS, early * blk), BF)
+    late = jax.ShapeDtypeStruct((HALF_ROWS + LATE * PART, LATE * blk), BF)
+    dma = pltpu.SemaphoreType.DMA
     return pl.pallas_call(
         ffn_body,
-        grid_spec=pltpu.PrefetchScalarGridSpec(
-            num_scalar_prefetch=1,
-            grid=(hidden // blk,),
-            in_specs=[full, full, colw, colw, roww],
-            out_specs=[full, full, pl.BlockSpec((1, 1, blk, dim), down_at), grad, grad, grad, grad],
-            scratch_shapes=[pltpu.VMEM((rows, dim), F32)] * 2 + [pltpu.VMEM((rows, blk), BF)] * 3
-            + [pltpu.VMEM((dim, rows), BF)],
-        ),
-        out_shape=[
-            jax.ShapeDtypeStruct((rows, dim), BF),
-            jax.ShapeDtypeStruct((rows, dim), BF),
-            jax.ShapeDtypeStruct((2, 2, HALF_ROWS, dim), BF),
-        ]
-        + [jax.ShapeDtypeStruct((2, HALF_ROWS, dim), BF)] * 4,
-        compiler_params=pltpu.CompilerParams(vmem_limit_bytes=VMEM_LIMIT),
+        grid=(hidden // blk,),
+        in_specs=[full, full, colw, colw, roww],
+        out_specs=[full, full, grad, grad] + [any_spec] * 6,
+        out_shape=[jax.ShapeDtypeStruct((rows, dim), BF)] * 2
+        + [wide, wide, come, come, wide, jax.ShapeDtypeStruct((2, early * PART, dim), BF), late, late],
+        scratch_shapes=[pltpu.VMEM((rows, dim), F32)] * 2
+        + [pltpu.VMEM((rows, blk), BF)] * 3
+        + [
+            pltpu.VMEM((dim, rows), BF),
+            pltpu.VMEM((2, SLOTS, HALF_ROWS, blk), BF),
+            pltpu.VMEM((SLOTS, blk, dim), BF),
+            dma((2, SLOTS)), dma((2,)), dma((4, SLOTS)), dma((2,)),
+        ],
+        compiler_params=pltpu.CompilerParams(collective_id=5, has_side_effects=True, vmem_limit_bytes=VMEM_LIMIT),
         name="ffn",
-    )(bits, xn, ct, wg, wu, wd)
+    )(xn, ct, wg, wu, wd)
 
 
 def pair_rows(w):
@@ -393,8 +498,8 @@
                 parts.append((ga_ref, gb_ref)[k % 2][0, f, :, s * LANES : (s + 1) * LANES].astype(F32))
             at = (f * tiles + q * 4) * 2
             gu_ref[:, at : at + 8, :] = jnp.swapaxes(jnp.stack(parts), 0, 1)
-    down_ref[0, 0] = da_ref[0, 0].astype(F32)
-    down_ref[1, 0] = db_ref[0, 0].astype(F32)
+    down_ref[:, 0, 0] = da_ref[0, 0].astype(F32).reshape(down_ref.shape[0], PART, WIDE)
+    down_ref[:, 1, 0] = db_ref[0, 0].astype(F32).reshape(down_ref.shape[0], PART, WIDE)
     width = qkv_ref.shape[2]
     qkv_ref[0] = aa_ref[0, 0, :, :width].astype(F32)
     qkv_ref[1] = aa_ref[0, 0, :, width:].astype(F32)
@@ -414,7 +519,7 @@
         grid=(2 * half,),
         out_shape=[
             jax.ShapeDtypeStruct((2 * HALF_ROWS, tiles, LANES), F32),
-            jax.ShapeDtypeStruct((2, 2, HALF_ROWS, WIDE), F32),
+            jax.ShapeDtypeStruct((HALF_ROWS // PART, 2, 2, PART, WIDE), F32),
             jax.ShapeDtypeStruct((3, 2 * HALF_ROWS, width), F32),
             jax.ShapeDtypeStruct((HALF_ROWS, WIDE), F32),
         ],
@@ -425,7 +530,7 @@
         ],
         out_specs=[
             pl.BlockSpec((blk, tiles, LANES), lambda i: (i, 0, 0)),
-            pl.BlockSpec((2, 1, blk, WIDE), lambda i: (0, i // half, lax.rem(i, half), 0)),
+            pl.BlockSpec((blk // PART, 2, 1, PART, WIDE), lambda i: (lax.rem(i, half), 0, i // half, 0, 0)),
             pl.BlockSpec((3, blk, width), lambda i: (0, i, 0)),
             pl.BlockSpec((blk // 2, WIDE), lambda i: (i, 0)),
         ],
@@ -445,7 +550,8 @@
 
 
 def ffn_back_body(
-    gx_ref, fo_ref, mid_ref, ct_ref, gain_ref, w_ref, out_ref, gm_ref, do_ref, gg_ref, gx_in, fo_in, ssem, rsem
+    gx_ref, fo_ref, mid_ref, ct_ref, gain_ref, w_ref, at_ref,
+    out_ref, gm_ref, do_ref, gw_ref, gg_ref, gx_in, fo_in, gb, ssem, rsem,
 ):
     peer = partner_barrier()
     rows = mid_ref.shape[0]
@@ -466,8 +572,10 @@
         gain_sum = gain_sum + gain_grad
         gm = ct_ref[sl, :].astype(F32) + back
         gm_ref[sl, :] = gm
-        do_ref[sl, :] = dot_nt(gm.astype(BF), w_ref[...]).astype(BF)
+        gb[sl, :] = gm.astype(BF)
+        do_ref[sl, :] = dot_nt(gb[sl, :], w_ref[...]).astype(BF)
     gg_ref[...] = gain_sum
+    gw_ref[...] = dot_tn(at_ref[...], gb[...]).astype(BF)
     for c in range(CHUNKS):
         sl = slice(c * blk, (c + 1) * blk)
         copies[CHUNKS + c].wait_recv()
@@ -476,7 +584,7 @@
         copy.wait_send()
 
 
-def ffn_back_call(gx, fo, mid, ct, gain, w):
+def ffn_back_call(gx, fo, mid, ct, gain, w, at):
     rows, dim = mid.shape
     width = w.shape[0]
     return pl.pallas_call(
@@ -485,11 +593,13 @@
             jax.ShapeDtypeStruct((rows, dim), BF),
             jax.ShapeDtypeStruct((rows, dim), F32),
             jax.ShapeDtypeStruct((rows, width), BF),
+            jax.ShapeDtypeStruct((width, dim), BF),
             jax.ShapeDtypeStruct((1, dim), F32),
         ],
-        in_specs=[whole_spec()] * 6,
-        out_specs=[whole_spec()] * 4,
+        in_specs=[whole_spec()] * 7,
+        out_specs=[whole_spec()] * 5,
         scratch_shapes=[
+            pltpu.VMEM((rows, dim), BF),
             pltpu.VMEM((rows, dim), BF),
             pltpu.VMEM((rows, dim), BF),
             pltpu.SemaphoreType.DMA((2 * CHUNKS,)),
@@ -497,67 +607,7 @@
         ],
         compiler_params=pltpu.CompilerParams(collective_id=2, has_side_effects=True, vmem_limit_bytes=VMEM_LIMIT),
         name="ffn_back",
-    )(gx, fo, mid, ct, gain, w)
-
-
-def qkv_back_body(
-    dq_ref, dk_ref, dv_ref, w_ref, xn_ref, x_ref, gain_ref, gm_ref, at_ref,
-    ig_ref, qk_ref, vo_ref, gg_ref, mine, theirs, ssem, rsem,
-):
-    peer = partner_barrier()
-    rows = x_ref.shape[0]
-    blk = rows // CHUNKS
-    width = dq_ref.shape[1]
-    copies = []
-    for c in range(CHUNKS):
-        sl = slice(c * blk, (c + 1) * blk)
-        total = dot_nt(dq_ref[sl, :], w_ref[0])
-        total = total + dot_nt(dk_ref[sl, :], w_ref[1])
-        total = total + dot_nt(dv_ref[sl, :], w_ref[2])
-        mine[sl, :] = total.astype(BF)
-        copy = send_rows(mine, theirs, pl.ds(c * blk, blk), ssem.at[c], rsem.at[c], peer)
-        copy.start()
-        copies.append(copy)
-    qk_ref[:, :width] = dot_tn(xn_ref[...], dq_ref[...]).astype(BF)
-    qk_ref[:, width:] = dot_tn(xn_ref[...], dk_ref[...]).astype(BF)
-    grad_v = dot_tn(xn_ref[...], dv_ref[...]).astype(BF)
-    vo_ref[:HALF_ROWS, :width] = grad_v[:HALF_ROWS]
-    vo_ref[:HALF_ROWS, width:] = grad_v[HALF_ROWS:]
-    vo_ref[HALF_ROWS:, :] = dot_tn(at_ref[...], gm_ref[...].astype(BF)).astype(BF)
-    gain_sum = jnp.zeros((1, x_ref.shape[1]), F32)
-    for c in range(CHUNKS):
-        sl = slice(c * blk, (c + 1) * blk)
-        copies[c].wait_recv()
-        grads = mine[sl, :].astype(F32) + theirs[sl, :].astype(F32)
-        back, gain_grad = norm_back(x_ref[sl, :].astype(F32), gain_ref[...], grads)
-        gain_sum = gain_sum + gain_grad
-        ig_ref[sl, :] = gm_ref[sl, :] + back
-    gg_ref[...] = gain_sum
-    for copy in copies:
-        copy.wait_send()
-
-
-def qkv_back_call(dq, dk, dv, w, xn, x, gain, gm, at):
-    rows, dim = x.shape
-    return pl.pallas_call(
-        qkv_back_body,
-        out_shape=[
-            jax.ShapeDtypeStruct((rows, dim), F32),
-            jax.ShapeDtypeStruct((dim, dim), BF),
-            jax.ShapeDtypeStruct((dim, dim), BF),
-            jax.ShapeDtypeStruct((1, dim), F32),
-        ],
-        in_specs=[whole_spec()] * 9,
-        out_specs=[whole_spec()] * 4,
-        scratch_shapes=[
-            pltpu.VMEM((rows, dim), BF),
-            pltpu.VMEM((rows, dim), BF),
-            pltpu.SemaphoreType.DMA((CHUNKS,)),
-            pltpu.SemaphoreType.DMA((CHUNKS,)),
-        ],
-        compiler_params=pltpu.CompilerParams(collective_id=3, has_side_effects=True, vmem_limit_bytes=VMEM_LIMIT),
-        name="qkv_back",
-    )(dq, dk, dv, w, xn, x, gain, gm, at)
+    )(gx, fo, mid, ct, gain, w, at)
 
 
 def peers_of(dp):
@@ -569,8 +619,9 @@
 
 
 def sum_body(
-    gk, rg, uk, ru, dk, rda, rdb, qk, vo, small_in, out_a, out_b, small_out,
-    L, S, Z, R, Y, F, sb, st, loc, s1s, s1r, sends, zr, rr, yr, ar, xr, lo, ss, sr,
+    gk, rg, uk, ru, late_x, late_y, dk, rd, go, dqkv, w3, xn, xin, gmid, gain_ref, small_in, out_a, out_b, ig, small_out,
+    L, S, Z, R, Y, sb, st, dl, wb, xb, mine_rows, their_rows, away_rows, xc, gc, ic,
+    loc, s1s, s1r, sends, zr, rr, yr, ar, xr, lo, ss, sr, ld, cs, cr, xg, io,
 ):
     dp = lax.axis_index("dp")
     t = lax.axis_index("tensor")
@@ -580,51 +631,82 @@
     mine = jnp.where(z == 2, WIDE // 2, 0)
     others = WIDE // 2 - mine
     n = GROUP_ROWS // ROWS
+    per = n // 4
     first = (px, py)
     last = (py, px)
     outs = (out_a, out_b)
     owner = (x, y)
-
-    def remote(src, dst, ssem, rsem, peer):
+    F = S
+
+    def remote(src, dst, ssem, rsem, peer, core=t):
         return pltpu.make_async_remote_copy(
-            src_ref=src, dst_ref=dst, send_sem=ssem, recv_sem=rsem, device_id=(peer, t), device_id_type=MESH
+            src_ref=src, dst_ref=dst, send_sem=ssem, recv_sem=rsem, device_id=(peer, core), device_id_type=MESH
         )
 
     def loads(g, b):
         rows = pl.ds(b * HALF_ROWS, HALF_ROWS)
-        if b < 2:
-            srcs = ((gk, uk)[g].at[b], (rg, ru)[g].at[b])
-        elif b == 2:
-            srcs = (dk.at[0, g], (rda, rdb)[g].at[...])
+        copies = [((gk, uk)[g].at[b] if b < 2 else dk.at[g], L.at[g, rows])]
+        near = (rg, ru)[g]
+        late = (late_x, late_y)[g]
+        top = pl.ds(0, HALF_ROWS)
+        if b == 0:
+            copies.append((near.at[:, pl.ds(0, WIDE)], S.at[g, rows]))
+        elif b == 1:
+            cut = near.shape[1] - WIDE
+            if cut:
+                copies.append((near.at[:, pl.ds(WIDE, cut)], S.at[g, rows, pl.ds(0, cut)]))
+            copies.append((late.at[top], S.at[g, rows, pl.ds(cut, WIDE - cut)]))
         else:
-            srcs = ((qk, vo)[g].at[pl.ds(pl.multiple_of(owner[g] * HALF_ROWS, HALF_ROWS), HALF_ROWS)],)
-        return [
-            pltpu.make_async_copy(src, (L, S)[k].at[g, rows], loc.at[g, b, k]) for k, src in enumerate(srcs)
-        ]
-
-    for b in range(4):
+            cut = rd.shape[1]
+            copies.append((rd.at[g], S.at[g, pl.ds(b * HALF_ROWS, cut)]))
+            for part in range((HALF_ROWS - cut) // PART):
+                copies.append(
+                    (late.at[pl.ds(HALF_ROWS + part * PART, PART)], S.at[g, pl.ds(b * HALF_ROWS + cut + part * PART, PART)])
+                )
+        return [pltpu.make_async_copy(src, dst, loc.at[g, b, k]) for k, (src, dst) in enumerate(copies)]
+
+    own_loads = [pltpu.make_async_copy(src, dst, ld.at[k]) for k, (src, dst) in enumerate(((dqkv, dl), (w3, wb), (xn, xb)))]
+    for b in range(3):
         for g in range(2):
             for copy in loads(g, b):
                 copy.start()
+    for copy in own_loads:
+        copy.start()
+
+    tail = pl.ds(3 * HALF_ROWS, HALF_ROWS)
+
+    def out_load(kept):
+        return pltpu.make_async_copy(go, L.at[1, tail] if kept else away_rows.at[1], loc.at[1, 3, 0])
+
+    def out_load_do(act):
+        @pl.when(y == 1)
+        def _():
+            act(out_load(True))
+
+        @pl.when(y == 0)
+        def _():
+            act(out_load(False))
+
+    out_load_do(lambda copy: copy.start())
 
     barrier = pltpu.get_barrier_semaphore()
     others_z = [lax.rem(z + k, 4) * 4 + y * 2 + x for k in range(1, 4)]
     for peer in [px, py] + others_z:
         pl.semaphore_signal(barrier, inc=1, device_id=(peer, t), device_id_type=MESH)
-    pl.semaphore_wait(barrier, 5)
+    pl.semaphore_signal(barrier, inc=1, device_id=(dp, 1 - t), device_id_type=MESH)
+    pl.semaphore_wait(barrier, 6)
 
     def first_exchange(g):
-        away = pl.ds(pl.multiple_of((1 - owner[g]) * HALF_ROWS, HALF_ROWS), HALF_ROWS)
-        return remote(
-            (qk, vo)[g].at[away], S.at[g, pl.ds(3 * HALF_ROWS, HALF_ROWS)], s1s.at[g], s1r.at[g], first[g]
-        )
-
-    small_x = remote(small_in, sb.at[0], ss.at[0], sr.at[0], px)
+        return remote(away_rows.at[g], S.at[g, tail], s1s.at[g], s1r.at[g], first[g])
+
+    def first_part(g, c):
+        at = pl.multiple_of(c * SWAP_ROWS, SWAP_ROWS)
+        dst = S.at[g, pl.ds(3 * HALF_ROWS + at, SWAP_ROWS)]
+        return remote(away_rows.at[g, pl.ds(at, SWAP_ROWS)], dst, s1s.at[g], s1r.at[g], first[g])
+
+    small_x = remote(st.at[2], sb.at[0], ss.at[0], sr.at[0], px)
     small_y = remote(st.at[0], sb.at[1], ss.at[1], sr.at[1], py)
     small_z = [remote(st.at[1], sb.at[2 + z], ss.at[2 + k], sr.at[2 + z], others_z[k]) for k in range(3)]
-    small_x.start()
-    for g in range(2):
-        first_exchange(g).start()
 
     def rows_of(i):
         return pl.ds(pl.multiple_of(i * ROWS, ROWS), ROWS)
@@ -653,97 +735,187 @@
     def l_copy(g, i):
         return pltpu.make_async_copy(F.at[g, rows_of(i)], outs[g].at[owner[g], rows_of(i)], lo.at[g])
 
+    def end_in(g, j):
+        r = rows_of(j)
+        L[g, r, :] = (L[g, r, :].astype(F32) + S[g, r, :].astype(F32)).astype(BF)
+        z_copy(g, j).start()
+
+    def end_out(g, j):
+        o_copy(g, j).wait_recv()
+        x_copy(g, j).start()
+        l_copy(g, j).start()
+
+    def mid_out(g, j):
+        a_copy(g, j, others).wait_recv()
+        o_copy(g, j).start()
+        x_copy(g, j).start()
+        l_copy(g, j).start()
+
+    def mid_join(g, j):
+        y_copy(g, j).wait_recv()
+        r = rows_of(j)
+        F[g, r, cols_of(mine)] = (R[g, r, :].astype(F32) + Y[g, r, :].astype(F32)).astype(BF)
+        a_copy(g, j, mine).start()
+
+    def mid_half(g, j):
+        r_copy(g, j).wait_recv()
+        r = rows_of(j)
+        R[g, r, :] = (R[g, r, :].astype(F32) + L[g, r, cols_of(mine)].astype(F32)).astype(BF)
+        y_copy(g, j).start()
+
+    def mid_in(g, j):
+        z_copy(g, j).wait_recv()
+        r = rows_of(j)
+        L[g, r, :] = (L[g, r, :].astype(F32) + S[g, r, :].astype(F32) + Z[g, r, :].astype(F32)).astype(BF)
+        r_copy(g, j).start()
+
+    def stage(act, g, j):
+        @pl.when((j >= 0) & (j < n))
+        def _():
+            act(g, j)
+
+    seq = xin.shape[0]
+    blk = seq // CHUNKS
+    width = dl.shape[2]
+
+    def piece_rows(c):
+        return pl.ds(c * blk, blk)
+
+    def core_copy(c):
+        return remote(mine_rows.at[piece_rows(c)], their_rows.at[piece_rows(c)], cs.at[c], cr.at[c], dp, 1 - t)
+
+    def norm_loads(c):
+        return [
+            pltpu.make_async_copy(xin.at[piece_rows(c)], xc.at[c % 2], xg.at[c % 2, 0]),
+            pltpu.make_async_copy(gmid.at[piece_rows(c)], gc.at[c % 2], xg.at[c % 2, 1]),
+        ]
+
+    def ig_copy(c):
+        return pltpu.make_async_copy(ic.at[c % 2], ig.at[piece_rows(c)], io.at[c % 2])
+
+    def piece_start():
+        for copy in own_loads:
+            copy.wait()
+
+    def piece_part(c):
+        r = piece_rows(c)
+        total = dot_nt(dl[0, r, :], wb[0]) + dot_nt(dl[1, r, :], wb[1]) + dot_nt(dl[2, r, :], wb[2])
+        mine_rows[r, :] = total.astype(BF)
+        core_copy(c).start()
+
+    def row_half(half):
+        return pl.ds(pl.multiple_of(half * HALF_ROWS, HALF_ROWS), HALF_ROWS)
+
+    def piece_qk(k):
+        cols = pl.ds(k * width, width)
+        L[0, tail, cols] = dot_tn(xb[:, row_half(x)], dl[k]).astype(BF)
+        away_rows[0, :, cols] = dot_tn(xb[:, row_half(1 - x)], dl[k]).astype(BF)
+
+    def piece_v():
+        for k in range(2):
+            cols = pl.ds(k * width, width)
+            grad = dot_tn(xb[:, k * HALF_ROWS : (k + 1) * HALF_ROWS], dl[2]).astype(BF)
+
+            @pl.when(y == 0)
+            def _():
+                L[1, tail, cols] = grad
+
+            @pl.when(y == 1)
+            def _():
+                away_rows[1, :, cols] = grad
+
+    def piece_send():
+        out_load_do(lambda copy: copy.wait())
+        for copy in norm_loads(0):
+            copy.start()
+        st[2] = small_in[...]
+
+    def piece_norm(c):
+        if c + 1 < CHUNKS:
+            for copy in norm_loads(c + 1):
+                copy.start()
+        for copy in norm_loads(c):
+            copy.wait()
+        core_copy(c).wait_recv()
+        if c >= 2:
+            ig_copy(c - 2).wait()
+        r = piece_rows(c)
+        grads = mine_rows[r, :].astype(F32) + their_rows[r, :].astype(F32)
+        back, gain_grad = norm_back(xc[c % 2].astype(F32), gain_ref[...], grads)
+        st[2, 0:1, :] = st[2, 0:1, :] + gain_grad
+        ic[c % 2] = gc[c % 2] + back
+        ig_copy(c).start()
+
+    def small_first():
+        small_x.start()
+
+    def small_second():
+        small_x.wait_recv()
+        st[0] = st[2] + sb[0]
+        small_y.start()
+
+    def small_third():
+        small_y.wait_recv()
+        st[1] = st[0] + sb[1]
+        for copy in small_z:
+            copy.start()
+
+    pieces = (
+        [piece_start]
+        + [functools.partial(piece_part, c) for c in range(CHUNKS)]
+        + [functools.partial(piece_qk, k) for k in range(2)]
+        + [piece_v, piece_send]
+        + [functools.partial(piece_norm, c) for c in range(CHUNKS)]
+        + [small_first, small_second, small_third]
+    )
+
     def body(i, carry):
-        @pl.when((i < n) & (lax.rem(i, n // 4) == 0))
-        def _():
-            for b in range(4):
-                @pl.when(i == b * (n // 4))
-                def _():
-                    for g in range(2):
+        for b in range(4):
+
+            @pl.when(i == b * per)
+            def _():
+                for g in range(2):
+                    if b < 3:
                         for copy in loads(g, b):
                             copy.wait()
-                        if b == 3:
-                            first_exchange(g).wait_recv()
-
-        @pl.when(is_end & (i < n))
+                    if b == 3:
+                        first_exchange(g).wait_recv()
+
+        @pl.when(is_end)
         def _():
             for g in range(2):
-                r = rows_of(i)
-                L[g, r, :] = (L[g, r, :].astype(F32) + S[g, r, :].astype(F32)).astype(BF)
-                z_copy(g, i).start()
+                stage(end_in, g, i)
+                stage(end_out, g, i - LAGS[4])
 
         @pl.when(is_mid)
         def _():
-            j = i - 4 * LAG
-
-            @pl.when((j >= 0) & (j < n))
+            for g in range(2):
+                stage(mid_out, g, i - LAGS[3])
+                stage(mid_join, g, i - LAGS[2])
+                stage(mid_half, g, i - LAGS[1])
+                stage(mid_in, g, i - LAGS[0])
+
+        begin = 2 + SPACE * (CHUNKS + 4)
+        c = (i - begin) // SWAP_STEP
+
+        @pl.when((i >= begin) & (c < HALF_ROWS // SWAP_ROWS) & (lax.rem(i - begin, SWAP_STEP) == 0))
+        def _():
+            for g in range(2):
+                first_part(g, c).start()
+
+        for k, piece in enumerate(pieces):
+
+            @pl.when(i == 1 + SPACE * k)
             def _():
-                for g in range(2):
-                    a_copy(g, j, others).wait_recv()
-                    o_copy(g, j).start()
-                    x_copy(g, j).start()
-                    l_copy(g, j).start()
-
-            j3 = i - 3 * LAG
-
-            @pl.when((j3 >= 0) & (j3 < n))
-            def _():
-                for g in range(2):
-                    y_copy(g, j3).wait_recv()
-                    r = rows_of(j3)
-                    F[g, r, cols_of(mine)] = (R[g, r, :].astype(F32) + Y[g, r, :].astype(F32)).astype(BF)
-                    a_copy(g, j3, mine).start()
-
-            j2 = i - 2 * LAG
-
-            @pl.when((j2 >= 0) & (j2 < n))
-            def _():
-                for g in range(2):
-                    r_copy(g, j2).wait_recv()
-                    r = rows_of(j2)
-                    R[g, r, :] = (R[g, r, :].astype(F32) + L[g, r, cols_of(mine)].astype(F32)).astype(BF)
-                    y_copy(g, j2).start()
-
-            j1 = i - LAG
-
-            @pl.when((j1 >= 0) & (j1 < n))
-            def _():
-                for g in range(2):
-                    z_copy(g, j1).wait_recv()
-                    r = rows_of(j1)
-                    L[g, r, :] = (L[g, r, :].astype(F32) + S[g, r, :].astype(F32) + Z[g, r, :].astype(F32)).astype(BF)
-                    r_copy(g, j1).start()
-
-        @pl.when(is_end)
-        def _():
-            j = i - 5 * LAG
-
-            @pl.when((j >= 0) & (j < n))
-            def _():
-                for g in range(2):
-                    o_copy(g, j).wait_recv()
-                    x_copy(g, j).start()
-                    l_copy(g, j).start()
-
-        @pl.when(i == n // 8)
-        def _():
-            small_x.wait_recv()
-            st[0] = small_in[...] + sb[0]
-            small_y.start()
-
-        @pl.when(i == n // 4)
-        def _():
-            small_y.wait_recv()
-            st[1] = st[0] + sb[1]
-            for copy in small_z:
-                copy.start()
+                piece()
 
         return carry
 
-    lax.fori_loop(0, n + 5 * LAG, body, 0)
+    lax.fori_loop(0, n + LAGS[4], body, 0)
 
     for k in range(3):
-        remote(st.at[1], sb.at[2 + lax.rem(z + k + 1, 4)], ss.at[2 + k], sr.at[2 + lax.rem(z + k + 1, 4)], others_z[k]).wait_recv()
+        zz = lax.rem(z + k + 1, 4)
+        remote(st.at[1], sb.at[2 + zz], ss.at[2 + k], sr.at[2 + zz], others_z[k]).wait_recv()
     sb[2 + z] = st[1]
     small_out[...] = (sb[2] + sb[3]) + (sb[4] + sb[5])
 
@@ -751,6 +923,10 @@
     small_y.wait_send()
     for copy in small_z:
         copy.wait_send()
+    for c in range(CHUNKS):
+        core_copy(c).wait_send()
+    for c in (CHUNKS - 2, CHUNKS - 1):
+        ig_copy(c).wait()
     for g in range(2):
         first_exchange(g).wait_send()
         away = 1 - owner[g]
@@ -761,7 +937,6 @@
 
         @pl.when(is_mid)
         def _():
-            half = pl.ds(0, WIDE // 2)
             remote(R.at[g], Y.at[g], sends.at[g, 1], rr.at[g, 0], mm).wait_send()
             remote(R.at[g], Y.at[g], sends.at[g, 2], yr.at[g, 0], last[g]).wait_send()
             remote(R.at[g], Y.at[g], sends.at[g, 3], ar.at[g, 0], mm).wait_send()
@@ -773,33 +948,41 @@
         pltpu.make_async_copy(F.at[g], outs[g].at[owner[g]], lo.at[g]).wait()
 
 
-def sum_call(gk, rg, uk, ru, dk, rda, rdb, qk, vo, small):
+def sum_call(gk, rg, uk, ru, late_x, late_y, dk, rd, go, dqkv, w3, xn, xin, gmid, gain, small):
     any_spec = pl.BlockSpec(memory_space=pl.ANY)
     n = GROUP_ROWS // ROWS
+    rows, dim = xin.shape
+    blk = rows // CHUNKS
     full = pltpu.VMEM((2, GROUP_ROWS, WIDE), BF)
     half = pltpu.VMEM((2, GROUP_ROWS, WIDE // 2), BF)
     dma = pltpu.SemaphoreType.DMA
     return pl.pallas_call(
         sum_body,
-        out_shape=[jax.ShapeDtypeStruct((2, GROUP_ROWS, WIDE), BF)] * 2 + [jax.ShapeDtypeStruct((SMALL, WIDE), F32)],
-        in_specs=[any_spec] * 9 + [whole_spec()],
-        out_specs=[any_spec] * 2 + [whole_spec()],
+        out_shape=[jax.ShapeDtypeStruct((2, GROUP_ROWS, WIDE), BF)] * 2
+        + [jax.ShapeDtypeStruct((rows, dim), F32), jax.ShapeDtypeStruct((SMALL, WIDE), F32)],
+        in_specs=[any_spec] * 14 + [whole_spec()] * 2,
+        out_specs=[any_spec] * 3 + [whole_spec()],
         scratch_shapes=[
-            full, full, full, half, half, full,
+            full, full, full, half, half,
             pltpu.VMEM((6, SMALL, WIDE), F32),
-            pltpu.VMEM((2, SMALL, WIDE), F32),
-            dma((2, 4, 2)), dma((2,)), dma((2,)), dma((2, 6)),
+            pltpu.VMEM((3, SMALL, WIDE), F32),
+            pltpu.VMEM(dqkv.shape, BF),
+            pltpu.VMEM(w3.shape, BF),
+            pltpu.VMEM((rows, dim), BF),
+            pltpu.VMEM((rows, dim), BF),
+            pltpu.VMEM((rows, dim), BF),
+            pltpu.VMEM((2, HALF_ROWS, WIDE), BF),
+            pltpu.VMEM((2, blk, dim), BF),
+            pltpu.VMEM((2, blk, dim), F32),
+            pltpu.VMEM((2, blk, dim), F32),
+            dma((2, 4, 8)), dma((2,)), dma((2,)), dma((2, 6)),
             dma((2, n)), dma((2, n)), dma((2, n)), dma((2, n)),
             dma((2,)), dma((2,)), dma((5,)), dma((6,)),
+            dma((3,)), dma((CHUNKS,)), dma((CHUNKS,)), dma((2, 2)), dma((2,)),
         ],
         compiler_params=pltpu.CompilerParams(collective_id=4, has_side_effects=True, vmem_limit_bytes=VMEM_LIMIT),
         name="grad_sum",
-    )(gk, rg, uk, ru, dk, rda, rdb, qk, vo, small)
-
-
-def first_swap(sends, bit):
-    pairs = [(d, d ^ bit) for d in range(16)]
-    return [lax.ppermute(s, "dp", pairs) for s in sends]
+    )(gk, rg, uk, ru, late_x, late_y, dk, rd, go, dqkv, w3, xn, xin, gmid, gain, small)
 
 
 def tables(time_ids):
@@ -834,8 +1017,6 @@
 def fast_local(
     block_input, segments, variates, time_ids, attn_gain, w_qkv, head_bias, w_out, ffn_gain, w_gate_up, w_down, cotangent
 ):
-    dp = lax.axis_index("dp")
-    bits = jnp.stack([dp % 2, (dp // 2) % 2]).astype(jnp.int32)
     w3 = jnp.transpose(w_qkv, (1, 0, 2))
     cosine, sine = tables(time_ids)
     base, segq, extk, bias_rows, onehot = mask_tables(segments, variates, head_bias)
@@ -844,17 +1025,21 @@
     xn, q, k, v = qkv_call(block_input, gain1, w3, cosine, sine)
     attended, o32, extq, wg, wu = attn_fwd_call(q, k, v, base, segq, extk, bias_rows, pair_rows(w_gate_up))
     mid, xn2 = attn_out_call(block_input, attended, w_out, gain2)
-    ffn_part, gx_part, down, gk, gs, uk, us = ffn_call(xn2, cotangent, wg, wu, w_down, bits)
-    rg, rda = first_swap([gs, down[1, 0]], 1)
-    ru, rdb = first_swap([us, down[1, 1]], 2)
-    block_output, grad_mid, do, g_gain2 = ffn_back_call(gx_part, ffn_part, mid, cotangent, gain2, w_out)
-    dq, dk, dv, gb = attn_bwd_call(q, k, v, do, o32, extq, extk, onehot, cosine, sine)
-    input_grad, qk, vo, g_gain1 = qkv_back_call(dq, dk, dv, w3, xn, block_input, gain1, grad_mid, attended)
+    ffn_part, gx_part, gk, uk, rg, ru, dk, rd, late_x, late_y = ffn_call(xn2, cotangent, wg, wu, w_down)
+    late_x = lax.ppermute(late_x, "dp", [(d, d ^ 1) for d in range(16)])
+    late_y = lax.ppermute(late_y, "dp", [(d, d ^ 2) for d in range(16)])
+    block_output, grad_mid, do, g_out, g_gain2 = ffn_back_call(
+        gx_part, ffn_part, mid, cotangent, gain2, w_out, attended
+    )
+    dqkv, gb = attn_bwd_call(q, k, v, do, o32, extq, extk, onehot, cosine, sine)
     g_bias = jnp.sum(gb, axis=(3, 4)).reshape(-1, 2).T
     heads = g_bias.shape[1]
     bias_row = jnp.pad(g_bias.reshape(1, -1), ((0, 0), (0, WIDE - 2 * heads)))
-    small = jnp.concatenate([g_gain1, g_gain2, bias_row, jnp.zeros((SMALL - 3, WIDE), F32)], axis=0)
-    sum_a, sum_b, small = sum_call(gk, rg, uk, ru, down, rda, rdb, qk, vo, small)
+    zero = jnp.zeros((1, WIDE), F32)
+    small = jnp.concatenate([zero, g_gain2, bias_row, jnp.zeros((SMALL - 3, WIDE), F32)], axis=0)
+    sum_a, sum_b, input_grad, small = sum_call(
+        gk, rg, uk, ru, late_x, late_y, dk, rd, g_out, dqkv, w3, xn, block_input, grad_mid, gain1, small
+    )
     sum_a = sum_a.reshape(2, 4, HALF_ROWS, WIDE)
     sum_b = sum_b.reshape(2, 4, HALF_ROWS, WIDE)
     g_gate_up, g_down, g_qkv, g_out = widen_call(sum_a, sum_b)

time: 437 us -> 415 us (0.950); the launches traced: 430 us -> 414 us
  Pallas kernels: 401 us -> 392 us
    pallas_call x2 -> x1, Pallas kernels: 71.3 us -> 56.2 us  [ffn_call(): pl.pallas_call(ffn_body, grid=(hidden // blk,), in_specs=[full, full, col...]
    pallas_call x1, Pallas kernels: 27.2 us -> 39.1 us  [attn_bwd_call(): pl.pallas_call(attn_bwd_body, grid=(pairs,), out_shape=[jax.ShapeDtypeStr...]
    pallas_call x1, Pallas kernels: 230 us -> 223 us  [sum_call(): pl.pallas_call(sum_body, out_shape=[jax.ShapeDtypeStruct((2, GROUP_ROWS,...]
  transfers between devices with their start and end apart: 4 -> 2, of which waited for: 1 -> 0; matrix products, arithmetic and copies ran while one was open for 1% -> 1% of each run, Pallas kernels for 14% -> 13%
where the time goes in v4:
time: 415 us; the launch traced here: 414 us
  Pallas kernels  392 us (94%)
  local copies, waits for them, and re-layouts  9.8 us (2%)
  other arithmetic  9.13 us (2%)
    pallas_call x1, Pallas kernels, sum_call(): pl.pallas_call(sum_body, out_shape=[jax.ShapeDtypeStruct((2, GROUP_ROWS,...  223 us
    pallas_call x1, Pallas kernels, ffn_call(): pl.pallas_call(ffn_body, grid=(hidden // blk,), in_specs=[full, full, col...  56.2 us
    pallas_call x1, Pallas kernels, attn_bwd_call(): pl.pallas_call(attn_bwd_body, grid=(pairs,), out_shape=[jax.ShapeDtypeStr...  39.1 us
    pallas_call x1, Pallas kernels, attn_fwd_call(): pl.pallas_call(attn_fwd_body, grid=(pairs,), out_shape=[jax.ShapeDtypeStr...  23.1 us
    pallas_call x1, Pallas kernels, widen_call(): pl.pallas_call(widen_body, grid=(2 * half,), out_shape=[jax.ShapeDtypeStr...  17 us
    pallas_call x1, Pallas kernels, ffn_back_call(): pl.pallas_call(ffn_back_body, out_shape=[jax.ShapeDtypeStruct((rows, dim)...  15.5 us
    pallas_call x1, Pallas kernels, attn_out_call(): pl.pallas_call(attn_out_body, out_shape=[jax.ShapeDtypeStruct((rows, dim)...  9.85 us
  transfers between devices with their start and end apart: 2, of which 0 were waited for; matrix products, arithmetic and copies ran while one was open for 1% of the time, Pallas kernels for 13%

profile of v4, /device:TPU:0, one launch (start us, length us, event | category | flops | bytes accessed | tf_op | source)
XLA Modules:
  0.0 413.9 jit_solution(10645746666853534537)
XLA Ops:
  0.7 0.8 subtract_reduce_fusion
  1.7 0.7 convert_element_type.8
  2.4 3.1 fusion
  5.5 8.0 %qkv.1 = (bf16[1024,1024]{1,0:T(8,128)(2,1)}, bf16[1024,512]{1,0:T(8,128)(2,1)}, bf16[1024,512]{1,0:T(8,128)(2,1)}, bf16[1024,512]{1,0:T(8,128)(2,1)}) custom-call(bf16[1024,1024]{1,0:T(8,128)(2,1)} %xin.1, f32[1,1024]{1,0:T(1,128)} %bitcast.35, bf16[3,1024,512]{2,1,0:T(8,128)(2,1)} %bitcast.29, f32[1024,128]{1,0:T(8,128)} %get-tuple-element.87.cos_ref, ...), custom_call_target="tpu_custom_call" | custom-call | tf_op jit(solution)/shard_map/qkv/pallas_call | solution.py:86
  13.4 0.7 select_select_fusion.bias_ref
  14.1 1.4 select_convert_fusion
  15.5 23.1 %attn_fwd.1 = (bf16[1024,512]{1,0:T(8,128)(2,1)}, f32[1024,512]{1,0:T(8,128)}, bf16[4,2,1024,128]{3,2,1,0:T(8,128)(2,1)}, bf16[1024,2048]{1,0:T(8,128)(2,1)}, bf16[1024,2048]{1,0:T(8,128)(2,1)}) custom-call(bf16[1024,512]{1,0:T(8,128)(2,1)} %get-tuple-element.45.q_ref, bf16[1024,512]{1,0:T(8,128)(2,1)} %get-tuple-element.46.k_ref, ...), custom_call_target="tpu_custom_call" | custom-call | tf_op jit(solution)/shard_map/attn_fwd/pallas_call | solution.py:152
  38.6 9.8 %attn_out.1 = (f32[1024,1024]{1,0:T(8,128)}, bf16[1024,1024]{1,0:T(8,128)(2,1)}) custom-call(bf16[1024,1024]{1,0:T(8,128)(2,1)} %xin.1, bf16[1024,512]{1,0:T(8,128)(2,1)} %get-tuple-element.48.o_ref.at_ref, bf16[512,1024]{1,0:T(8,128)(2,1)} %w_ref.3, f32[1,1024]{1,0:T(1,128)} %bitcast.32), custom_call_target="tpu_custom_call" | custom-call | tf_op jit(solution)/shard_map/attn_out/pallas_call | solution.py:285
  48.5 56.2 %ffn.1 = (bf16[1024,1024]{1,0:T(8,128)(2,1)}, bf16[1024,1024]{1,0:T(8,128)(2,1)}, bf16[2,512,1024]{2,1,0:T(8,128)(2,1)}, bf16[2,512,1024]{2,1,0:T(8,128)(2,1)}, ...) custom-call(bf16[1024,1024]{1,0:T(8,128)(2,1)} %get-tuple-element.49, ...), custom_call_target="tpu_custom_call" | custom-call | tf_op jit(solution)/shard_map/ffn/pallas_call | solution.py:465
  104.7 1.6 collective-permute-start
  106.9 15.5 %ffn_back.1 = (bf16[1024,1024]{1,0:T(8,128)(2,1)}, f32[1024,1024]{1,0:T(8,128)}, bf16[1024,512]{1,0:T(8,128)(2,1)}, bf16[512,1024]{1,0:T(8,128)(2,1)}, f32[1,1024]{1,0:T(1,128)}) custom-call(bf16[1024,1024]{1,0:T(8,128)(2,1)} %get-tuple-element.52.gx_ref, bf16[1024,1024]{1,0:T(8,128)(2,1)} %get-tuple-element.53.fo_ref, ...), custom_call_target="tpu_custom_call" | custom-call | tf_op jit(solution)/shard_map/ffn_back/pallas_call | solution.py:590
  122.5 0.6 pad_maximum_fusion.oh_ref
  123.1 39.1 %attn_bwd.1 = (bf16[3,1024,512]{2,1,0:T(8,128)(2,1)}, f32[4,2,2,8,256]{4,3,2,1,0:T(8,128)}) custom-call(bf16[1024,512]{1,0:T(8,128)(2,1)} %get-tuple-element.45.q_ref, bf16[1024,512]{1,0:T(8,128)(2,1)} %get-tuple-element.46.k_ref, bf16[1024,512]{1,0:T(8,128)(2,1)} %get-tuple-element.47.v_ref, bf16[1024,512]{1,0:T(8,128)(2,1)} %get-tuple-element.65.do_ref, ...), custom_call_target="tpu_custom_call" | custom-call | tf_op jit(solution)/shard_map/attn_bwd/pallas_call | solution.py:225
  162.2 1.0 reduce_sum.9
  163.4 0.7 fusion.2.small_in
  164.1 1.1 copy-done.2
  165.7 223.2 %grad_sum.1 = (bf16[2,2048,1024]{2,1,0:T(8,128)(2,1)}, bf16[2,2048,1024]{2,1,0:T(8,128)(2,1)}, f32[1024,1024]{1,0:T(8,128)}, f32[8,1024]{1,0:T(8,128)}) custom-call(bf16[2,512,1024]{2,1,0:T(8,128)(2,1)} %get-tuple-element.56.gk, bf16[512,1024]{1,0:T(8,128)(2,1)} %get-tuple-element.57.rg, bf16[2,512,1024]{2,1,0:T(8,128)(2,1)} %get-tuple-element.58.uk, ...), custom_call_target="tpu_custom_call" | custom-call | tf_op jit(solution)/shard_map/grad_sum/pallas_call | solution.py:959
  389.0 0.7 slice_reduce_fusion
  389.7 1.4 fusion.9
  391.1 0.6 reshape_squeeze.3
  391.8 17.0 %widen.1 = (f32[1024,32,128]{2,1,0:T(8,128)}, f32[8,2,2,64,1024]{4,3,2,1,0:T(8,128)}, f32[3,1024,512]{2,1,0:T(8,128)}, f32[512,1024]{1,0:T(8,128)}) custom-call(bf16[2,4,512,1024]{3,2,1,0:T(8,128)(2,1)} %bitcast.26, bf16[2,4,512,1024]{3,2,1,0:T(8,128)(2,1)} %bitcast.22, bf16[2,4,512,1024]{3,2,1,0:T(8,128)(2,1)} %bitcast.27, ...), custom_call_target="tpu_custom_call" | custom-call | tf_op jit(solution)/shard_map/widen/pallas_call | solution.py:517
  408.8 1.3 copy.31
  410.1 1.6 copy-done
  411.7 2.0 copy.32
  (34 shorter events, 1.6 us)
Async XLA Ops:
  5.5 8.6 %copy-start.4 = (s32[1024]{0:T(1024)S(1)}, s32[1024]{0:T(1024)}, u32[]{:S(2)}) copy-start(s32[1024]{0:T(1024)} %param.14) | copy-start | bytes 12292
  5.5 8.6 %copy-start.5 = (s32[1024]{0:T(1024)S(1)}, s32[1024]{0:T(1024)}, u32[]{:S(2)}) copy-start(s32[1024]{0:T(1024)} %param.13) | copy-start | bytes 12292
  104.7 59.4 %collective-permute-start = (bf16[768,1024]{1,0:T(8,128)(2,1)}, bf16[768,1024]{1,0:T(8,128)(2,1)S(1)}, u32[]{:S(2)}, u32[]{:S(2)}) collective-permute-start(bf16[768,1024]{1,0:T(8,128)(2,1)} %get-tuple-element.60), channel_id=1, source_target_pairs={{0,2},{2,0},{4,6},{6,4},{8,10},{10,8},{12,14},{14,12},{16,18},{18,... | collective-permute-start | bytes 4718600 | tf_op jit(solution)/shard_map/ppermute | solution.py:1029
  106.2 57.8 %collective-permute-start.1 = (bf16[768,1024]{1,0:T(8,128)(2,1)}, bf16[768,1024]{1,0:T(8,128)(2,1)S(1)}, u32[]{:S(2)}, u32[]{:S(2)}) collective-permute-start(bf16[768,1024]{1,0:T(8,128)(2,1)} %get-tuple-element.61), channel_id=1, source_target_pairs={{0,4},{2,6},{4,0},{6,2},{8,12},{10,14},{12,8},{14,10},{16,20},{18,... | collective-permute-start | bytes 4718600 | tf_op jit(solution)/shard_map/ppermute | solution.py:1030
  123.1 40.3 %copy-start.6 = (f32[1,1024]{1,0:T(1,128)S(1)}, f32[1,1024]{1,0:T(1,128)}, u32[]{:S(2)}) copy-start(f32[1,1024]{1,0:T(1,128)} %get-tuple-element.71) | copy-start | bytes 12292
  164.1 1.1 copy-start.2
  164.1 1.7 copy-start.3
  391.7 17.0 %copy-start.1 = (bf16[1024,1024]{1,0:T(8,128)(2,1)S(1)}, bf16[1024,1024]{1,0:T(8,128)(2,1)}, u32[]{:S(2)}) copy-start(bf16[1024,1024]{1,0:T(8,128)(2,1)} %get-tuple-element.110) | copy-start | bytes 6291460
  408.8 2.9 copy-start

commit v5 on v4

--- a/solution.py
+++ b/solution.py
@@ -22,11 +22,11 @@
 ONE_COL = 20
 ROWS = 32
 LAGS = (2, 4, 6, 8, 10)
-SPACE = 1
-SWAP_ROWS = 64
-SWAP_STEP = 2
+SWAP_ROWS = 32
 HALF_ROWS = 512
+QUARTER_ROWS = HALF_ROWS // 2
 GROUP_ROWS = 4 * HALF_ROWS
+KEPT_ROWS = GROUP_ROWS - QUARTER_ROWS
 WIDE = 1024
 SMALL = 8
 FFN_ROWS = 512
@@ -620,8 +620,8 @@
 
 def sum_body(
     gk, rg, uk, ru, late_x, late_y, dk, rd, go, dqkv, w3, xn, xin, gmid, gain_ref, small_in, out_a, out_b, ig, small_out,
-    L, S, Z, R, Y, sb, st, dl, wb, xb, mine_rows, their_rows, away_rows, xc, gc, ic,
-    loc, s1s, s1r, sends, zr, rr, yr, ar, xr, lo, ss, sr, ld, cs, cr, xg, io,
+    L, S, Z, R, Y, DL, DS, DA, G, sb, st, dl, wb, xb, mine_rows, their_rows, away_rows, xc, gc, ic,
+    loc, s1s, s1r, sends, zr, rr, yr, ar, xr, lo, ss, sr, ld, cs, cr, xg, io, s2s, s2r, gs, gr,
 ):
     dp = lax.axis_index("dp")
     t = lax.axis_index("tensor")
@@ -630,12 +630,15 @@
     is_end = (z == 0) | (z == 3)
     mine = jnp.where(z == 2, WIDE // 2, 0)
     others = WIDE // 2 - mine
-    n = GROUP_ROWS // ROWS
-    per = n // 4
+    n = KEPT_ROWS // ROWS
+    cut_at = 2 * HALF_ROWS // ROWS
+    tail_at = (2 * HALF_ROWS + QUARTER_ROWS) // ROWS
+    starts = (0, HALF_ROWS // ROWS, cut_at, tail_at)
     first = (px, py)
     last = (py, px)
     outs = (out_a, out_b)
     owner = (x, y)
+    bit = (y, x)
     F = S
 
     def remote(src, dst, ssem, rsem, peer, core=t):
@@ -645,10 +648,13 @@
 
     def loads(g, b):
         rows = pl.ds(b * HALF_ROWS, HALF_ROWS)
-        copies = [((gk, uk)[g].at[b] if b < 2 else dk.at[g], L.at[g, rows])]
         near = (rg, ru)[g]
         late = (late_x, late_y)[g]
         top = pl.ds(0, HALF_ROWS)
+        if b < 2:
+            copies = [((gk, uk)[g].at[b], L.at[g, rows])]
+        else:
+            copies = [(dk.at[g], DL.at[g])]
         if b == 0:
             copies.append((near.at[:, pl.ds(0, WIDE)], S.at[g, rows]))
         elif b == 1:
@@ -658,11 +664,8 @@
             copies.append((late.at[top], S.at[g, rows, pl.ds(cut, WIDE - cut)]))
         else:
             cut = rd.shape[1]
-            copies.append((rd.at[g], S.at[g, pl.ds(b * HALF_ROWS, cut)]))
-            for part in range((HALF_ROWS - cut) // PART):
-                copies.append(
-                    (late.at[pl.ds(HALF_ROWS + part * PART, PART)], S.at[g, pl.ds(b * HALF_ROWS + cut + part * PART, PART)])
-                )
+            copies.append((rd.at[g], DS.at[g, pl.ds(0, cut)]))
+            copies.append((late.at[pl.ds(HALF_ROWS, HALF_ROWS - cut)], DS.at[g, pl.ds(cut, HALF_ROWS - cut)]))
         return [pltpu.make_async_copy(src, dst, loc.at[g, b, k]) for k, (src, dst) in enumerate(copies)]
 
     own_loads = [pltpu.make_async_copy(src, dst, ld.at[k]) for k, (src, dst) in enumerate(((dqkv, dl), (w3, wb), (xn, xb)))]
@@ -673,7 +676,7 @@
     for copy in own_loads:
         copy.start()
 
-    tail = pl.ds(3 * HALF_ROWS, HALF_ROWS)
+    tail = pl.ds(2 * HALF_ROWS + QUARTER_ROWS, HALF_ROWS)
 
     def out_load(kept):
         return pltpu.make_async_copy(go, L.at[1, tail] if kept else away_rows.at[1], loc.at[1, 3, 0])
@@ -701,8 +704,38 @@
 
     def first_part(g, c):
         at = pl.multiple_of(c * SWAP_ROWS, SWAP_ROWS)
-        dst = S.at[g, pl.ds(3 * HALF_ROWS + at, SWAP_ROWS)]
+        dst = S.at[g, pl.ds(2 * HALF_ROWS + QUARTER_ROWS + at, SWAP_ROWS)]
         return remote(away_rows.at[g, pl.ds(at, SWAP_ROWS)], dst, s1s.at[g], s1r.at[g], first[g])
+
+    quarter = pl.ds(2 * HALF_ROWS, QUARTER_ROWS)
+
+    def second_exchange(g):
+        return remote(DA.at[g], S.at[g, quarter], s2s.at[g], s2r.at[g], last[g])
+
+    def second_part(g, c):
+        at = pl.multiple_of(c * SWAP_ROWS, SWAP_ROWS)
+        rows = pl.ds(at, SWAP_ROWS)
+        dst = S.at[g, pl.ds(2 * HALF_ROWS + at, SWAP_ROWS)]
+        return remote(DA.at[g, rows], dst, s2s.at[g], s2r.at[g], last[g])
+
+    def down_quarter(half):
+        return pl.ds(pl.multiple_of(half * QUARTER_ROWS, QUARTER_ROWS), QUARTER_ROWS)
+
+    def piece_down(g):
+        for copy in loads(g, 2):
+            copy.wait()
+        keep = down_quarter(bit[g])
+        away = down_quarter(1 - bit[g])
+        L[g, quarter, :] = (DL[g, keep, :].astype(F32) + DS[g, keep, :].astype(F32)).astype(BF)
+        DA[g] = (DL[g, away, :].astype(F32) + DS[g, away, :].astype(F32)).astype(BF)
+
+    def piece_swap(c):
+        for g in range(2):
+            first_part(g, c).start()
+
+    def piece_second(c):
+        for g in range(2):
+            second_part(g, c).start()
 
     small_x = remote(st.at[2], sb.at[0], ss.at[0], sr.at[0], px)
     small_y = remote(st.at[0], sb.at[1], ss.at[1], sr.at[1], py)
@@ -729,11 +762,39 @@
     def o_copy(g, i):
         return remote(F.at[g, rows_of(i)], F.at[g, rows_of(i)], sends.at[g, 4], zr.at[g, i], zn)
 
+    def out_rows(g, i):
+        shift = jnp.where(i < cut_at, 0, jnp.where(i < tail_at, bit[g] * QUARTER_ROWS, QUARTER_ROWS))
+        return pl.ds(pl.multiple_of(i * ROWS + shift, ROWS), ROWS)
+
     def x_copy(g, i):
-        return remote(F.at[g, rows_of(i)], outs[g].at[owner[g], rows_of(i)], sends.at[g, 5], xr.at[g], first[g])
+        return remote(F.at[g, rows_of(i)], outs[g].at[owner[g], out_rows(g, i)], sends.at[g, 5], xr.at[g], first[g])
 
     def l_copy(g, i):
-        return pltpu.make_async_copy(F.at[g, rows_of(i)], outs[g].at[owner[g], rows_of(i)], lo.at[g])
+        return pltpu.make_async_copy(F.at[g, rows_of(i)], outs[g].at[owner[g], out_rows(g, i)], lo.at[g])
+
+    def quarter_rows(i):
+        return pl.ds(pl.multiple_of((i - cut_at) * ROWS, ROWS), ROWS)
+
+    def g_copy(g, i):
+        return remote(F.at[g, rows_of(i)], G.at[g, quarter_rows(i)], gs.at[g], gr.at[g, i - cut_at], last[g])
+
+    def pass_on(g, i):
+        rows = pl.ds(pl.multiple_of(i * ROWS + (1 - bit[g]) * QUARTER_ROWS, ROWS), ROWS)
+        src = G.at[g, quarter_rows(i)]
+        g_copy(g, i).wait_recv()
+        remote(src, outs[g].at[owner[g], rows], sends.at[g, 5], xr.at[g], first[g]).start()
+        pltpu.make_async_copy(src, outs[g].at[owner[g], rows], lo.at[g]).start()
+
+    def is_cut(i):
+        return (i >= cut_at) & (i < tail_at)
+
+    def finish(g, i):
+        x_copy(g, i).start()
+        l_copy(g, i).start()
+
+        @pl.when(is_cut(i))
+        def _():
+            g_copy(g, i).start()
 
     def end_in(g, j):
         r = rows_of(j)
@@ -742,26 +803,35 @@
 
     def end_out(g, j):
         o_copy(g, j).wait_recv()
-        x_copy(g, j).start()
-        l_copy(g, j).start()
+        finish(g, j)
 
     def mid_out(g, j):
         a_copy(g, j, others).wait_recv()
         o_copy(g, j).start()
-        x_copy(g, j).start()
-        l_copy(g, j).start()
+        finish(g, j)
 
     def mid_join(g, j):
-        y_copy(g, j).wait_recv()
-        r = rows_of(j)
-        F[g, r, cols_of(mine)] = (R[g, r, :].astype(F32) + Y[g, r, :].astype(F32)).astype(BF)
-        a_copy(g, j, mine).start()
+        @pl.when(jnp.logical_not(is_cut(j)))
+        def _():
+            y_copy(g, j).wait_recv()
+            r = rows_of(j)
+            F[g, r, cols_of(mine)] = (R[g, r, :].astype(F32) + Y[g, r, :].astype(F32)).astype(BF)
+            a_copy(g, j, mine).start()
 
     def mid_half(g, j):
         r_copy(g, j).wait_recv()
         r = rows_of(j)
-        R[g, r, :] = (R[g, r, :].astype(F32) + L[g, r, cols_of(mine)].astype(F32)).astype(BF)
-        y_copy(g, j).start()
+        total = (R[g, r, :].astype(F32) + L[g, r, cols_of(mine)].astype(F32)).astype(BF)
+
+        @pl.when(is_cut(j))
+        def _():
+            F[g, r, cols_of(mine)] = total
+            a_copy(g, j, mine).start()
+
+        @pl.when(jnp.logical_not(is_cut(j)))
+        def _():
+            R[g, r, :] = total
+            y_copy(g, j).start()
 
     def mid_in(g, j):
         z_copy(g, j).wait_recv()
@@ -779,19 +849,19 @@
     width = dl.shape[2]
 
     def piece_rows(c):
-        return pl.ds(c * blk, blk)
+        return pl.ds(pl.multiple_of(c * blk, blk), blk)
 
     def core_copy(c):
         return remote(mine_rows.at[piece_rows(c)], their_rows.at[piece_rows(c)], cs.at[c], cr.at[c], dp, 1 - t)
 
     def norm_loads(c):
         return [
-            pltpu.make_async_copy(xin.at[piece_rows(c)], xc.at[c % 2], xg.at[c % 2, 0]),
-            pltpu.make_async_copy(gmid.at[piece_rows(c)], gc.at[c % 2], xg.at[c % 2, 1]),
+            pltpu.make_async_copy(xin.at[piece_rows(c)], xc.at[lax.rem(c, 2)], xg.at[lax.rem(c, 2), 0]),
+            pltpu.make_async_copy(gmid.at[piece_rows(c)], gc.at[lax.rem(c, 2)], xg.at[lax.rem(c, 2), 1]),
         ]
 
     def ig_copy(c):
-        return pltpu.make_async_copy(ic.at[c % 2], ig.at[piece_rows(c)], io.at[c % 2])
+        return pltpu.make_async_copy(ic.at[lax.rem(c, 2)], ig.at[piece_rows(c)], io.at[lax.rem(c, 2)])
 
     def piece_start():
         for copy in own_loads:
@@ -831,19 +901,25 @@
         st[2] = small_in[...]
 
     def piece_norm(c):
-        if c + 1 < CHUNKS:
+        @pl.when(c + 1 < CHUNKS)
+        def _():
             for copy in norm_loads(c + 1):
                 copy.start()
+
         for copy in norm_loads(c):
             copy.wait()
         core_copy(c).wait_recv()
-        if c >= 2:
+
+        @pl.when(c >= 2)
+        def _():
             ig_copy(c - 2).wait()
+
         r = piece_rows(c)
         grads = mine_rows[r, :].astype(F32) + their_rows[r, :].astype(F32)
-        back, gain_grad = norm_back(xc[c % 2].astype(F32), gain_ref[...], grads)
+        s = lax.rem(c, 2)
+        back, gain_grad = norm_back(xc[s].astype(F32), gain_ref[...], grads)
         st[2, 0:1, :] = st[2, 0:1, :] + gain_grad
-        ic[c % 2] = gc[c % 2] + back
+        ic[s] = gc[s] + back
         ig_copy(c).start()
 
     def small_first():
@@ -860,25 +936,35 @@
         for copy in small_z:
             copy.start()
 
-    pieces = (
-        [piece_start]
-        + [functools.partial(piece_part, c) for c in range(CHUNKS)]
-        + [functools.partial(piece_qk, k) for k in range(2)]
-        + [piece_v, piece_send]
-        + [functools.partial(piece_norm, c) for c in range(CHUNKS)]
-        + [small_first, small_second, small_third]
-    )
+    pieces = [
+        (1, 1, lambda c: piece_down(0)),
+        (2, 1, lambda c: piece_down(1)),
+        (3, QUARTER_ROWS // SWAP_ROWS, piece_second),
+        (3, 1, lambda c: piece_start()),
+        (4, CHUNKS, piece_part),
+        (4 + CHUNKS, 1, lambda c: piece_qk(0)),
+        (5 + CHUNKS, 1, lambda c: piece_qk(1)),
+        (6 + CHUNKS, 1, lambda c: piece_v()),
+        (7 + CHUNKS, 1, lambda c: piece_send()),
+        (8 + CHUNKS, HALF_ROWS // SWAP_ROWS, piece_swap),
+        (9 + CHUNKS, CHUNKS, piece_norm),
+        (10 + 2 * CHUNKS, 1, lambda c: small_first()),
+        (14 + 2 * CHUNKS, 1, lambda c: small_second()),
+        (18 + 2 * CHUNKS, 1, lambda c: small_third()),
+    ]
 
     def body(i, carry):
         for b in range(4):
 
-            @pl.when(i == b * per)
+            @pl.when(i == starts[b])
             def _():
                 for g in range(2):
-                    if b < 3:
+                    if b < 2:
                         for copy in loads(g, b):
                             copy.wait()
-                    if b == 3:
+                    elif b == 2:
+                        second_exchange(g).wait_recv()
+                    else:
                         first_exchange(g).wait_recv()
 
         @pl.when(is_end)
@@ -895,19 +981,18 @@
                 stage(mid_half, g, i - LAGS[1])
                 stage(mid_in, g, i - LAGS[0])
 
-        begin = 2 + SPACE * (CHUNKS + 4)
-        c = (i - begin) // SWAP_STEP
-
-        @pl.when((i >= begin) & (c < HALF_ROWS // SWAP_ROWS) & (lax.rem(i - begin, SWAP_STEP) == 0))
-        def _():
-            for g in range(2):
-                first_part(g, c).start()
-
-        for k, piece in enumerate(pieces):
-
-            @pl.when(i == 1 + SPACE * k)
+        for g in range(2):
+            j = i - LAGS[4] - 2
+
+            @pl.when(is_cut(j))
             def _():
-                piece()
+                pass_on(g, j)
+
+        for begin, steps, piece in pieces:
+
+            @pl.when((i >= begin) & (i < begin + steps))
+            def _():
+                piece(i - begin)
 
         return carry
 
@@ -938,23 +1023,28 @@
         @pl.when(is_mid)
         def _():
             remote(R.at[g], Y.at[g], sends.at[g, 1], rr.at[g, 0], mm).wait_send()
-            remote(R.at[g], Y.at[g], sends.at[g, 2], yr.at[g, 0], last[g]).wait_send()
+            some = pl.ds(0, KEPT_ROWS - QUARTER_ROWS)
+            remote(R.at[g, some], Y.at[g, some], sends.at[g, 2], yr.at[g, 0], last[g]).wait_send()
             remote(R.at[g], Y.at[g], sends.at[g, 3], ar.at[g, 0], mm).wait_send()
             remote(F.at[g], F.at[g], sends.at[g, 4], zr.at[g, 0], zn).wait_send()
 
-        whole = remote(F.at[g], outs[g].at[away], sends.at[g, 5], xr.at[g], first[g])
+        second_exchange(g).wait_send()
+        remote(G.at[g], G.at[g], gs.at[g], gr.at[g, 0], last[g]).wait_send()
+        whole = remote(outs[g].at[away], outs[g].at[away], sends.at[g, 5], xr.at[g], first[g])
         whole.wait_send()
         whole.wait_recv()
-        pltpu.make_async_copy(F.at[g], outs[g].at[owner[g]], lo.at[g]).wait()
+        pltpu.make_async_copy(outs[g].at[owner[g]], outs[g].at[owner[g]], lo.at[g]).wait()
 
 
 def sum_call(gk, rg, uk, ru, late_x, late_y, dk, rd, go, dqkv, w3, xn, xin, gmid, gain, small):
     any_spec = pl.BlockSpec(memory_space=pl.ANY)
-    n = GROUP_ROWS // ROWS
+    n = KEPT_ROWS // ROWS
     rows, dim = xin.shape
     blk = rows // CHUNKS
-    full = pltpu.VMEM((2, GROUP_ROWS, WIDE), BF)
-    half = pltpu.VMEM((2, GROUP_ROWS, WIDE // 2), BF)
+    full = pltpu.VMEM((2, KEPT_ROWS, WIDE), BF)
+    half = pltpu.VMEM((2, KEPT_ROWS, WIDE // 2), BF)
+    quarter = pltpu.VMEM((2, QUARTER_ROWS, WIDE), BF)
+    down = pltpu.VMEM((2, HALF_ROWS, WIDE), BF)
     dma = pltpu.SemaphoreType.DMA
     return pl.pallas_call(
         sum_body,
@@ -963,7 +1053,7 @@
         in_specs=[any_spec] * 14 + [whole_spec()] * 2,
         out_specs=[any_spec] * 3 + [whole_spec()],
         scratch_shapes=[
-            full, full, full, half, half,
+            full, full, full, half, half, down, down, quarter, quarter,
             pltpu.VMEM((6, SMALL, WIDE), F32),
             pltpu.VMEM((3, SMALL, WIDE), F32),
             pltpu.VMEM(dqkv.shape, BF),
@@ -979,6 +1069,7 @@
             dma((2, n)), dma((2, n)), dma((2, n)), dma((2, n)),
             dma((2,)), dma((2,)), dma((5,)), dma((6,)),
             dma((3,)), dma((CHUNKS,)), dma((CHUNKS,)), dma((2, 2)), dma((2,)),
+            dma((2,)), dma((2,)), dma((2,)), dma((2, QUARTER_ROWS // ROWS)),
         ],
         compiler_params=pltpu.CompilerParams(collective_id=4, has_side_effects=True, vmem_limit_bytes=VMEM_LIMIT),
         name="grad_sum",

time: 415 us -> 389 us (0.937)
  Pallas kernels: 392 us -> 367 us
    pallas_call x1, Pallas kernels: 223 us -> 210 us  [sum_call(): pl.pallas_call(sum_body, out_shape=[jax.ShapeDtypeStruct((2, GROUP_ROWS,...]
    pallas_call x1, Pallas kernels: 39.1 us -> 27.1 us  [attn_bwd_call(): pl.pallas_call(attn_bwd_body, grid=(pairs,), out_shape=[jax.ShapeDtypeStr...]
  transfers between devices with their start and end apart: 2 -> 2, of which waited for: 0 -> 0; matrix products, arithmetic and copies ran while one was open for 1% -> 1% of each run, Pallas kernels for 13% -> 11%
where the time goes in v5:
time: 389 us
  Pallas kernels  367 us (94%)
  local copies, waits for them, and re-layouts  9.8 us (3%)
  other arithmetic  9.13 us (2%)
    pallas_call x1, Pallas kernels, sum_call(): pl.pallas_call(sum_body, out_shape=[jax.ShapeDtypeStruct((2, GROUP_ROWS,...  210 us
    pallas_call x1, Pallas kernels, ffn_call(): pl.pallas_call(ffn_body, grid=(hidden // blk,), in_specs=[full, full, col...  56.1 us
    pallas_call x1, Pallas kernels, attn_bwd_call(): pl.pallas_call(attn_bwd_body, grid=(pairs,), out_shape=[jax.ShapeDtypeStr...  27.1 us
    pallas_call x1, Pallas kernels, attn_fwd_call(): pl.pallas_call(attn_fwd_body, grid=(pairs,), out_shape=[jax.ShapeDtypeStr...  23.1 us
    pallas_call x1, Pallas kernels, widen_call(): pl.pallas_call(widen_body, grid=(2 * half,), out_shape=[jax.ShapeDtypeStr...  17 us
    pallas_call x1, Pallas kernels, ffn_back_call(): pl.pallas_call(ffn_back_body, out_shape=[jax.ShapeDtypeStruct((rows, dim)...  15.5 us
    pallas_call x1, Pallas kernels, attn_out_call(): pl.pallas_call(attn_out_body, out_shape=[jax.ShapeDtypeStruct((rows, dim)...  9.85 us
    pallas_call x1, Pallas kernels, qkv_call(): pl.pallas_call(qkv_body, grid=(rows // blk,), out_shape=[jax.ShapeDtypeSt...  7.97 us
  transfers between devices with their start and end apart: 2, of which 0 were waited for; matrix products, arithmetic and copies ran while one was open for 1% of the time, Pallas kernels for 11%

profile of v5, /device:TPU:0, one launch (start us, length us, event | category | flops | bytes accessed | tf_op | source)
XLA Modules:
  0.0 388.7 jit_solution(3979543431809583000)
XLA Ops:
  0.7 0.8 subtract_reduce_fusion
  1.7 0.7 convert_element_type.8
  2.4 3.1 fusion
  5.5 8.0 %qkv.1 = (bf16[1024,1024]{1,0:T(8,128)(2,1)}, bf16[1024,512]{1,0:T(8,128)(2,1)}, bf16[1024,512]{1,0:T(8,128)(2,1)}, bf16[1024,512]{1,0:T(8,128)(2,1)}) custom-call(bf16[1024,1024]{1,0:T(8,128)(2,1)} %xin.1, f32[1,1024]{1,0:T(1,128)} %bitcast.35, bf16[3,1024,512]{2,1,0:T(8,128)(2,1)} %bitcast.29, f32[1024,128]{1,0:T(8,128)} %get-tuple-element.87.cos_ref, ...), custom_call_target="tpu_custom_call" | custom-call | tf_op jit(solution)/shard_map/qkv/pallas_call | solution.py:86
  13.4 0.7 select_select_fusion.bias_ref
  14.1 1.4 select_convert_fusion
  15.6 23.1 %attn_fwd.1 = (bf16[1024,512]{1,0:T(8,128)(2,1)}, f32[1024,512]{1,0:T(8,128)}, bf16[4,2,1024,128]{3,2,1,0:T(8,128)(2,1)}, bf16[1024,2048]{1,0:T(8,128)(2,1)}, bf16[1024,2048]{1,0:T(8,128)(2,1)}) custom-call(bf16[1024,512]{1,0:T(8,128)(2,1)} %get-tuple-element.45.q_ref, bf16[1024,512]{1,0:T(8,128)(2,1)} %get-tuple-element.46.k_ref, ...), custom_call_target="tpu_custom_call" | custom-call | tf_op jit(solution)/shard_map/attn_fwd/pallas_call | solution.py:152
  38.7 9.8 %attn_out.1 = (f32[1024,1024]{1,0:T(8,128)}, bf16[1024,1024]{1,0:T(8,128)(2,1)}) custom-call(bf16[1024,1024]{1,0:T(8,128)(2,1)} %xin.1, bf16[1024,512]{1,0:T(8,128)(2,1)} %get-tuple-element.48.o_ref.at_ref, bf16[512,1024]{1,0:T(8,128)(2,1)} %w_ref.3, f32[1,1024]{1,0:T(1,128)} %bitcast.32), custom_call_target="tpu_custom_call" | custom-call | tf_op jit(solution)/shard_map/attn_out/pallas_call | solution.py:285
  48.5 56.1 %ffn.1 = (bf16[1024,1024]{1,0:T(8,128)(2,1)}, bf16[1024,1024]{1,0:T(8,128)(2,1)}, bf16[2,512,1024]{2,1,0:T(8,128)(2,1)}, bf16[2,512,1024]{2,1,0:T(8,128)(2,1)}, ...) custom-call(bf16[1024,1024]{1,0:T(8,128)(2,1)} %get-tuple-element.49, ...), custom_call_target="tpu_custom_call" | custom-call | tf_op jit(solution)/shard_map/ffn/pallas_call | solution.py:465
  104.6 1.6 collective-permute-start
  106.8 15.5 %ffn_back.1 = (bf16[1024,1024]{1,0:T(8,128)(2,1)}, f32[1024,1024]{1,0:T(8,128)}, bf16[1024,512]{1,0:T(8,128)(2,1)}, bf16[512,1024]{1,0:T(8,128)(2,1)}, f32[1,1024]{1,0:T(1,128)}) custom-call(bf16[1024,1024]{1,0:T(8,128)(2,1)} %get-tuple-element.52.gx_ref, bf16[1024,1024]{1,0:T(8,128)(2,1)} %get-tuple-element.53.fo_ref, ...), custom_call_target="tpu_custom_call" | custom-call | tf_op jit(solution)/shard_map/ffn_back/pallas_call | solution.py:590
  122.4 0.6 pad_maximum_fusion.oh_ref
  123.1 27.1 %attn_bwd.1 = (bf16[3,1024,512]{2,1,0:T(8,128)(2,1)}, f32[4,2,2,8,256]{4,3,2,1,0:T(8,128)}) custom-call(bf16[1024,512]{1,0:T(8,128)(2,1)} %get-tuple-element.45.q_ref, bf16[1024,512]{1,0:T(8,128)(2,1)} %get-tuple-element.46.k_ref, bf16[1024,512]{1,0:T(8,128)(2,1)} %get-tuple-element.47.v_ref, bf16[1024,512]{1,0:T(8,128)(2,1)} %get-tuple-element.65.do_ref, ...), custom_call_target="tpu_custom_call" | custom-call | tf_op jit(solution)/shard_map/attn_bwd/pallas_call | solution.py:225
  150.2 1.0 reduce_sum.9
  151.4 0.7 fusion.2.small_in
  152.1 1.1 copy-done.2
  153.7 210.2 %grad_sum.1 = (bf16[2,2048,1024]{2,1,0:T(8,128)(2,1)}, bf16[2,2048,1024]{2,1,0:T(8,128)(2,1)}, f32[1024,1024]{1,0:T(8,128)}, f32[8,1024]{1,0:T(8,128)}) custom-call(bf16[2,512,1024]{2,1,0:T(8,128)(2,1)} %get-tuple-element.56.gk, bf16[512,1024]{1,0:T(8,128)(2,1)} %get-tuple-element.57.rg, bf16[2,512,1024]{2,1,0:T(8,128)(2,1)} %get-tuple-element.58.uk, ...), custom_call_target="tpu_custom_call" | custom-call | tf_op jit(solution)/shard_map/grad_sum/pallas_call | solution.py:1049
  364.0 0.7 slice_reduce_fusion
  364.7 1.4 fusion.9
  366.1 0.6 reshape_squeeze.3
  366.7 17.0 %widen.1 = (f32[1024,32,128]{2,1,0:T(8,128)}, f32[8,2,2,64,1024]{4,3,2,1,0:T(8,128)}, f32[3,1024,512]{2,1,0:T(8,128)}, f32[512,1024]{1,0:T(8,128)}) custom-call(bf16[2,4,512,1024]{3,2,1,0:T(8,128)(2,1)} %bitcast.26, bf16[2,4,512,1024]{3,2,1,0:T(8,128)(2,1)} %bitcast.22, bf16[2,4,512,1024]{3,2,1,0:T(8,128)(2,1)} %bitcast.27, ...), custom_call_target="tpu_custom_call" | custom-call | tf_op jit(solution)/shard_map/widen/pallas_call | solution.py:517
  383.8 1.3 copy.31
  385.1 1.6 copy-done
  386.7 2.0 copy.32
  (34 shorter events, 1.6 us)
Async XLA Ops:
  5.5 8.7 %copy-start.4 = (s32[1024]{0:T(1024)S(1)}, s32[1024]{0:T(1024)}, u32[]{:S(2)}) copy-start(s32[1024]{0:T(1024)} %param.14) | copy-start | bytes 12292
  5.5 8.7 %copy-start.5 = (s32[1024]{0:T(1024)S(1)}, s32[1024]{0:T(1024)}, u32[]{:S(2)}) copy-start(s32[1024]{0:T(1024)} %param.13) | copy-start | bytes 12292
  104.6 47.4 %collective-permute-start = (bf16[768,1024]{1,0:T(8,128)(2,1)}, bf16[768,1024]{1,0:T(8,128)(2,1)S(1)}, u32[]{:S(2)}, u32[]{:S(2)}) collective-permute-start(bf16[768,1024]{1,0:T(8,128)(2,1)} %get-tuple-element.60), channel_id=1, source_target_pairs={{0,2},{2,0},{4,6},{6,4},{8,10},{10,8},{12,14},{14,12},{16,18},{18,... | collective-permute-start | bytes 4718600 | tf_op jit(solution)/shard_map/ppermute | solution.py:1120
  106.2 45.9 %collective-permute-start.1 = (bf16[768,1024]{1,0:T(8,128)(2,1)}, bf16[768,1024]{1,0:T(8,128)(2,1)S(1)}, u32[]{:S(2)}, u32[]{:S(2)}) collective-permute-start(bf16[768,1024]{1,0:T(8,128)(2,1)} %get-tuple-element.61), channel_id=1, source_target_pairs={{0,4},{2,6},{4,0},{6,2},{8,12},{10,14},{12,8},{14,10},{16,20},{18,... | collective-permute-start | bytes 4718600 | tf_op jit(solution)/shard_map/ppermute | solution.py:1121
  123.1 28.3 %copy-start.6 = (f32[1,1024]{1,0:T(1,128)S(1)}, f32[1,1024]{1,0:T(1,128)}, u32[]{:S(2)}) copy-start(f32[1,1024]{1,0:T(1,128)} %get-tuple-element.71) | copy-start | bytes 12292
  152.1 1.1 copy-start.2
  152.1 1.7 copy-start.3
  366.7 17.0 %copy-start.1 = (bf16[1024,1024]{1,0:T(8,128)(2,1)S(1)}, bf16[1024,1024]{1,0:T(8,128)(2,1)}, u32[]{:S(2)}) copy-start(bf16[1024,1024]{1,0:T(8,128)(2,1)} %get-tuple-element.110) | copy-start | bytes 6291460
  383.7 2.9 copy-start

commit v6 on v5

--- a/solution.py
+++ b/solution.py
@@ -29,6 +29,7 @@
 KEPT_ROWS = GROUP_ROWS - QUARTER_ROWS
 WIDE = 1024
 SMALL = 8
+QBLK = 256
 FFN_ROWS = 512
 FFN_COLS = 256
 
@@ -111,6 +112,12 @@
             (wg_ref, wu_ref)[k % 2][:, s * LANES : (s + 1) * LANES] = turned[k].astype(BF)
     blk = 256
     lane = lax.broadcasted_iota(jnp.int32, (blk, LANES), 1)
+    kind = lax.broadcasted_iota(jnp.int32, (1, LANES), 1) // VAR_COLS
+    bias_rows = []
+    for h in range(2):
+        head = pl.program_id(0) * 2 + h
+        hi, mid, low = split3(jnp.full((1, LANES), bias_ref[0, head] - bias_ref[1, head], F32))
+        bias_rows.append(jnp.where(kind == 0, hi, jnp.where(kind == 1, mid, jnp.where(kind == 2, low, 0.0))))
     kx = jnp.concatenate([k_ref[...], extk_ref[...]], axis=1)
     ones = jnp.ones((rows, LANES), BF)
     vx = jnp.concatenate([v_ref[...], ones], axis=1)
@@ -121,7 +128,7 @@
         segq = segq_ref[sl, :]
         outs = []
         for h in range(2):
-            ext = base * bias_ref[0, h : h + 1, :] + segq
+            ext = base * bias_rows[h] + segq
             mine = (lane >= HEAD) if h else (lane < HEAD)
             qx = jnp.concatenate([jnp.where(mine, q, 0.0), ext], axis=1).astype(BF)
             s = dot_nt(qx, kx)
@@ -141,7 +148,7 @@
         o_ref[sl, :] = o.astype(BF)
 
 
-def attn_fwd_call(q, k, v, base, segq, extk, bias_rows, w_pairs):
+def attn_fwd_call(q, k, v, base, segq, extk, head_bias, w_pairs):
     rows, width = q.shape
     pairs = width // LANES
     dim, tiles, _ = w_pairs.shape
@@ -161,21 +168,22 @@
         ],
         in_specs=[
             col, col, col, full, full, full,
-            pl.BlockSpec((1, 2, LANES), lambda p: (p, 0, 0)),
+            pl.BlockSpec(memory_space=pltpu.SMEM),
             pl.BlockSpec((share, tiles, LANES), lambda p: (p, 0, 0)),
         ],
         out_specs=[col, col, pl.BlockSpec((1, 2, rows, LANES), lambda p: (p, 0, 0, 0)), half_w, half_w],
         compiler_params=pltpu.CompilerParams(vmem_limit_bytes=VMEM_LIMIT),
         name="attn_fwd",
-    )(q, k, v, base, segq, extk, bias_rows, w_pairs)
+    )(q, k, v, base, segq, extk, head_bias, w_pairs)
 
 
 def attn_bwd_body(
-    q_ref, k_ref, v_ref, do_ref, o32_ref, extq_ref, extk_ref, oh_ref, cos_ref, sin_ref, d_ref, gb_ref, dqt_ref
+    q_ref, k_ref, v_ref, do_ref, o32_ref, extq_ref, extk_ref, var_ref, cos_ref, sin_ref, d_ref, gb_ref, dqt_ref
 ):
     rows = q_ref.shape[0]
     blk = 256
     lane = lax.broadcasted_iota(jnp.int32, (blk, LANES), 1)
+    kinds = lax.broadcasted_iota(jnp.int32, (8, blk), 0)
     kx = jnp.concatenate([k_ref[...], extk_ref[...]], axis=1)
     kxt = kx.T
     lane_all = lax.broadcasted_iota(jnp.int32, (rows, LANES), 1)
@@ -203,9 +211,9 @@
             dqt = dot_nn(kxt, dst)
             dqt_ref[h * HEAD : (h + 1) * HEAD, sl] = dqt[h * HEAD : (h + 1) * HEAD, :]
             g = dqt[LANES : LANES + 8, :]
-            oh = oh_ref[0, :, sl]
-            same = same + g * oh
-            other = other + g * oh_ref[1, :, sl]
+            match = kinds == var_ref[:, sl]
+            same = same + jnp.where(match, g, 0.0)
+            other = other + jnp.where(match | (kinds >= VAR_COLS), 0.0, g)
         gb_ref[0, h, 0] = same
         gb_ref[0, h, 1] = other
     cosine = cos_ref[...]
@@ -216,7 +224,7 @@
     d_ref[2] = dv.astype(BF)
 
 
-def attn_bwd_call(q, k, v, do, o32, extq, extk, onehot, cosine, sine):
+def attn_bwd_call(q, k, v, do, o32, extq, extk, variates, cosine, sine):
     rows, width = q.shape
     pairs = width // LANES
     col = pl.BlockSpec((rows, LANES), lambda p: (0, p))
@@ -230,14 +238,14 @@
             col, col, col, col, col,
             pl.BlockSpec((1, 2, rows, LANES), lambda p: (p, 0, 0, 0)),
             full,
-            pl.BlockSpec((2, 8, rows), lambda p: (0, 0, 0)),
+            pl.BlockSpec((1, rows), lambda p: (0, 0)),
             full, full,
         ],
         out_specs=[pl.BlockSpec((3, rows, LANES), lambda p: (0, 0, p)), pl.BlockSpec((1, 2, 2, 8, blk), lambda p: (p, 0, 0, 0, 0))],
         scratch_shapes=[pltpu.VMEM((LANES, rows), F32)],
         compiler_params=pltpu.CompilerParams(vmem_limit_bytes=VMEM_LIMIT),
         name="attn_bwd",
-    )(q, k, v, do, o32, extq, extk, onehot, cosine, sine)
+    )(q, k, v, do, o32, extq, extk, variates, cosine, sine)
 
 
 def partner_barrier():
@@ -488,7 +496,10 @@
     return tiled.reshape(dim, two * width // LANES, LANES)
 
 
-def widen_body(ga_ref, gb_ref, da_ref, db_ref, aa_ref, v_ref, o_ref, gu_ref, down_ref, qkv_ref, out_ref):
+def widen_body(
+    ga_ref, gb_ref, da_ref, db_ref, aa_ref, v_ref, o_ref, small_ref,
+    gu_ref, down_ref, qkv_ref, out_ref, g1_ref, g2_ref, gbias_ref,
+):
     tiles = WIDE // LANES
     for f in range(2):
         for q in range(tiles // 4):
@@ -506,15 +517,30 @@
     qkv_ref[2] = v_ref[0, 0].astype(F32)
     out_ref[...] = o_ref[0, 0].astype(F32)
 
-
-def widen_call(a, b):
+    @pl.when(pl.program_id(0) == 0)
+    def _():
+        g1_ref[...] = small_ref[0:1, :]
+        g2_ref[...] = small_ref[1:2, :]
+        row = lax.broadcasted_iota(jnp.int32, gbias_ref.shape, 0)
+        col = lax.broadcasted_iota(jnp.int32, gbias_ref.shape, 1)
+        total = jnp.zeros(gbias_ref.shape, F32)
+        for h in range(gbias_ref.shape[1]):
+            for s in range(2):
+                at = (h % 2 * 2 + s) * QBLK
+                one = jnp.sum(small_ref[2 + h // 2 : 3 + h // 2, at : at + QBLK], axis=1, keepdims=True)
+                total = jnp.where((row == s) & (col == h), one, total)
+        gbias_ref[...] = total
+
+
+def widen_call(a, b, small, heads):
     blk = 256
     half = HALF_ROWS // blk
     tiles = 4 * WIDE // LANES
     width = WIDE // 2
     gate = pl.BlockSpec((1, 2, blk, WIDE), lambda i: (i // half, 0, lax.rem(i, half), 0))
     block = lambda n: pl.BlockSpec((1, 1, blk, WIDE), lambda i: (i // half, n, lax.rem(i, half), 0))
-    gu, down, qkv, out = pl.pallas_call(
+    fixed = lambda shape: pl.BlockSpec(shape, lambda i: (0, 0))
+    gu, down, qkv, out, g1, g2, gbias = pl.pallas_call(
         widen_body,
         grid=(2 * half,),
         out_shape=[
@@ -522,23 +548,30 @@
             jax.ShapeDtypeStruct((HALF_ROWS // PART, 2, 2, PART, WIDE), F32),
             jax.ShapeDtypeStruct((3, 2 * HALF_ROWS, width), F32),
             jax.ShapeDtypeStruct((HALF_ROWS, WIDE), F32),
+            jax.ShapeDtypeStruct((1, WIDE), F32),
+            jax.ShapeDtypeStruct((1, WIDE), F32),
+            jax.ShapeDtypeStruct((2, heads), F32),
         ],
         in_specs=[
             gate, gate, block(2), block(2), block(3),
             pl.BlockSpec((1, 1, blk, width), lambda i: (0, 3, lax.rem(i, half), i // half)),
             pl.BlockSpec((1, 1, blk // 2, WIDE), lambda i: (1, 3, i, 0)),
+            fixed((SMALL, WIDE)),
         ],
         out_specs=[
             pl.BlockSpec((blk, tiles, LANES), lambda i: (i, 0, 0)),
             pl.BlockSpec((blk // PART, 2, 1, PART, WIDE), lambda i: (lax.rem(i, half), 0, i // half, 0, 0)),
             pl.BlockSpec((3, blk, width), lambda i: (0, i, 0)),
             pl.BlockSpec((blk // 2, WIDE), lambda i: (i, 0)),
+            fixed((1, WIDE)),
+            fixed((1, WIDE)),
+            fixed((2, heads)),
         ],
         compiler_params=pltpu.CompilerParams(vmem_limit_bytes=VMEM_LIMIT),
         name="widen",
-    )(a, b, a, b, a, b, b)
+    )(a, b, a, b, a, b, b, small)
     gu = jnp.transpose(gu.reshape(2 * HALF_ROWS, tiles // 2, 2, LANES), (0, 2, 1, 3)).reshape(2 * HALF_ROWS, 2, 2 * WIDE)
-    return gu, down.reshape(4 * HALF_ROWS, WIDE), qkv, out
+    return gu, down.reshape(4 * HALF_ROWS, WIDE), qkv, out, g1, g2, gbias
 
 
 def norm_back(rows_now, gain, grads):
@@ -550,64 +583,91 @@
 
 
 def ffn_back_body(
-    gx_ref, fo_ref, mid_ref, ct_ref, gain_ref, w_ref, at_ref,
-    out_ref, gm_ref, do_ref, gw_ref, gg_ref, gx_in, fo_in, gb, ssem, rsem,
+    gain_ref, w_ref, at_ref, gx, fo, mid, ct,
+    do_ref, gw_ref, gg_ref, out, gm,
+    gx_in, fo_in, gx_v, fo_v, mid_v, ct_v, gm_v, out_v, gb, ssem, rsem, lsem, osem,
 ):
+    rows = mid.shape[0]
+    blk = rows // CHUNKS
+
+    def rows_of(c):
+        return pl.ds(c * blk, blk)
+
+    loads = [
+        [
+            pltpu.make_async_copy(src.at[rows_of(c)], dst.at[rows_of(c)], lsem.at[k, c])
+            for k, (src, dst) in enumerate(((gx, gx_v), (mid, mid_v), (ct, ct_v), (fo, fo_v)))
+        ]
+        for c in range(CHUNKS)
+    ]
+    for c in range(CHUNKS):
+        for copy in loads[c]:
+            copy.start()
     peer = partner_barrier()
-    rows = mid_ref.shape[0]
-    blk = rows // CHUNKS
     copies = []
-    for n, (src, dst) in enumerate(((gx_ref, gx_in), (fo_ref, fo_in))):
+    for n, (src, dst) in enumerate(((gx, gx_in), (fo, fo_in))):
         for c in range(CHUNKS):
             at = n * CHUNKS + c
-            copy = send_rows(src, dst, pl.ds(c * blk, blk), ssem.at[at], rsem.at[at], peer)
+            copy = send_rows(src, dst, rows_of(c), ssem.at[at], rsem.at[at], peer)
             copy.start()
             copies.append(copy)
-    gain_sum = jnp.zeros((1, mid_ref.shape[1]), F32)
+    stores = []
+    gain_sum = jnp.zeros((1, mid.shape[1]), F32)
     for c in range(CHUNKS):
         sl = slice(c * blk, (c + 1) * blk)
+        for copy in loads[c][:3]:
+            copy.wait()
         copies[c].wait_recv()
-        grads = gx_ref[sl, :].astype(F32) + gx_in[sl, :].astype(F32)
-        back, gain_grad = norm_back(mid_ref[sl, :], gain_ref[...], grads)
+        grads = gx_v[sl, :].astype(F32) + gx_in[sl, :].astype(F32)
+        back, gain_grad = norm_back(mid_v[sl, :], gain_ref[...], grads)
         gain_sum = gain_sum + gain_grad
-        gm = ct_ref[sl, :].astype(F32) + back
-        gm_ref[sl, :] = gm
-        gb[sl, :] = gm.astype(BF)
+        grad_mid = ct_v[sl, :].astype(F32) + back
+        gm_v[sl, :] = grad_mid
+        stores.append(pltpu.make_async_copy(gm_v.at[rows_of(c)], gm.at[rows_of(c)], osem.at[0, c]))
+        stores[-1].start()
+        gb[sl, :] = grad_mid.astype(BF)
         do_ref[sl, :] = dot_nt(gb[sl, :], w_ref[...]).astype(BF)
     gg_ref[...] = gain_sum
-    gw_ref[...] = dot_tn(at_ref[...], gb[...]).astype(BF)
     for c in range(CHUNKS):
         sl = slice(c * blk, (c + 1) * blk)
+        loads[c][3].wait()
         copies[CHUNKS + c].wait_recv()
-        out_ref[sl, :] = (mid_ref[sl, :] + (fo_ref[sl, :].astype(F32) + fo_in[sl, :].astype(F32))).astype(BF)
+        out_v[sl, :] = (mid_v[sl, :] + (fo_v[sl, :].astype(F32) + fo_in[sl, :].astype(F32))).astype(BF)
+        stores.append(pltpu.make_async_copy(out_v.at[rows_of(c)], out.at[rows_of(c)], osem.at[1, c]))
+        stores[-1].start()
+    gw_ref[...] = dot_tn(at_ref[...], gb[...]).astype(BF)
     for copy in copies:
         copy.wait_send()
+    for copy in stores:
+        copy.wait()
 
 
 def ffn_back_call(gx, fo, mid, ct, gain, w, at):
     rows, dim = mid.shape
     width = w.shape[0]
-    return pl.pallas_call(
+    any_spec = pl.BlockSpec(memory_space=pl.ANY)
+    low = pltpu.VMEM((rows, dim), BF)
+    wide = pltpu.VMEM((rows, dim), F32)
+    dma = pltpu.SemaphoreType.DMA
+    do, gw, gg, out, gm = pl.pallas_call(
         ffn_back_body,
         out_shape=[
-            jax.ShapeDtypeStruct((rows, dim), BF),
-            jax.ShapeDtypeStruct((rows, dim), F32),
             jax.ShapeDtypeStruct((rows, width), BF),
             jax.ShapeDtypeStruct((width, dim), BF),
             jax.ShapeDtypeStruct((1, dim), F32),
+            jax.ShapeDtypeStruct((rows, dim), BF),
+            jax.ShapeDtypeStruct((rows, dim), F32),
         ],
-        in_specs=[whole_spec()] * 7,
-        out_specs=[whole_spec()] * 5,
+        in_specs=[whole_spec()] * 3 + [any_spec] * 4,
+        out_specs=[whole_spec()] * 3 + [any_spec] * 2,
         scratch_shapes=[
-            pltpu.VMEM((rows, dim), BF),
-            pltpu.VMEM((rows, dim), BF),
-            pltpu.VMEM((rows, dim), BF),
-            pltpu.SemaphoreType.DMA((2 * CHUNKS,)),
-            pltpu.SemaphoreType.DMA((2 * CHUNKS,)),
+            low, low, low, low, wide, low, wide, low, low,
+            dma((2 * CHUNKS,)), dma((2 * CHUNKS,)), dma((4, CHUNKS)), dma((2, CHUNKS)),
         ],
         compiler_params=pltpu.CompilerParams(collective_id=2, has_side_effects=True, vmem_limit_bytes=VMEM_LIMIT),
         name="ffn_back",
-    )(gx, fo, mid, ct, gain, w, at)
+    )(gain, w, at, gx, fo, mid, ct)
+    return out, gm, do, gw, gg
 
 
 def peers_of(dp):
@@ -619,7 +679,7 @@
 
 
 def sum_body(
-    gk, rg, uk, ru, late_x, late_y, dk, rd, go, dqkv, w3, xn, xin, gmid, gain_ref, small_in, out_a, out_b, ig, small_out,
+    gk, rg, uk, ru, late_x, late_y, dk, rd, go, dqkv, w3, xn, xin, gmid, gain_ref, gain2_ref, bias_ref, out_a, out_b, ig, small_out,
     L, S, Z, R, Y, DL, DS, DA, G, sb, st, dl, wb, xb, mine_rows, their_rows, away_rows, xc, gc, ic,
     loc, s1s, s1r, sends, zr, rr, yr, ar, xr, lo, ss, sr, ld, cs, cr, xg, io, s2s, s2r, gs, gr,
 ):
@@ -898,7 +958,11 @@
         out_load_do(lambda copy: copy.wait())
         for copy in norm_loads(0):
             copy.start()
-        st[2] = small_in[...]
+        st[2] = jnp.zeros((SMALL, WIDE), F32)
+        st[2, 1:2, :] = gain2_ref[...]
+        for p in range(bias_ref.shape[0]):
+            sums = [jnp.sum(bias_ref[p, h, s], axis=0, keepdims=True) for h in range(2) for s in range(2)]
+            st[2, 2 + p : 3 + p, :] = jnp.concatenate(sums, axis=1)
 
     def piece_norm(c):
         @pl.when(c + 1 < CHUNKS)
@@ -1036,7 +1100,7 @@
         pltpu.make_async_copy(outs[g].at[owner[g]], outs[g].at[owner[g]], lo.at[g]).wait()
 
 
-def sum_call(gk, rg, uk, ru, late_x, late_y, dk, rd, go, dqkv, w3, xn, xin, gmid, gain, small):
+def sum_call(gk, rg, uk, ru, late_x, late_y, dk, rd, go, dqkv, w3, xn, xin, gmid, gain, gain2, bias):
     any_spec = pl.BlockSpec(memory_space=pl.ANY)
     n = KEPT_ROWS // ROWS
     rows, dim = xin.shape
@@ -1050,7 +1114,7 @@
         sum_body,
         out_shape=[jax.ShapeDtypeStruct((2, GROUP_ROWS, WIDE), BF)] * 2
         + [jax.ShapeDtypeStruct((rows, dim), F32), jax.ShapeDtypeStruct((SMALL, WIDE), F32)],
-        in_specs=[any_spec] * 14 + [whole_spec()] * 2,
+        in_specs=[any_spec] * 14 + [whole_spec()] * 3,
         out_specs=[any_spec] * 3 + [whole_spec()],
         scratch_shapes=[
             full, full, full, half, half, down, down, quarter, quarter,
@@ -1073,7 +1137,7 @@
         ],
         compiler_params=pltpu.CompilerParams(collective_id=4, has_side_effects=True, vmem_limit_bytes=VMEM_LIMIT),
         name="grad_sum",
-    )(gk, rg, uk, ru, late_x, late_y, dk, rd, go, dqkv, w3, xn, xin, gmid, gain, small)
+    )(gk, rg, uk, ru, late_x, late_y, dk, rd, go, dqkv, w3, xn, xin, gmid, gain, gain2, bias)
 
 
 def tables(time_ids):
@@ -1084,7 +1148,7 @@
     return jnp.cos(angles), jnp.sin(angles) * sign[None, :]
 
 
-def mask_tables(segments, variates, head_bias):
+def mask_tables(segments, variates):
     lane = jnp.arange(LANES)[None, :]
     var_here = (lane % VAR_COLS == variates[:, None]) & (lane < 3 * VAR_COLS)
     seg_here = (lane - SEG_COL == segments[:, None]) & (lane >= SEG_COL) & (lane < ONE_COL)
@@ -1093,16 +1157,7 @@
     base = jnp.where(var_here, 1.0, 0.0)
     segq = jnp.where(seg_cols & ~seg_here, MASKED, 0.0)
     extk = jnp.where(var_here | seg_here | ones, 1.0, 0.0).astype(BF)
-    gap = head_bias[0] - head_bias[1]
-    hi = lax.reduce_precision(gap, 8, 7)
-    mid = lax.reduce_precision(gap - hi, 8, 7)
-    low = gap - hi - mid
-    kind = lane // VAR_COLS
-    rows = jnp.where(kind == 0, hi[:, None], jnp.where(kind == 1, mid[:, None], jnp.where(kind == 2, low[:, None], 0.0)))
-    match = jnp.arange(8)[:, None] == variates[None, :]
-    valid = jnp.arange(8)[:, None] < VAR_COLS
-    onehot = jnp.stack([jnp.where(match, 1.0, 0.0), jnp.where(valid & ~match, 1.0, 0.0)])
-    return base, segq, extk, rows.reshape(-1, 2, LANES), onehot
+    return base, segq, extk
 
 
 def fast_local(
@@ -1110,11 +1165,11 @@
 ):
     w3 = jnp.transpose(w_qkv, (1, 0, 2))
     cosine, sine = tables(time_ids)
-    base, segq, extk, bias_rows, onehot = mask_tables(segments, variates, head_bias)
+    base, segq, extk = mask_tables(segments, variates)
     gain1 = attn_gain[None, :]
     gain2 = ffn_gain[None, :]
     xn, q, k, v = qkv_call(block_input, gain1, w3, cosine, sine)
-    attended, o32, extq, wg, wu = attn_fwd_call(q, k, v, base, segq, extk, bias_rows, pair_rows(w_gate_up))
+    attended, o32, extq, wg, wu = attn_fwd_call(q, k, v, base, segq, extk, head_bias, pair_rows(w_gate_up))
     mid, xn2 = attn_out_call(block_input, attended, w_out, gain2)
     ffn_part, gx_part, gk, uk, rg, ru, dk, rd, late_x, late_y = ffn_call(xn2, cotangent, wg, wu, w_down)
     late_x = lax.ppermute(late_x, "dp", [(d, d ^ 1) for d in range(16)])
@@ -1122,21 +1177,16 @@
     block_output, grad_mid, do, g_out, g_gain2 = ffn_back_call(
         gx_part, ffn_part, mid, cotangent, gain2, w_out, attended
     )
-    dqkv, gb = attn_bwd_call(q, k, v, do, o32, extq, extk, onehot, cosine, sine)
-    g_bias = jnp.sum(gb, axis=(3, 4)).reshape(-1, 2).T
-    heads = g_bias.shape[1]
-    bias_row = jnp.pad(g_bias.reshape(1, -1), ((0, 0), (0, WIDE - 2 * heads)))
-    zero = jnp.zeros((1, WIDE), F32)
-    small = jnp.concatenate([zero, g_gain2, bias_row, jnp.zeros((SMALL - 3, WIDE), F32)], axis=0)
+    dqkv, g_bias = attn_bwd_call(q, k, v, do, o32, extq, extk, variates[None, :], cosine, sine)
     sum_a, sum_b, input_grad, small = sum_call(
-        gk, rg, uk, ru, late_x, late_y, dk, rd, g_out, dqkv, w3, xn, block_input, grad_mid, gain1, small
+        gk, rg, uk, ru, late_x, late_y, dk, rd, g_out, dqkv, w3, xn, block_input, grad_mid, gain1, g_gain2, g_bias
     )
     sum_a = sum_a.reshape(2, 4, HALF_ROWS, WIDE)
     sum_b = sum_b.reshape(2, 4, HALF_ROWS, WIDE)
-    g_gate_up, g_down, g_qkv, g_out = widen_call(sum_a, sum_b)
-    g_bias = small[2, : 2 * heads].reshape(2, heads)
+    heads = head_bias.shape[1]
+    g_gate_up, g_down, g_qkv, g_out, g_gain1, g_gain2, g_bias = widen_call(sum_a, sum_b, small, heads)
     return (
-        block_output, input_grad, small[0], jnp.transpose(g_qkv, (1, 0, 2)), g_bias, g_out, small[1], g_gate_up, g_down,
+        block_output, input_grad, g_gain1[0], jnp.transpose(g_qkv, (1, 0, 2)), g_bias, g_out, g_gain2[0], g_gate_up, g_down,
     )
 
 

time: 389 us -> 380 us (0.977)
  other arithmetic: 9.13 us -> 5.22 us
  transfers between devices with their start and end apart: 2 -> 2, of which waited for: 0 -> 0; matrix products, arithmetic and copies ran while one was open for 1% -> 0% of each run, Pallas kernels for 11% -> 11%
where the time goes in v6:
time: 380 us
  Pallas kernels  365 us (96%)
  local copies, waits for them, and re-layouts  6.68 us (2%)
  other arithmetic  5.22 us (1%)
    pallas_call x1, Pallas kernels, sum_call(): pl.pallas_call(sum_body, out_shape=[jax.ShapeDtypeStruct((2, GROUP_ROWS,...  210 us
    pallas_call x1, Pallas kernels, ffn_call(): pl.pallas_call(ffn_body, grid=(hidden // blk,), in_specs=[full, full, col...  56.1 us
    pallas_call x1, Pallas kernels, attn_bwd_call(): pl.pallas_call(attn_bwd_body, grid=(pairs,), out_shape=[jax.ShapeDtypeStr...  27.1 us
    pallas_call x1, Pallas kernels, attn_fwd_call(): pl.pallas_call(attn_fwd_body, grid=(pairs,), out_shape=[jax.ShapeDtypeStr...  23 us
    pallas_call x1, Pallas kernels, widen_call(): pl.pallas_call(widen_body, grid=(2 * half,), out_shape=[jax.ShapeDtypeStr...  17.3 us
    pallas_call x1, Pallas kernels, ffn_back_call(): pl.pallas_call(ffn_back_body, out_shape=[jax.ShapeDtypeStruct((rows, widt...  13.1 us
    pallas_call x1, Pallas kernels, attn_out_call(): pl.pallas_call(attn_out_body, out_shape=[jax.ShapeDtypeStruct((rows, dim)...  9.92 us
    pallas_call x1, Pallas kernels, qkv_call(): pl.pallas_call(qkv_body, grid=(rows // blk,), out_shape=[jax.ShapeDtypeSt...  7.95 us
  transfers between devices with their start and end apart: 2, of which 0 were waited for; matrix products, arithmetic and copies ran while one was open for 0% of the time, Pallas kernels for 11%

profile of v6, /device:TPU:0, one launch (start us, length us, event | category | flops | bytes accessed | tf_op | source)
XLA Modules:
  0.0 379.7 jit_solution(11628212706241266174)
XLA Ops:
  0.7 0.1 mul.36
  0.8 0.7 convert_element_type.6
  1.5 3.0 fusion
  4.6 8.0 %qkv.1 = (bf16[1024,1024]{1,0:T(8,128)(2,1)}, bf16[1024,512]{1,0:T(8,128)(2,1)}, bf16[1024,512]{1,0:T(8,128)(2,1)}, bf16[1024,512]{1,0:T(8,128)(2,1)}) custom-call(bf16[1024,1024]{1,0:T(8,128)(2,1)} %xin.1, f32[1,1024]{1,0:T(1,128)} %bitcast.33, bf16[3,1024,512]{2,1,0:T(8,128)(2,1)} %bitcast.27, f32[1024,128]{1,0:T(8,128)} %get-tuple-element.91.cos_ref, ...), custom_call_target="tpu_custom_call" | custom-call | tf_op jit(solution)/shard_map/qkv/pallas_call | solution.py:87
  12.5 0.0 copy-done.4
  12.5 1.4 select_convert_fusion
  14.0 23.0 %attn_fwd.1 = (bf16[1024,512]{1,0:T(8,128)(2,1)}, f32[1024,512]{1,0:T(8,128)}, bf16[4,2,1024,128]{3,2,1,0:T(8,128)(2,1)}, bf16[1024,2048]{1,0:T(8,128)(2,1)}, bf16[1024,2048]{1,0:T(8,128)(2,1)}) custom-call(bf16[1024,512]{1,0:T(8,128)(2,1)} %get-tuple-element.48.q_ref, bf16[1024,512]{1,0:T(8,128)(2,1)} %get-tuple-element.49.k_ref, ...), custom_call_target="tpu_custom_call" | custom-call | tf_op jit(solution)/shard_map/attn_fwd/pallas_call | solution.py:159
  37.0 9.9 %attn_out.1 = (f32[1024,1024]{1,0:T(8,128)}, bf16[1024,1024]{1,0:T(8,128)(2,1)}) custom-call(bf16[1024,1024]{1,0:T(8,128)(2,1)} %xin.1, bf16[1024,512]{1,0:T(8,128)(2,1)} %get-tuple-element.51.o_ref.at_ref, bf16[512,1024]{1,0:T(8,128)(2,1)} %w_ref.3, f32[1,1024]{1,0:T(1,128)} %bitcast.30), custom_call_target="tpu_custom_call" | custom-call | tf_op jit(solution)/shard_map/attn_out/pallas_call | solution.py:293
  46.9 56.1 %ffn.1 = (bf16[1024,1024]{1,0:T(8,128)(2,1)}, bf16[1024,1024]{1,0:T(8,128)(2,1)}, bf16[2,512,1024]{2,1,0:T(8,128)(2,1)}, bf16[2,512,1024]{2,1,0:T(8,128)(2,1)}, ...) custom-call(bf16[1024,1024]{1,0:T(8,128)(2,1)} %get-tuple-element.52, ...), custom_call_target="tpu_custom_call" | custom-call | tf_op jit(solution)/shard_map/ffn/pallas_call | solution.py:473
  103.0 1.6 collective-permute-start
  104.6 0.5 collective-permute-start.1
  105.1 13.1 %ffn_back.1 = (bf16[1024,512]{1,0:T(8,128)(2,1)}, bf16[512,1024]{1,0:T(8,128)(2,1)}, f32[1,1024]{1,0:T(1,128)}, bf16[1024,1024]{1,0:T(8,128)(2,1)}, f32[1024,1024]{1,0:T(8,128)}) custom-call(f32[1,1024]{1,0:T(1,128)} %bitcast.31, bf16[512,1024]{1,0:T(8,128)(2,1)} %w_ref.3, bf16[1024,512]{1,0:T(8,128)(2,1)} %get-tuple-element.51.o_ref.at_ref, ...), custom_call_target="tpu_custom_call" | custom-call | tf_op jit(solution)/shard_map/ffn_back/pallas_call | solution.py:652
  118.2 27.1 %attn_bwd.1 = (bf16[3,1024,512]{2,1,0:T(8,128)(2,1)}, f32[4,2,2,8,256]{4,3,2,1,0:T(8,128)}) custom-call(bf16[1024,512]{1,0:T(8,128)(2,1)} %get-tuple-element.48.q_ref, bf16[1024,512]{1,0:T(8,128)(2,1)} %get-tuple-element.49.k_ref, bf16[1024,512]{1,0:T(8,128)(2,1)} %get-tuple-element.50.v_ref, bf16[1024,512]{1,0:T(8,128)(2,1)} %get-tuple-element.68.do_ref, ...), custom_call_target="tpu_custom_call" | custom-call | tf_op jit(solution)/shard_map/attn_bwd/pallas_call | solution.py:233
  145.3 0.0 collective-permute-done.late_x
  145.3 0.0 copy-start.2
  145.4 0.0 collective-permute-done.1.late_y
  145.4 0.0 copy-start.3
  145.4 1.1 copy-done.2
  146.5 0.5 copy-done.3
  147.0 210.4 %grad_sum.1 = (bf16[2,2048,1024]{2,1,0:T(8,128)(2,1)}, bf16[2,2048,1024]{2,1,0:T(8,128)(2,1)}, f32[1024,1024]{1,0:T(8,128)}, f32[8,1024]{1,0:T(8,128)}) custom-call(bf16[2,512,1024]{2,1,0:T(8,128)(2,1)} %get-tuple-element.59.gk, bf16[512,1024]{1,0:T(8,128)(2,1)} %get-tuple-element.60.rg, bf16[2,512,1024]{2,1,0:T(8,128)(2,1)} %get-tuple-element.61.uk, ...), custom_call_target="tpu_custom_call" | custom-call | tf_op jit(solution)/shard_map/grad_sum/pallas_call | solution.py:1113
  357.4 17.3 %widen.1 = (f32[1024,32,128]{2,1,0:T(8,128)}, f32[8,2,2,64,1024]{4,3,2,1,0:T(8,128)}, f32[3,1024,512]{2,1,0:T(8,128)}, f32[512,1024]{1,0:T(8,128)}, f32[1,1024]{...) custom-call(bf16[2,4,512,1024]{3,2,1,0:T(8,128)(2,1)} %bitcast.24, bf16[2,4,512,1024]{3,2,1,0:T(8,128)(2,1)} %bitcast.20, ...), custom_call_target="tpu_custom_call" | custom-call | tf_op jit(solution)/shard_map/widen/pallas_call | solution.py:543
  374.7 1.3 copy.25
  376.1 1.6 copy-done
  377.7 2.0 copy.26
  (13 shorter events, 0.1 us)
Async XLA Ops:
  4.5 8.0 %copy-start.4 = (s32[1024]{0:T(1024)S(1)}, s32[1024]{0:T(1024)}, u32[]{:S(2)}) copy-start(s32[1024]{0:T(1024)} %param.14) | copy-start | bytes 12292
  4.6 8.0 %copy-start.5 = (s32[1024]{0:T(1024)S(1)}, s32[1024]{0:T(1024)}, u32[]{:S(2)}) copy-start(s32[1024]{0:T(1024)} %param.13) | copy-start | bytes 12292
  103.0 42.3 %collective-permute-start = (bf16[768,1024]{1,0:T(8,128)(2,1)}, bf16[768,1024]{1,0:T(8,128)(2,1)S(1)}, u32[]{:S(2)}, u32[]{:S(2)}) collective-permute-start(bf16[768,1024]{1,0:T(8,128)(2,1)} %get-tuple-element.63), channel_id=1, source_target_pairs={{0,2},{2,0},{4,6},{6,4},{8,10},{10,8},{12,14},{14,12},{16,18},{18,... | collective-permute-start | bytes 4718600 | tf_op jit(solution)/shard_map/ppermute | solution.py:1175
  104.6 40.8 %collective-permute-start.1 = (bf16[768,1024]{1,0:T(8,128)(2,1)}, bf16[768,1024]{1,0:T(8,128)(2,1)S(1)}, u32[]{:S(2)}, u32[]{:S(2)}) collective-permute-start(bf16[768,1024]{1,0:T(8,128)(2,1)} %get-tuple-element.64), channel_id=1, source_target_pairs={{0,4},{2,6},{4,0},{6,2},{8,12},{10,14},{12,8},{14,10},{16,20},{18,... | collective-permute-start | bytes 4718600 | tf_op jit(solution)/shard_map/ppermute | solution.py:1176
  145.3 1.1 copy-start.2
  145.4 1.6 copy-start.3
  357.4 17.3 %copy-start.1 = (bf16[1024,1024]{1,0:T(8,128)(2,1)S(1)}, bf16[1024,1024]{1,0:T(8,128)(2,1)}, u32[]{:S(2)}) copy-start(bf16[1024,1024]{1,0:T(8,128)(2,1)} %get-tuple-element.107) | copy-start | bytes 6291460
  374.7 2.9 copy-start

commit v7 on v6

--- a/solution.py
+++ b/solution.py
@@ -30,8 +30,8 @@
 WIDE = 1024
 SMALL = 8
 QBLK = 256
-FFN_ROWS = 512
-FFN_COLS = 256
+FFN_ROWS = 256
+FFN_COLS = 512
 
 
 def dot_nn(a, b):
@@ -61,13 +61,17 @@
     return jnp.where(lane < HEAD // 2, pltpu.roll(u, LANES - HEAD // 2, 1), pltpu.roll(u, HEAD // 2, 1))
 
 
-def qkv_body(x_ref, gain_ref, w_ref, cos_ref, sin_ref, xn_ref, q_ref, k_ref, v_ref):
+def qkv_body(x_ref, gain_ref, w_ref, cos_ref, sin_ref, xn_ref, q_ref, k_ref, v_ref, cos_out, sin_out):
     x = x_ref[...].astype(F32)
     inv = lax.rsqrt(jnp.mean(x * x, axis=-1, keepdims=True) + EPSILON)
     xn = (x * inv * gain_ref[...]).astype(BF)
     xn_ref[...] = xn
-    cosine = cos_ref[...]
-    sine = sin_ref[...]
+    half = cos_ref[...].T
+    cosine = jnp.concatenate([half] * 4, axis=1)
+    half = sin_ref[...].T
+    sine = jnp.concatenate([-half, half] * 2, axis=1)
+    cos_out[...] = cosine
+    sin_out[...] = sine
     for part, out, factor in ((0, q_ref, HEAD**-0.5), (1, k_ref, 1.0)):
         lin = dot_nn(xn, w_ref[part])
         for s in range(lin.shape[1] // LANES):
@@ -87,29 +91,26 @@
     return pl.pallas_call(
         qkv_body,
         grid=(rows // blk,),
-        out_shape=[jax.ShapeDtypeStruct((rows, dim), BF)] + [jax.ShapeDtypeStruct((rows, width), BF)] * 3,
+        out_shape=[jax.ShapeDtypeStruct((rows, dim), BF)]
+        + [jax.ShapeDtypeStruct((rows, width), BF)] * 3
+        + [jax.ShapeDtypeStruct((rows, LANES), F32)] * 2,
         in_specs=[
             row(dim),
             pl.BlockSpec((1, dim), lambda i: (0, 0)),
             pl.BlockSpec(w.shape, lambda i: (0, 0, 0)),
-            row(LANES),
-            row(LANES),
+            pl.BlockSpec((HEAD // 2, blk), lambda i: (0, i)),
+            pl.BlockSpec((HEAD // 2, blk), lambda i: (0, i)),
         ],
-        out_specs=[row(dim), row(width), row(width), row(width)],
+        out_specs=[row(dim), row(width), row(width), row(width), row(LANES), row(LANES)],
         compiler_params=pltpu.CompilerParams(vmem_limit_bytes=VMEM_LIMIT),
         name="qkv",
     )(x, gain, w, cosine, sine)
 
 
 def attn_fwd_body(
-    q_ref, k_ref, v_ref, base_ref, segq_ref, extk_ref, bias_ref, w_ref, o_ref, o32_ref, extq_ref, wg_ref, wu_ref
+    q_ref, k_ref, v_ref, base_ref, segq_ref, extk_ref, bias_ref, o_ref, o32_ref, extq_ref
 ):
     rows = q_ref.shape[0]
-    for t in range(w_ref.shape[1] // 8):
-        turned = jnp.swapaxes(w_ref[:, t * 8 : (t + 1) * 8, :].astype(F32), 0, 1)
-        for k in range(8):
-            s = t * 4 + k // 2
-            (wg_ref, wu_ref)[k % 2][:, s * LANES : (s + 1) * LANES] = turned[k].astype(BF)
     blk = 256
     lane = lax.broadcasted_iota(jnp.int32, (blk, LANES), 1)
     kind = lax.broadcasted_iota(jnp.int32, (1, LANES), 1) // VAR_COLS
@@ -148,12 +149,9 @@
         o_ref[sl, :] = o.astype(BF)
 
 
-def attn_fwd_call(q, k, v, base, segq, extk, head_bias, w_pairs):
+def attn_fwd_call(q, k, v, base, segq, extk, head_bias):
     rows, width = q.shape
     pairs = width // LANES
-    dim, tiles, _ = w_pairs.shape
-    share = dim // pairs
-    half_w = pl.BlockSpec((share, tiles * LANES // 2), lambda p: (p, 0))
     col = pl.BlockSpec((rows, LANES), lambda p: (0, p))
     full = pl.BlockSpec((rows, LANES), lambda p: (0, 0))
     return pl.pallas_call(
@@ -163,18 +161,15 @@
             jax.ShapeDtypeStruct((rows, width), BF),
             jax.ShapeDtypeStruct((rows, width), F32),
             jax.ShapeDtypeStruct((pairs, 2, rows, LANES), BF),
-            jax.ShapeDtypeStruct((dim, tiles * LANES // 2), BF),
-            jax.ShapeDtypeStruct((dim, tiles * LANES // 2), BF),
         ],
         in_specs=[
             col, col, col, full, full, full,
             pl.BlockSpec(memory_space=pltpu.SMEM),
-            pl.BlockSpec((share, tiles, LANES), lambda p: (p, 0, 0)),
         ],
-        out_specs=[col, col, pl.BlockSpec((1, 2, rows, LANES), lambda p: (p, 0, 0, 0)), half_w, half_w],
+        out_specs=[col, col, pl.BlockSpec((1, 2, rows, LANES), lambda p: (p, 0, 0, 0))],
         compiler_params=pltpu.CompilerParams(vmem_limit_bytes=VMEM_LIMIT),
         name="attn_fwd",
-    )(q, k, v, base, segq, extk, head_bias, w_pairs)
+    )(q, k, v, base, segq, extk, head_bias)
 
 
 def attn_bwd_body(
@@ -266,48 +261,73 @@
 CHUNKS = 4
 
 
-def attn_out_body(x_ref, o_ref, w_ref, gain_ref, mid_ref, xn_ref, mine, theirs, ssem, rsem):
+def attn_out_body(o_ref, w_ref, gain_ref, x, mid, xn, x_v, mid_v, xn_v, mine, theirs, ssem, rsem, lsem, osem):
+    rows = x.shape[0]
+    blk = rows // CHUNKS
+
+    def rows_of(c):
+        return pl.ds(pl.multiple_of(c * blk, blk), blk)
+
+    def load(c):
+        return pltpu.make_async_copy(x.at[rows_of(c)], x_v.at[rows_of(c)], lsem.at[c])
+
+    def stores(c):
+        return [
+            pltpu.make_async_copy(mid_v.at[rows_of(c)], mid.at[rows_of(c)], osem.at[0, c]),
+            pltpu.make_async_copy(xn_v.at[rows_of(c)], xn.at[rows_of(c)], osem.at[1, c]),
+        ]
+
+    for c in range(CHUNKS):
+        load(c).start()
     peer = partner_barrier()
-    rows = x_ref.shape[0]
-    blk = rows // CHUNKS
-    copies = []
+
+    def core_copy(c):
+        return send_rows(mine, theirs, rows_of(c), ssem.at[c], rsem.at[c], peer)
+
+    @pl.loop(0, CHUNKS)
+    def _(c):
+        mine[rows_of(c), :] = dot_nn(o_ref[rows_of(c), :], w_ref[...]).astype(BF)
+        core_copy(c).start()
+
+    @pl.loop(0, CHUNKS)
+    def _(c):
+        r = rows_of(c)
+        load(c).wait()
+        core_copy(c).wait_recv()
+        total = x_v[r, :].astype(F32) + (mine[r, :].astype(F32) + theirs[r, :].astype(F32))
+        inv = lax.rsqrt(jnp.mean(total * total, axis=-1, keepdims=True) + EPSILON)
+        mid_v[r, :] = total
+        xn_v[r, :] = (total * inv * gain_ref[...]).astype(BF)
+        for copy in stores(c):
+            copy.start()
+
     for c in range(CHUNKS):
-        sl = slice(c * blk, (c + 1) * blk)
-        mine[sl, :] = dot_nn(o_ref[sl, :], w_ref[...]).astype(BF)
-        copy = send_rows(mine, theirs, pl.ds(c * blk, blk), ssem.at[c], rsem.at[c], peer)
-        copy.start()
-        copies.append(copy)
-    for c in range(CHUNKS):
-        sl = slice(c * blk, (c + 1) * blk)
-        copies[c].wait_recv()
-        mid = x_ref[sl, :].astype(F32) + (mine[sl, :].astype(F32) + theirs[sl, :].astype(F32))
-        inv = lax.rsqrt(jnp.mean(mid * mid, axis=-1, keepdims=True) + EPSILON)
-        mid_ref[sl, :] = mid
-        xn_ref[sl, :] = (mid * inv * gain_ref[...]).astype(BF)
-    for c in range(CHUNKS):
-        copies[c].wait_send()
+        core_copy(c).wait_send()
+        for copy in stores(c):
+            copy.wait()
 
 
 def attn_out_call(x, o, w, gain):
     rows, dim = x.shape
+    any_spec = pl.BlockSpec(memory_space=pl.ANY)
+    low = pltpu.VMEM((rows, dim), BF)
+    dma = pltpu.SemaphoreType.DMA
     return pl.pallas_call(
         attn_out_body,
         out_shape=[jax.ShapeDtypeStruct((rows, dim), F32), jax.ShapeDtypeStruct((rows, dim), BF)],
-        in_specs=[whole_spec()] * 4,
-        out_specs=[whole_spec()] * 2,
+        in_specs=[whole_spec()] * 3 + [any_spec],
+        out_specs=[any_spec] * 2,
         scratch_shapes=[
-            pltpu.VMEM((rows, dim), BF),
-            pltpu.VMEM((rows, dim), BF),
-            pltpu.SemaphoreType.DMA((CHUNKS,)),
-            pltpu.SemaphoreType.DMA((CHUNKS,)),
+            low, pltpu.VMEM((rows, dim), F32), low, low, low,
+            dma((CHUNKS,)), dma((CHUNKS,)), dma((CHUNKS,)), dma((2, CHUNKS)),
         ],
         compiler_params=pltpu.CompilerParams(collective_id=1, has_side_effects=True, vmem_limit_bytes=VMEM_LIMIT),
         name="attn_out",
-    )(x, o, w, gain)
-
-
-LATE = 4
-SLOTS = 4
+    )(o, w, gain, x)
+
+
+LATE = 2
+SLOTS = 2
 PART = FFN_COLS // 4
 
 
@@ -321,9 +341,9 @@
 
 
 def ffn_body(
-    xn_ref, ct_ref, wg_ref, wu_ref, wd_ref,
+    xn_ref, ct_ref, w0_ref, wn_ref, wd_ref,
     out_ref, gx_ref, gk_ref, uk_ref, rg, ru, dk, rd, late_x, late_y,
-    acc_o, acc_g, hid, dg, du, xt, away_w, away_d, ws, wr, ds, dr,
+    acc_o, acc_g, hid, dg, du, xt, wgu, away_w, away_d, ws, wr, ds, dr,
 ):
     j = pl.program_id(0)
     t = lax.axis_index("tensor")
@@ -397,6 +417,12 @@
             def _():
                 act(down_late(g, at))
 
+    def part_rows(src, to, r):
+        turned = jnp.swapaxes(src[r].astype(F32), 0, 1)
+        for k in range(8):
+            s = k // 2
+            wgu[to, k % 2, r, s * LANES : (s + 1) * LANES] = turned[k].astype(BF)
+
     @pl.when(j == 0)
     def _():
         barrier = pltpu.get_barrier_semaphore()
@@ -407,9 +433,15 @@
         acc_g[...] = jnp.zeros_like(acc_g)
         xt[...] = xn_ref[...].T
 
-    wg = wg_ref[...]
-    wu = wu_ref[...]
+        @pl.loop(0, rows // LANES)
+        def _(c):
+            part_rows(w0_ref, 0, pl.ds(pl.multiple_of(c * LANES, LANES), LANES))
+
+    now = lax.rem(j, 2)
+    wg = wgu[now, 0]
+    wu = wgu[now, 1]
     wd = wd_ref[...]
+    part_rows(wn_ref, 1 - now, slice(None))
     for i in range(rows // FFN_ROWS):
         sl = slice(i * FFN_ROWS, (i + 1) * FFN_ROWS)
         xn = xn_ref[sl, :]
@@ -455,13 +487,16 @@
             remote(part, part, ds.at[g, 0], dr.at[g], near[g]).wait_recv()
 
 
-def ffn_call(xn, ct, wg, wu, wd):
+def ffn_call(xn, ct, w_pairs, wd):
     rows, dim = xn.shape
     hidden = wd.shape[0]
     blk = FFN_COLS
     per = WIDE // blk
     full = pl.BlockSpec((rows, dim), lambda j: (0, 0))
-    colw = pl.BlockSpec((dim, blk), lambda j: (0, j))
+    steps = hidden // blk
+    tiles = 2 * blk // LANES
+    first_w = pl.BlockSpec((dim, tiles, LANES), lambda j: (0, 0, 0))
+    next_w = pl.BlockSpec((dim, tiles, LANES), lambda j: (0, jnp.minimum(j + 1, steps - 1), 0))
     roww = pl.BlockSpec((blk, dim), lambda j: (j, 0))
     grad = pl.BlockSpec((1, HALF_ROWS, blk), lambda j: (j // per, 0, lax.rem(j, per)))
     any_spec = pl.BlockSpec(memory_space=pl.ANY)
@@ -473,7 +508,7 @@
     return pl.pallas_call(
         ffn_body,
         grid=(hidden // blk,),
-        in_specs=[full, full, colw, colw, roww],
+        in_specs=[full, full, first_w, next_w, roww],
         out_specs=[full, full, grad, grad] + [any_spec] * 6,
         out_shape=[jax.ShapeDtypeStruct((rows, dim), BF)] * 2
         + [wide, wide, come, come, wide, jax.ShapeDtypeStruct((2, early * PART, dim), BF), late, late],
@@ -481,13 +516,14 @@
         + [pltpu.VMEM((rows, blk), BF)] * 3
         + [
             pltpu.VMEM((dim, rows), BF),
+            pltpu.VMEM((2, 2, dim, blk), BF),
             pltpu.VMEM((2, SLOTS, HALF_ROWS, blk), BF),
             pltpu.VMEM((SLOTS, blk, dim), BF),
             dma((2, SLOTS)), dma((2,)), dma((4, SLOTS)), dma((2,)),
         ],
         compiler_params=pltpu.CompilerParams(collective_id=5, has_side_effects=True, vmem_limit_bytes=VMEM_LIMIT),
         name="ffn",
-    )(xn, ct, wg, wu, wd)
+    )(xn, ct, w_pairs, w_pairs, wd)
 
 
 def pair_rows(w):
@@ -591,55 +627,59 @@
     blk = rows // CHUNKS
 
     def rows_of(c):
-        return pl.ds(c * blk, blk)
-
-    loads = [
-        [
-            pltpu.make_async_copy(src.at[rows_of(c)], dst.at[rows_of(c)], lsem.at[k, c])
-            for k, (src, dst) in enumerate(((gx, gx_v), (mid, mid_v), (ct, ct_v), (fo, fo_v)))
-        ]
-        for c in range(CHUNKS)
-    ]
+        return pl.ds(pl.multiple_of(c * blk, blk), blk)
+
+    def load(k, c):
+        src, dst = ((gx, gx_v), (mid, mid_v), (ct, ct_v), (fo, fo_v))[k]
+        return pltpu.make_async_copy(src.at[rows_of(c)], dst.at[rows_of(c)], lsem.at[k, c])
+
+    def store(k, c):
+        src, dst = ((gm_v, gm), (out_v, out))[k]
+        return pltpu.make_async_copy(src.at[rows_of(c)], dst.at[rows_of(c)], osem.at[k, c])
+
     for c in range(CHUNKS):
-        for copy in loads[c]:
-            copy.start()
+        for k in range(4):
+            load(k, c).start()
     peer = partner_barrier()
-    copies = []
-    for n, (src, dst) in enumerate(((gx, gx_in), (fo, fo_in))):
+
+    def core_copy(n, c):
+        src, dst = ((gx, gx_in), (fo, fo_in))[n]
+        return send_rows(src, dst, rows_of(c), ssem.at[n * CHUNKS + c], rsem.at[n * CHUNKS + c], peer)
+
+    for n in range(2):
         for c in range(CHUNKS):
-            at = n * CHUNKS + c
-            copy = send_rows(src, dst, rows_of(c), ssem.at[at], rsem.at[at], peer)
-            copy.start()
-            copies.append(copy)
-    stores = []
-    gain_sum = jnp.zeros((1, mid.shape[1]), F32)
+            core_copy(n, c).start()
+    gg_ref[...] = jnp.zeros_like(gg_ref)
+
+    @pl.loop(0, CHUNKS)
+    def _(c):
+        r = rows_of(c)
+        for k in range(3):
+            load(k, c).wait()
+        core_copy(0, c).wait_recv()
+        grads = gx_v[r, :].astype(F32) + gx_in[r, :].astype(F32)
+        back, gain_grad = norm_back(mid_v[r, :], gain_ref[...], grads)
+        gg_ref[...] += gain_grad
+        grad_mid = ct_v[r, :].astype(F32) + back
+        gm_v[r, :] = grad_mid
+        store(0, c).start()
+        low = grad_mid.astype(BF)
+        gb[r, :] = low
+        do_ref[r, :] = dot_nt(low, w_ref[...]).astype(BF)
+
+    @pl.loop(0, CHUNKS)
+    def _(c):
+        r = rows_of(c)
+        load(3, c).wait()
+        core_copy(1, c).wait_recv()
+        out_v[r, :] = (mid_v[r, :] + (fo_v[r, :].astype(F32) + fo_in[r, :].astype(F32))).astype(BF)
+        store(1, c).start()
+
+    gw_ref[...] = dot_tn(at_ref[...], gb[...]).astype(BF)
     for c in range(CHUNKS):
-        sl = slice(c * blk, (c + 1) * blk)
-        for copy in loads[c][:3]:
-            copy.wait()
-        copies[c].wait_recv()
-        grads = gx_v[sl, :].astype(F32) + gx_in[sl, :].astype(F32)
-        back, gain_grad = norm_back(mid_v[sl, :], gain_ref[...], grads)
-        gain_sum = gain_sum + gain_grad
-        grad_mid = ct_v[sl, :].astype(F32) + back
-        gm_v[sl, :] = grad_mid
-        stores.append(pltpu.make_async_copy(gm_v.at[rows_of(c)], gm.at[rows_of(c)], osem.at[0, c]))
-        stores[-1].start()
-        gb[sl, :] = grad_mid.astype(BF)
-        do_ref[sl, :] = dot_nt(gb[sl, :], w_ref[...]).astype(BF)
-    gg_ref[...] = gain_sum
-    for c in range(CHUNKS):
-        sl = slice(c * blk, (c + 1) * blk)
-        loads[c][3].wait()
-        copies[CHUNKS + c].wait_recv()
-        out_v[sl, :] = (mid_v[sl, :] + (fo_v[sl, :].astype(F32) + fo_in[sl, :].astype(F32))).astype(BF)
-        stores.append(pltpu.make_async_copy(out_v.at[rows_of(c)], out.at[rows_of(c)], osem.at[1, c]))
-        stores[-1].start()
-    gw_ref[...] = dot_tn(at_ref[...], gb[...]).astype(BF)
-    for copy in copies:
-        copy.wait_send()
-    for copy in stores:
-        copy.wait()
+        for k in range(2):
+            core_copy(k, c).wait_send()
+            store(k, c).wait()
 
 
 def ffn_back_call(gx, fo, mid, ct, gain, w, at):
@@ -937,7 +977,7 @@
         return pl.ds(pl.multiple_of(half * HALF_ROWS, HALF_ROWS), HALF_ROWS)
 
     def piece_qk(k):
-        cols = pl.ds(k * width, width)
+        cols = pl.ds(pl.multiple_of(k * width, width), width)
         L[0, tail, cols] = dot_tn(xb[:, row_half(x)], dl[k]).astype(BF)
         away_rows[0, :, cols] = dot_tn(xb[:, row_half(1 - x)], dl[k]).astype(BF)
 
@@ -1006,8 +1046,7 @@
         (3, QUARTER_ROWS // SWAP_ROWS, piece_second),
         (3, 1, lambda c: piece_start()),
         (4, CHUNKS, piece_part),
-        (4 + CHUNKS, 1, lambda c: piece_qk(0)),
-        (5 + CHUNKS, 1, lambda c: piece_qk(1)),
+        (4 + CHUNKS, 2, piece_qk),
         (6 + CHUNKS, 1, lambda c: piece_v()),
         (7 + CHUNKS, 1, lambda c: piece_send()),
         (8 + CHUNKS, HALF_ROWS // SWAP_ROWS, piece_swap),
@@ -1143,9 +1182,8 @@
 def tables(time_ids):
     half = HEAD // 2
     freqs = jnp.exp(jnp.arange(half, dtype=F32) * (-2.0 * math.log(10000.0) / HEAD))
-    angles = time_ids.astype(F32)[:, None] * jnp.tile(freqs, LANES // half)[None, :]
-    sign = jnp.where(jnp.arange(LANES) % HEAD < half, -1.0, 1.0)
-    return jnp.cos(angles), jnp.sin(angles) * sign[None, :]
+    angles = freqs[:, None] * time_ids.astype(F32)[None, :]
+    return jnp.cos(angles), jnp.sin(angles)
 
 
 def mask_tables(segments, variates):
@@ -1168,10 +1206,10 @@
     base, segq, extk = mask_tables(segments, variates)
     gain1 = attn_gain[None, :]
     gain2 = ffn_gain[None, :]
-    xn, q, k, v = qkv_call(block_input, gain1, w3, cosine, sine)
-    attended, o32, extq, wg, wu = attn_fwd_call(q, k, v, base, segq, extk, head_bias, pair_rows(w_gate_up))
+    xn, q, k, v, cosine, sine = qkv_call(block_input, gain1, w3, cosine, sine)
+    attended, o32, extq = attn_fwd_call(q, k, v, base, segq, extk, head_bias)
     mid, xn2 = attn_out_call(block_input, attended, w_out, gain2)
-    ffn_part, gx_part, gk, uk, rg, ru, dk, rd, late_x, late_y = ffn_call(xn2, cotangent, wg, wu, w_down)
+    ffn_part, gx_part, gk, uk, rg, ru, dk, rd, late_x, late_y = ffn_call(xn2, cotangent, pair_rows(w_gate_up), w_down)
     late_x = lax.ppermute(late_x, "dp", [(d, d ^ 1) for d in range(16)])
     late_y = lax.ppermute(late_y, "dp", [(d, d ^ 2) for d in range(16)])
     block_output, grad_mid, do, g_out, g_gain2 = ffn_back_call(

time: 380 us -> 372 us (0.979)
  Pallas kernels: 365 us -> 359 us
    pallas_call x1, Pallas kernels: 23 us -> 15.3 us  [attn_fwd_call(): pl.pallas_call(attn_fwd_body, grid=(pairs,), out_shape=[jax.ShapeDtypeStr...]
    pallas_call x1, Pallas kernels: 56.1 us -> 61 us  [ffn_call(): pl.pallas_call(ffn_body, grid=(hidden // blk,), in_specs=[full, full, fir...]
where the time goes in v7:
time: 372 us
  Pallas kernels  359 us (97%)
  local copies, waits for them, and re-layouts  6.6 us (2%)
    pallas_call x1, Pallas kernels, sum_call(): pl.pallas_call(sum_body, out_shape=[jax.ShapeDtypeStruct((2, GROUP_ROWS,...  210 us
    pallas_call x1, Pallas kernels, ffn_call(): pl.pallas_call(ffn_body, grid=(hidden // blk,), in_specs=[full, full, fir...  61 us
    pallas_call x1, Pallas kernels, attn_bwd_call(): pl.pallas_call(attn_bwd_body, grid=(pairs,), out_shape=[jax.ShapeDtypeStr...  26.9 us
    pallas_call x1, Pallas kernels, widen_call(): pl.pallas_call(widen_body, grid=(2 * half,), out_shape=[jax.ShapeDtypeStr...  17.3 us
    pallas_call x1, Pallas kernels, attn_fwd_call(): pl.pallas_call(attn_fwd_body, grid=(pairs,), out_shape=[jax.ShapeDtypeStr...  15.3 us
    pallas_call x1, Pallas kernels, ffn_back_call(): pl.pallas_call(ffn_back_body, out_shape=[jax.ShapeDtypeStruct((rows, widt...  12.3 us
    pallas_call x1, Pallas kernels, qkv_call(): pl.pallas_call(qkv_body, grid=(rows // blk,), out_shape=[jax.ShapeDtypeSt...  7.95 us
    pallas_call x1, Pallas kernels, attn_out_call(): pl.pallas_call(attn_out_body, out_shape=[jax.ShapeDtypeStruct((rows, dim)...  7.72 us
  transfers between devices with their start and end apart: 2, of which 0 were waited for; matrix products, arithmetic and copies ran while one was open for 0% of the time, Pallas kernels for 11%

profile of v7, /device:TPU:0, one launch (start us, length us, event | category | flops | bytes accessed | tf_op | source)
XLA Modules:
  0.0 371.8 jit_solution(14096331333695852595)
XLA Ops:
  0.7 0.7 convert_element_type.6
  1.4 1.2 multiply_sine_fusion
  2.6 7.9 %qkv.1 = (bf16[1024,1024]{1,0:T(8,128)(2,1)}, bf16[1024,512]{1,0:T(8,128)(2,1)}, bf16[1024,512]{1,0:T(8,128)(2,1)}, bf16[1024,512]{1,0:T(8,128)(2,1)}, f32[1024,128]{1,0:T(8,128)}, /*index=5*/f32[1024,128]{1,0:T(8,128)}) custom-call(bf16[1024,1024]{1,0:T(8,128)(2,1)} %xin.1, f32[1,1024]{1,0:T(1,128)} %bitcast.34, bf16[3,1024,512]{2,1,0:T(8,128)(2,1)} %bitcast.29, ...), custom_call_target="tpu_custom_call" | custom-call | tf_op jit(solution)/shard_map/qkv/pallas_call | solution.py:91
  10.6 0.0 copy-done.4
  10.6 0.0 copy-done.5
  10.6 1.5 select_convert_fusion
  12.1 15.3 %attn_fwd.1 = (bf16[1024,512]{1,0:T(8,128)(2,1)}, f32[1024,512]{1,0:T(8,128)}, bf16[4,2,1024,128]{3,2,1,0:T(8,128)(2,1)}) custom-call(bf16[1024,512]{1,0:T(8,128)(2,1)} %get-tuple-element.48.q_ref, bf16[1024,512]{1,0:T(8,128)(2,1)} %get-tuple-element.49.k_ref, bf16[1024,512]{1,0:T(8,128)(2,1)} %get-tuple-element.50.v_ref, ...), custom_call_target="tpu_custom_call" | custom-call | tf_op jit(solution)/shard_map/attn_fwd/pallas_call | solution.py:157
  27.5 7.7 %attn_out.1 = (f32[1024,1024]{1,0:T(8,128)}, bf16[1024,1024]{1,0:T(8,128)(2,1)}) custom-call(bf16[1024,512]{1,0:T(8,128)(2,1)} %get-tuple-element.51.o_ref.at_ref, bf16[512,1024]{1,0:T(8,128)(2,1)} %w_ref.3, f32[1,1024]{1,0:T(1,128)} %bitcast.31, bf16[1024,1024]{1,0:T(8,128)(2,1)} %xin.1), custom_call_target="tpu_custom_call" | custom-call | tf_op jit(solution)/shard_map/attn_out/pallas_call | solution.py:315
  35.2 61.0 %ffn.1 = (bf16[1024,1024]{1,0:T(8,128)(2,1)}, bf16[1024,1024]{1,0:T(8,128)(2,1)}, bf16[2,512,1024]{2,1,0:T(8,128)(2,1)}, bf16[2,512,1024]{2,1,0:T(8,128)(2,1)}, ...) custom-call(bf16[1024,1024]{1,0:T(8,128)(2,1)} %get-tuple-element.52, ...), custom_call_target="tpu_custom_call" | custom-call | tf_op jit(solution)/shard_map/ffn/pallas_call | solution.py:508
  96.2 1.6 collective-permute-start
  97.8 0.5 collective-permute-start.1
  98.3 12.3 %ffn_back.1 = (bf16[1024,512]{1,0:T(8,128)(2,1)}, bf16[512,1024]{1,0:T(8,128)(2,1)}, f32[1,1024]{1,0:T(1,128)}, bf16[1024,1024]{1,0:T(8,128)(2,1)}, f32[1024,1024]{1,0:T(8,128)}) custom-call(f32[1,1024]{1,0:T(1,128)} %bitcast.32, bf16[512,1024]{1,0:T(8,128)(2,1)} %w_ref.3, bf16[1024,512]{1,0:T(8,128)(2,1)} %get-tuple-element.51.o_ref.at_ref, ...), custom_call_target="tpu_custom_call" | custom-call | tf_op jit(solution)/shard_map/ffn_back/pallas_call | solution.py:692
  110.6 26.9 %attn_bwd.1 = (bf16[3,1024,512]{2,1,0:T(8,128)(2,1)}, f32[4,2,2,8,256]{4,3,2,1,0:T(8,128)}) custom-call(bf16[1024,512]{1,0:T(8,128)(2,1)} %get-tuple-element.48.q_ref, bf16[1024,512]{1,0:T(8,128)(2,1)} %get-tuple-element.49.k_ref, bf16[1024,512]{1,0:T(8,128)(2,1)} %get-tuple-element.50.v_ref, bf16[1024,512]{1,0:T(8,128)(2,1)} %get-tuple-element.66.do_ref, ...), custom_call_target="tpu_custom_call" | custom-call | tf_op jit(solution)/shard_map/attn_bwd/pallas_call | solution.py:228
  137.5 0.0 collective-permute-done.late_x
  137.5 0.0 copy-start.2
  137.5 0.0 collective-permute-done.1.late_y
  137.5 0.0 copy-start.3
  137.5 1.1 copy-done.2
  138.6 0.5 copy-done.3
  139.1 210.4 %grad_sum.1 = (bf16[2,2048,1024]{2,1,0:T(8,128)(2,1)}, bf16[2,2048,1024]{2,1,0:T(8,128)(2,1)}, f32[1024,1024]{1,0:T(8,128)}, f32[8,1024]{1,0:T(8,128)}) custom-call(bf16[2,512,1024]{2,1,0:T(8,128)(2,1)} %get-tuple-element.57.gk, bf16[512,1024]{1,0:T(8,128)(2,1)} %get-tuple-element.58.rg, bf16[2,512,1024]{2,1,0:T(8,128)(2,1)} %get-tuple-element.59.uk, ...), custom_call_target="tpu_custom_call" | custom-call | tf_op jit(solution)/shard_map/grad_sum/pallas_call | solution.py:1152
  349.5 17.3 %widen.1 = (f32[1024,32,128]{2,1,0:T(8,128)}, f32[4,2,2,128,1024]{4,3,2,1,0:T(8,128)}, f32[3,1024,512]{2,1,0:T(8,128)}, f32[512,1024]{1,0:T(8,128)}, f32[1,1024]...) custom-call(bf16[2,4,512,1024]{3,2,1,0:T(8,128)(2,1)} %bitcast.24, bf16[2,4,512,1024]{3,2,1,0:T(8,128)(2,1)} %bitcast.20, ...), custom_call_target="tpu_custom_call" | custom-call | tf_op jit(solution)/shard_map/widen/pallas_call | solution.py:579
  366.9 1.3 copy.25
  368.2 1.6 copy-done
  369.8 2.0 copy.26
  (10 shorter events, 0.0 us)
Async XLA Ops:
  2.6 8.0 %copy-start.4 = (s32[1024]{0:T(1024)S(1)}, s32[1024]{0:T(1024)}, u32[]{:S(2)}) copy-start(s32[1024]{0:T(1024)} %param.14) | copy-start | bytes 12292
  2.6 8.0 %copy-start.5 = (s32[1024]{0:T(1024)S(1)}, s32[1024]{0:T(1024)}, u32[]{:S(2)}) copy-start(s32[1024]{0:T(1024)} %param.13) | copy-start | bytes 12292
  96.2 41.2 %collective-permute-start = (bf16[768,1024]{1,0:T(8,128)(2,1)}, bf16[768,1024]{1,0:T(8,128)(2,1)S(1)}, u32[]{:S(2)}, u32[]{:S(2)}) collective-permute-start(bf16[768,1024]{1,0:T(8,128)(2,1)} %get-tuple-element.61), channel_id=1, source_target_pairs={{0,2},{2,0},{4,6},{6,4},{8,10},{10,8},{12,14},{14,12},{16,18},{18,... | collective-permute-start | bytes 4718600 | tf_op jit(solution)/shard_map/ppermute | solution.py:1213
  97.8 39.7 %collective-permute-start.1 = (bf16[768,1024]{1,0:T(8,128)(2,1)}, bf16[768,1024]{1,0:T(8,128)(2,1)S(1)}, u32[]{:S(2)}, u32[]{:S(2)}) collective-permute-start(bf16[768,1024]{1,0:T(8,128)(2,1)} %get-tuple-element.62), channel_id=1, source_target_pairs={{0,4},{2,6},{4,0},{6,2},{8,12},{10,14},{12,8},{14,10},{16,20},{18,... | collective-permute-start | bytes 4718600 | tf_op jit(solution)/shard_map/ppermute | solution.py:1214
  137.5 1.1 copy-start.2
  137.5 1.6 copy-start.3
  349.5 17.3 %copy-start.1 = (bf16[1024,1024]{1,0:T(8,128)(2,1)S(1)}, bf16[1024,1024]{1,0:T(8,128)(2,1)}, u32[]{:S(2)}) copy-start(bf16[1024,1024]{1,0:T(8,128)(2,1)} %get-tuple-element.107) | copy-start | bytes 6291460
  366.9 2.9 copy-start

commit v8 on v7

--- a/solution.py
+++ b/solution.py
@@ -30,7 +30,7 @@
 WIDE = 1024
 SMALL = 8
 QBLK = 256
-FFN_ROWS = 256
+FFN_ROWS = 512
 FFN_COLS = 512
 
 
@@ -533,8 +533,8 @@
 
 
 def widen_body(
-    ga_ref, gb_ref, da_ref, db_ref, aa_ref, v_ref, o_ref, small_ref,
-    gu_ref, down_ref, qkv_ref, out_ref, g1_ref, g2_ref, gbias_ref,
+    ga_ref, gb_ref, da_ref, db_ref, aa_ref, v_ref, o_ref, small_ref, rows_ref, ig_ref,
+    gu_ref, down_ref, qkv_ref, out_ref, g1_ref, g2_ref, gbias_ref, rows_out, ig_out,
 ):
     tiles = WIDE // LANES
     for f in range(2):
@@ -552,6 +552,8 @@
     qkv_ref[1] = aa_ref[0, 0, :, width:].astype(F32)
     qkv_ref[2] = v_ref[0, 0].astype(F32)
     out_ref[...] = o_ref[0, 0].astype(F32)
+    rows_out[...] = rows_ref[...]
+    ig_out[...] = ig_ref[...]
 
     @pl.when(pl.program_id(0) == 0)
     def _():
@@ -568,7 +570,7 @@
         gbias_ref[...] = total
 
 
-def widen_call(a, b, small, heads):
+def widen_call(a, b, small, heads, block_output, input_grad):
     blk = 256
     half = HALF_ROWS // blk
     tiles = 4 * WIDE // LANES
@@ -576,7 +578,10 @@
     gate = pl.BlockSpec((1, 2, blk, WIDE), lambda i: (i // half, 0, lax.rem(i, half), 0))
     block = lambda n: pl.BlockSpec((1, 1, blk, WIDE), lambda i: (i // half, n, lax.rem(i, half), 0))
     fixed = lambda shape: pl.BlockSpec(shape, lambda i: (0, 0))
-    gu, down, qkv, out, g1, g2, gbias = pl.pallas_call(
+    rows = block_output.shape[0]
+    steps = 2 * half
+    share = pl.BlockSpec((rows // steps, WIDE), lambda i: (i, 0))
+    gu, down, qkv, out, g1, g2, gbias, block_output, input_grad = pl.pallas_call(
         widen_body,
         grid=(2 * half,),
         out_shape=[
@@ -587,12 +592,16 @@
             jax.ShapeDtypeStruct((1, WIDE), F32),
             jax.ShapeDtypeStruct((1, WIDE), F32),
             jax.ShapeDtypeStruct((2, heads), F32),
+            jax.ShapeDtypeStruct(block_output.shape, BF),
+            jax.ShapeDtypeStruct(input_grad.shape, F32),
         ],
         in_specs=[
             gate, gate, block(2), block(2), block(3),
             pl.BlockSpec((1, 1, blk, width), lambda i: (0, 3, lax.rem(i, half), i // half)),
             pl.BlockSpec((1, 1, blk // 2, WIDE), lambda i: (1, 3, i, 0)),
             fixed((SMALL, WIDE)),
+            share,
+            share,
         ],
         out_specs=[
             pl.BlockSpec((blk, tiles, LANES), lambda i: (i, 0, 0)),
@@ -602,12 +611,14 @@
             fixed((1, WIDE)),
             fixed((1, WIDE)),
             fixed((2, heads)),
+            share,
+            share,
         ],
         compiler_params=pltpu.CompilerParams(vmem_limit_bytes=VMEM_LIMIT),
         name="widen",
-    )(a, b, a, b, a, b, b, small)
+    )(a, b, a, b, a, b, b, small, block_output, input_grad)
     gu = jnp.transpose(gu.reshape(2 * HALF_ROWS, tiles // 2, 2, LANES), (0, 2, 1, 3)).reshape(2 * HALF_ROWS, 2, 2 * WIDE)
-    return gu, down.reshape(4 * HALF_ROWS, WIDE), qkv, out, g1, g2, gbias
+    return gu, down.reshape(4 * HALF_ROWS, WIDE), qkv, out, g1, g2, gbias, block_output, input_grad
 
 
 def norm_back(rows_now, gain, grads):
@@ -769,12 +780,9 @@
         return [pltpu.make_async_copy(src, dst, loc.at[g, b, k]) for k, (src, dst) in enumerate(copies)]
 
     own_loads = [pltpu.make_async_copy(src, dst, ld.at[k]) for k, (src, dst) in enumerate(((dqkv, dl), (w3, wb), (xn, xb)))]
-    for b in range(3):
-        for g in range(2):
-            for copy in loads(g, b):
-                copy.start()
-    for copy in own_loads:
-        copy.start()
+    for g in range(2):
+        for copy in loads(g, 0):
+            copy.start()
 
     tail = pl.ds(2 * HALF_ROWS + QUARTER_ROWS, HALF_ROWS)
 
@@ -789,8 +797,6 @@
         @pl.when(y == 0)
         def _():
             act(out_load(False))
-
-    out_load_do(lambda copy: copy.start())
 
     barrier = pltpu.get_barrier_semaphore()
     others_z = [lax.rem(z + k, 4) * 4 + y * 2 + x for k in range(1, 4)]
@@ -798,6 +804,13 @@
         pl.semaphore_signal(barrier, inc=1, device_id=(peer, t), device_id_type=MESH)
     pl.semaphore_signal(barrier, inc=1, device_id=(dp, 1 - t), device_id_type=MESH)
     pl.semaphore_wait(barrier, 6)
+    for b in (2, 1):
+        for g in range(2):
+            for copy in loads(g, b):
+                copy.start()
+    for copy in own_loads:
+        copy.start()
+    out_load_do(lambda copy: copy.start())
 
     def first_exchange(g):
         return remote(away_rows.at[g], S.at[g, tail], s1s.at[g], s1r.at[g], first[g])
@@ -1222,7 +1235,9 @@
     sum_a = sum_a.reshape(2, 4, HALF_ROWS, WIDE)
     sum_b = sum_b.reshape(2, 4, HALF_ROWS, WIDE)
     heads = head_bias.shape[1]
-    g_gate_up, g_down, g_qkv, g_out, g_gain1, g_gain2, g_bias = widen_call(sum_a, sum_b, small, heads)
+    g_gate_up, g_down, g_qkv, g_out, g_gain1, g_gain2, g_bias, block_output, input_grad = widen_call(
+        sum_a, sum_b, small, heads, block_output, input_grad
+    )
     return (
         block_output, input_grad, g_gain1[0], jnp.transpose(g_qkv, (1, 0, 2)), g_bias, g_out, g_gain2[0], g_gate_up, g_down,
     )

time: 372 us -> 370 us (level)
  local copies, waits for them, and re-layouts: 6.6 us -> 1.64 us
    unnamed x14 -> x8, local copies, waits for them, and re-layouts: 6.6 us -> 1.64 us
    pallas_call x1, Pallas kernels: 17.3 us -> 21.5 us  [widen_call(): pl.pallas_call(widen_body, grid=(2 * half,), out_shape=[jax.ShapeDtypeStr...]
where the time goes in v8:
time: 370 us
  Pallas kernels  362 us (98%)
    pallas_call x1, Pallas kernels, sum_call(): pl.pallas_call(sum_body, out_shape=[jax.ShapeDtypeStruct((2, GROUP_ROWS,...  210 us
    pallas_call x1, Pallas kernels, ffn_call(): pl.pallas_call(ffn_body, grid=(hidden // blk,), in_specs=[full, full, fir...  59.5 us
    pallas_call x1, Pallas kernels, attn_bwd_call(): pl.pallas_call(attn_bwd_body, grid=(pairs,), out_shape=[jax.ShapeDtypeStr...  26.9 us
    pallas_call x1, Pallas kernels, widen_call(): pl.pallas_call(widen_body, grid=(2 * half,), out_shape=[jax.ShapeDtypeStr...  21.5 us
    pallas_call x1, Pallas kernels, attn_fwd_call(): pl.pallas_call(attn_fwd_body, grid=(pairs,), out_shape=[jax.ShapeDtypeStr...  15.3 us
    pallas_call x1, Pallas kernels, ffn_back_call(): pl.pallas_call(ffn_back_body, out_shape=[jax.ShapeDtypeStruct((rows, widt...  12.4 us
    pallas_call x1, Pallas kernels, qkv_call(): pl.pallas_call(qkv_body, grid=(rows // blk,), out_shape=[jax.ShapeDtypeSt...  7.94 us
    pallas_call x1, Pallas kernels, attn_out_call(): pl.pallas_call(attn_out_body, out_shape=[jax.ShapeDtypeStruct((rows, dim)...  7.72 us
  transfers between devices with their start and end apart: 2, of which 0 were waited for; matrix products, arithmetic and copies ran while one was open for 0% of the time, Pallas kernels for 11%

profile of v8, /device:TPU:0, one launch (start us, length us, event | category | flops | bytes accessed | tf_op | source)
XLA Modules:
  0.0 369.7 jit_solution(16167615869304999336)
XLA Ops:
  0.7 0.7 convert_element_type.6
  1.4 1.2 multiply_sine_fusion
  2.6 0.0 copy-start.2
  2.6 0.0 copy-start.3
  2.6 7.9 %qkv.1 = (bf16[1024,1024]{1,0:T(8,128)(2,1)}, bf16[1024,512]{1,0:T(8,128)(2,1)}, bf16[1024,512]{1,0:T(8,128)(2,1)}, bf16[1024,512]{1,0:T(8,128)(2,1)}, f32[1024,128]{1,0:T(8,128)}, /*index=5*/f32[1024,128]{1,0:T(8,128)}) custom-call(bf16[1024,1024]{1,0:T(8,128)(2,1)} %xin.1, f32[1,1024]{1,0:T(1,128)} %bitcast.34, bf16[3,1024,512]{2,1,0:T(8,128)(2,1)} %bitcast.29, ...), custom_call_target="tpu_custom_call" | custom-call | tf_op jit(solution)/shard_map/qkv/pallas_call | solution.py:91
  10.6 0.0 copy-done.2
  10.6 0.0 copy-done.3
  10.6 1.4 select_convert_fusion
  12.1 15.3 %attn_fwd.1 = (bf16[1024,512]{1,0:T(8,128)(2,1)}, f32[1024,512]{1,0:T(8,128)}, bf16[4,2,1024,128]{3,2,1,0:T(8,128)(2,1)}) custom-call(bf16[1024,512]{1,0:T(8,128)(2,1)} %get-tuple-element.50.q_ref, bf16[1024,512]{1,0:T(8,128)(2,1)} %get-tuple-element.51.k_ref, bf16[1024,512]{1,0:T(8,128)(2,1)} %get-tuple-element.52.v_ref, ...), custom_call_target="tpu_custom_call" | custom-call | tf_op jit(solution)/shard_map/attn_fwd/pallas_call | solution.py:157
  27.4 7.7 %attn_out.1 = (f32[1024,1024]{1,0:T(8,128)}, bf16[1024,1024]{1,0:T(8,128)(2,1)}) custom-call(bf16[1024,512]{1,0:T(8,128)(2,1)} %get-tuple-element.53.o_ref.at_ref, bf16[512,1024]{1,0:T(8,128)(2,1)} %w_ref.3, f32[1,1024]{1,0:T(1,128)} %bitcast.31, bf16[1024,1024]{1,0:T(8,128)(2,1)} %xin.1), custom_call_target="tpu_custom_call" | custom-call | tf_op jit(solution)/shard_map/attn_out/pallas_call | solution.py:315
  35.1 59.5 %ffn.1 = (bf16[1024,1024]{1,0:T(8,128)(2,1)}, bf16[1024,1024]{1,0:T(8,128)(2,1)}, bf16[2,512,1024]{2,1,0:T(8,128)(2,1)}, bf16[2,512,1024]{2,1,0:T(8,128)(2,1)}, ...) custom-call(bf16[1024,1024]{1,0:T(8,128)(2,1)} %get-tuple-element.54, ...), custom_call_target="tpu_custom_call" | custom-call | tf_op jit(solution)/shard_map/ffn/pallas_call | solution.py:508
  94.6 1.5 collective-permute-start
  96.1 0.5 collective-permute-start.1
  96.7 12.4 %ffn_back.1 = (bf16[1024,512]{1,0:T(8,128)(2,1)}, bf16[512,1024]{1,0:T(8,128)(2,1)}, f32[1,1024]{1,0:T(1,128)}, bf16[1024,1024]{1,0:T(8,128)(2,1)}, f32[1024,1024]{1,0:T(8,128)}) custom-call(f32[1,1024]{1,0:T(1,128)} %bitcast.32, bf16[512,1024]{1,0:T(8,128)(2,1)} %w_ref.3, bf16[1024,512]{1,0:T(8,128)(2,1)} %get-tuple-element.53.o_ref.at_ref, ...), custom_call_target="tpu_custom_call" | custom-call | tf_op jit(solution)/shard_map/ffn_back/pallas_call | solution.py:703
  109.1 26.9 %attn_bwd.1 = (bf16[3,1024,512]{2,1,0:T(8,128)(2,1)}, f32[4,2,2,8,256]{4,3,2,1,0:T(8,128)}) custom-call(bf16[1024,512]{1,0:T(8,128)(2,1)} %get-tuple-element.50.q_ref, bf16[1024,512]{1,0:T(8,128)(2,1)} %get-tuple-element.51.k_ref, bf16[1024,512]{1,0:T(8,128)(2,1)} %get-tuple-element.52.v_ref, bf16[1024,512]{1,0:T(8,128)(2,1)} %get-tuple-element.67.do_ref, ...), custom_call_target="tpu_custom_call" | custom-call | tf_op jit(solution)/shard_map/attn_bwd/pallas_call | solution.py:228
  136.0 0.0 collective-permute-done.late_x
  136.0 0.0 copy-start
  136.0 0.0 collective-permute-done.1.late_y
  136.0 0.0 copy-start.1
  136.0 1.1 copy-done
  137.1 0.5 copy-done.1
  137.6 210.4 %grad_sum.1 = (bf16[2,2048,1024]{2,1,0:T(8,128)(2,1)}, bf16[2,2048,1024]{2,1,0:T(8,128)(2,1)}, f32[1024,1024]{1,0:T(8,128)}, f32[8,1024]{1,0:T(8,128)}) custom-call(bf16[2,512,1024]{2,1,0:T(8,128)(2,1)} %get-tuple-element.55.gk, bf16[512,1024]{1,0:T(8,128)(2,1)} %get-tuple-element.56.rg, bf16[2,512,1024]{2,1,0:T(8,128)(2,1)} %get-tuple-element.57.uk, ...), custom_call_target="tpu_custom_call" | custom-call | tf_op jit(solution)/shard_map/grad_sum/pallas_call | solution.py:1165
  348.0 21.5 %widen.1 = (f32[1024,32,128]{2,1,0:T(8,128)}, f32[4,2,2,128,1024]{4,3,2,1,0:T(8,128)}, f32[3,1024,512]{2,1,0:T(8,128)}, f32[512,1024]{1,0:T(8,128)}, f32[1,1024]...) custom-call(bf16[2,4,512,1024]{3,2,1,0:T(8,128)(2,1)} %bitcast.24, ...), custom_call_target="tpu_custom_call" | custom-call | tf_op jit(solution)/shard_map/widen/pallas_call | solution.py:584
  (5 shorter events, 0.0 us)
Async XLA Ops:
  2.6 8.0 %copy-start.2 = (s32[1024]{0:T(1024)S(1)}, s32[1024]{0:T(1024)}, u32[]{:S(2)}) copy-start(s32[1024]{0:T(1024)} %param.14) | copy-start | bytes 12292
  2.6 8.0 %copy-start.3 = (s32[1024]{0:T(1024)S(1)}, s32[1024]{0:T(1024)}, u32[]{:S(2)}) copy-start(s32[1024]{0:T(1024)} %param.13) | copy-start | bytes 12292
  94.6 41.4 %collective-permute-start = (bf16[768,1024]{1,0:T(8,128)(2,1)}, bf16[768,1024]{1,0:T(8,128)(2,1)S(1)}, u32[]{:S(2)}, u32[]{:S(2)}) collective-permute-start(bf16[768,1024]{1,0:T(8,128)(2,1)} %get-tuple-element.59), channel_id=1, source_target_pairs={{0,2},{2,0},{4,6},{6,4},{8,10},{10,8},{12,14},{14,12},{16,18},{18,... | collective-permute-start | bytes 4718600 | tf_op jit(solution)/shard_map/ppermute | solution.py:1226
  96.1 39.8 %collective-permute-start.1 = (bf16[768,1024]{1,0:T(8,128)(2,1)}, bf16[768,1024]{1,0:T(8,128)(2,1)S(1)}, u32[]{:S(2)}, u32[]{:S(2)}) collective-permute-start(bf16[768,1024]{1,0:T(8,128)(2,1)} %get-tuple-element.60), channel_id=1, source_target_pairs={{0,4},{2,6},{4,0},{6,2},{8,12},{10,14},{12,8},{14,10},{16,20},{18,... | collective-permute-start | bytes 4718600 | tf_op jit(solution)/shard_map/ppermute | solution.py:1227
  136.0 1.1 copy-start
  136.0 1.6 copy-start.1

commit v9 on v8

--- a/solution.py
+++ b/solution.py
@@ -15,6 +15,7 @@
 F32 = jnp.float32
 MESH = pl.DeviceIdType.MESH
 VMEM_LIMIT = 60 * 1024 * 1024
+VMEM_MOST = 67043328 - 512 * 1024
 LANES = 128
 HEAD = 64
 VAR_COLS = 4
@@ -238,7 +239,7 @@
         ],
         out_specs=[pl.BlockSpec((3, rows, LANES), lambda p: (0, 0, p)), pl.BlockSpec((1, 2, 2, 8, blk), lambda p: (p, 0, 0, 0, 0))],
         scratch_shapes=[pltpu.VMEM((LANES, rows), F32)],
-        compiler_params=pltpu.CompilerParams(vmem_limit_bytes=VMEM_LIMIT),
+        compiler_params=pltpu.CompilerParams(vmem_limit_bytes=VMEM_MOST),
         name="attn_bwd",
     )(q, k, v, do, o32, extq, extk, variates, cosine, sine)
 
@@ -715,7 +716,7 @@
             low, low, low, low, wide, low, wide, low, low,
             dma((2 * CHUNKS,)), dma((2 * CHUNKS,)), dma((4, CHUNKS)), dma((2, CHUNKS)),
         ],
-        compiler_params=pltpu.CompilerParams(collective_id=2, has_side_effects=True, vmem_limit_bytes=VMEM_LIMIT),
+        compiler_params=pltpu.CompilerParams(collective_id=2, has_side_effects=True, vmem_limit_bytes=VMEM_MOST),
         name="ffn_back",
     )(gain, w, at, gx, fo, mid, ct)
     return out, gm, do, gw, gg

time: 370 us -> 368 us (level)
  no operation moved by 1% of the time
where the time goes in v9:
time: 368 us
  Pallas kernels  362 us (98%)
    pallas_call x1, Pallas kernels, sum_call(): pl.pallas_call(sum_body, out_shape=[jax.ShapeDtypeStruct((2, GROUP_ROWS,...  210 us
    pallas_call x1, Pallas kernels, ffn_call(): pl.pallas_call(ffn_body, grid=(hidden // blk,), in_specs=[full, full, fir...  59.5 us
    pallas_call x1, Pallas kernels, attn_bwd_call(): pl.pallas_call(attn_bwd_body, grid=(pairs,), out_shape=[jax.ShapeDtypeStr...  26.9 us
    pallas_call x1, Pallas kernels, widen_call(): pl.pallas_call(widen_body, grid=(2 * half,), out_shape=[jax.ShapeDtypeStr...  21.5 us
    pallas_call x1, Pallas kernels, attn_fwd_call(): pl.pallas_call(attn_fwd_body, grid=(pairs,), out_shape=[jax.ShapeDtypeStr...  15.3 us
    pallas_call x1, Pallas kernels, ffn_back_call(): pl.pallas_call(ffn_back_body, out_shape=[jax.ShapeDtypeStruct((rows, widt...  12.3 us
    pallas_call x1, Pallas kernels, qkv_call(): pl.pallas_call(qkv_body, grid=(rows // blk,), out_shape=[jax.ShapeDtypeSt...  7.94 us
    pallas_call x1, Pallas kernels, attn_out_call(): pl.pallas_call(attn_out_body, out_shape=[jax.ShapeDtypeStruct((rows, dim)...  7.73 us
  transfers between devices with their start and end apart: 2, of which 0 were waited for; matrix products, arithmetic and copies ran while one was open for 0% of the time, Pallas kernels for 11%

profile of v9, /device:TPU:0, one launch (start us, length us, event | category | flops | bytes accessed | tf_op | source)
XLA Modules:
  0.0 368.1 jit_solution(11187692264522197013)
XLA Ops:
  0.7 0.7 convert_element_type.6
  1.4 1.2 multiply_sine_fusion
  2.6 0.0 copy-start
  2.6 0.0 copy-start.1
  2.6 7.9 %qkv.1 = (bf16[1024,1024]{1,0:T(8,128)(2,1)}, bf16[1024,512]{1,0:T(8,128)(2,1)}, bf16[1024,512]{1,0:T(8,128)(2,1)}, bf16[1024,512]{1,0:T(8,128)(2,1)}, f32[1024,128]{1,0:T(8,128)}, /*index=5*/f32[1024,128]{1,0:T(8,128)}) custom-call(bf16[1024,1024]{1,0:T(8,128)(2,1)} %xin.1, f32[1,1024]{1,0:T(1,128)} %bitcast.34, bf16[3,1024,512]{2,1,0:T(8,128)(2,1)} %bitcast.29, ...), custom_call_target="tpu_custom_call" | custom-call | tf_op jit(solution)/shard_map/qkv/pallas_call | solution.py:92
  10.6 0.0 copy-done
  10.6 0.0 copy-done.1
  10.6 1.5 select_convert_fusion
  12.1 15.3 %attn_fwd.1 = (bf16[1024,512]{1,0:T(8,128)(2,1)}, f32[1024,512]{1,0:T(8,128)}, bf16[4,2,1024,128]{3,2,1,0:T(8,128)(2,1)}) custom-call(bf16[1024,512]{1,0:T(8,128)(2,1)} %get-tuple-element.50.q_ref, bf16[1024,512]{1,0:T(8,128)(2,1)} %get-tuple-element.51.k_ref, bf16[1024,512]{1,0:T(8,128)(2,1)} %get-tuple-element.52.v_ref, ...), custom_call_target="tpu_custom_call" | custom-call | tf_op jit(solution)/shard_map/attn_fwd/pallas_call | solution.py:158
  27.4 7.7 %attn_out.1 = (f32[1024,1024]{1,0:T(8,128)}, bf16[1024,1024]{1,0:T(8,128)(2,1)}) custom-call(bf16[1024,512]{1,0:T(8,128)(2,1)} %get-tuple-element.53.o_ref.at_ref, bf16[512,1024]{1,0:T(8,128)(2,1)} %w_ref.3, f32[1,1024]{1,0:T(1,128)} %bitcast.31, bf16[1024,1024]{1,0:T(8,128)(2,1)} %xin.1), custom_call_target="tpu_custom_call" | custom-call | tf_op jit(solution)/shard_map/attn_out/pallas_call | solution.py:316
  35.1 59.5 %ffn.1 = (bf16[1024,1024]{1,0:T(8,128)(2,1)}, bf16[1024,1024]{1,0:T(8,128)(2,1)}, bf16[2,512,1024]{2,1,0:T(8,128)(2,1)}, bf16[2,512,1024]{2,1,0:T(8,128)(2,1)}, ...) custom-call(bf16[1024,1024]{1,0:T(8,128)(2,1)} %get-tuple-element.54, ...), custom_call_target="tpu_custom_call" | custom-call | tf_op jit(solution)/shard_map/ffn/pallas_call | solution.py:509
  94.6 1.6 collective-permute-start
  96.2 0.5 collective-permute-start.1
  96.7 12.3 %ffn_back.1 = (bf16[1024,512]{1,0:T(8,128)(2,1)}, bf16[512,1024]{1,0:T(8,128)(2,1)}, f32[1,1024]{1,0:T(1,128)}, bf16[1024,1024]{1,0:T(8,128)(2,1)}, f32[1024,1024]{1,0:T(8,128)}) custom-call(f32[1,1024]{1,0:T(1,128)} %bitcast.32, bf16[512,1024]{1,0:T(8,128)(2,1)} %w_ref.3, bf16[1024,512]{1,0:T(8,128)(2,1)} %get-tuple-element.53.o_ref.at_ref, ...), custom_call_target="tpu_custom_call" | custom-call | tf_op jit(solution)/shard_map/ffn_back/pallas_call | solution.py:704
  109.0 26.9 %attn_bwd.1 = (bf16[3,1024,512]{2,1,0:T(8,128)(2,1)}, f32[4,2,2,8,256]{4,3,2,1,0:T(8,128)}) custom-call(bf16[1024,512]{1,0:T(8,128)(2,1)} %get-tuple-element.50.q_ref, bf16[1024,512]{1,0:T(8,128)(2,1)} %get-tuple-element.51.k_ref, bf16[1024,512]{1,0:T(8,128)(2,1)} %get-tuple-element.52.v_ref, bf16[1024,512]{1,0:T(8,128)(2,1)} %get-tuple-element.67.do_ref, ...), custom_call_target="tpu_custom_call" | custom-call | tf_op jit(solution)/shard_map/attn_bwd/pallas_call | solution.py:229
  135.9 0.0 collective-permute-done.late_x
  135.9 0.0 collective-permute-done.1.late_y
  135.9 210.4 %grad_sum.1 = (bf16[2,2048,1024]{2,1,0:T(8,128)(2,1)}, bf16[2,2048,1024]{2,1,0:T(8,128)(2,1)}, f32[1024,1024]{1,0:T(8,128)}, f32[8,1024]{1,0:T(8,128)}) custom-call(bf16[2,512,1024]{2,1,0:T(8,128)(2,1)} %get-tuple-element.55.gk, bf16[512,1024]{1,0:T(8,128)(2,1)} %get-tuple-element.56.rg, bf16[2,512,1024]{2,1,0:T(8,128)(2,1)} %get-tuple-element.57.uk, ...), custom_call_target="tpu_custom_call" | custom-call | tf_op jit(solution)/shard_map/grad_sum/pallas_call | solution.py:1166
  346.3 21.5 %widen.1 = (f32[1024,32,128]{2,1,0:T(8,128)}, f32[4,2,2,128,1024]{4,3,2,1,0:T(8,128)}, f32[3,1024,512]{2,1,0:T(8,128)}, f32[512,1024]{1,0:T(8,128)}, f32[1,1024]...) custom-call(bf16[2,4,512,1024]{3,2,1,0:T(8,128)(2,1)} %bitcast.24, ...), custom_call_target="tpu_custom_call" | custom-call | tf_op jit(solution)/shard_map/widen/pallas_call | solution.py:585
  (5 shorter events, 0.0 us)
Async XLA Ops:
  2.6 8.0 %copy-start = (s32[1024]{0:T(1024)S(1)}, s32[1024]{0:T(1024)}, u32[]{:S(2)}) copy-start(s32[1024]{0:T(1024)} %param.14) | copy-start | bytes 12292
  2.6 8.0 %copy-start.1 = (s32[1024]{0:T(1024)S(1)}, s32[1024]{0:T(1024)}, u32[]{:S(2)}) copy-start(s32[1024]{0:T(1024)} %param.13) | copy-start | bytes 12292
  94.6 41.3 %collective-permute-start = (bf16[768,1024]{1,0:T(8,128)(2,1)}, bf16[768,1024]{1,0:T(8,128)(2,1)}, u32[]{:S(2)}, u32[]{:S(2)}) collective-permute-start(bf16[768,1024]{1,0:T(8,128)(2,1)} %get-tuple-element.59), channel_id=1, source_target_pairs={{0,2},{2,0},{4,6},{6,4},{8,10},{10,8},{12,14},{14,12},{16,18},{18,... | collective-permute-start | bytes 4718600 | tf_op jit(solution)/shard_map/ppermute | solution.py:1227
  96.2 39.8 %collective-permute-start.1 = (bf16[768,1024]{1,0:T(8,128)(2,1)}, bf16[768,1024]{1,0:T(8,128)(2,1)}, u32[]{:S(2)}, u32[]{:S(2)}) collective-permute-start(bf16[768,1024]{1,0:T(8,128)(2,1)} %get-tuple-element.60), channel_id=1, source_target_pairs={{0,4},{2,6},{4,0},{6,2},{8,12},{10,14},{12,8},{14,10},{16,20},{18,... | collective-permute-start | bytes 4718600 | tf_op jit(solution)/shard_map/ppermute | solution.py:1228

commit v10 on v9

--- a/solution.py
+++ b/solution.py
@@ -31,7 +31,7 @@
 WIDE = 1024
 SMALL = 8
 QBLK = 256
-FFN_ROWS = 512
+FFN_ROWS = 1024
 FFN_COLS = 512
 
 

time: 368 us -> 368 us (level)
  no operation moved by 1% of the time
where the time goes in v10:
time: 368 us
  Pallas kernels  361 us (98%)
    pallas_call x1, Pallas kernels, sum_call(): pl.pallas_call(sum_body, out_shape=[jax.ShapeDtypeStruct((2, GROUP_ROWS,...  210 us
    pallas_call x1, Pallas kernels, ffn_call(): pl.pallas_call(ffn_body, grid=(hidden // blk,), in_specs=[full, full, fir...  59.1 us
    pallas_call x1, Pallas kernels, attn_bwd_call(): pl.pallas_call(attn_bwd_body, grid=(pairs,), out_shape=[jax.ShapeDtypeStr...  26.9 us
    pallas_call x1, Pallas kernels, widen_call(): pl.pallas_call(widen_body, grid=(2 * half,), out_shape=[jax.ShapeDtypeStr...  21.5 us
    pallas_call x1, Pallas kernels, attn_fwd_call(): pl.pallas_call(attn_fwd_body, grid=(pairs,), out_shape=[jax.ShapeDtypeStr...  15.3 us
    pallas_call x1, Pallas kernels, ffn_back_call(): pl.pallas_call(ffn_back_body, out_shape=[jax.ShapeDtypeStruct((rows, widt...  12.3 us
    pallas_call x1, Pallas kernels, qkv_call(): pl.pallas_call(qkv_body, grid=(rows // blk,), out_shape=[jax.ShapeDtypeSt...  7.94 us
    pallas_call x1, Pallas kernels, attn_out_call(): pl.pallas_call(attn_out_body, out_shape=[jax.ShapeDtypeStruct((rows, dim)...  7.73 us
  transfers between devices with their start and end apart: 2, of which 0 were waited for; matrix products, arithmetic and copies ran while one was open for 0% of the time, Pallas kernels for 11%

profile of v10, /device:TPU:0, one launch (start us, length us, event | category | flops | bytes accessed | tf_op | source)
XLA Modules:
  0.0 367.7 jit_solution(14758263111251751542)
XLA Ops:
  0.7 0.7 convert_element_type.6
  1.4 1.2 multiply_sine_fusion
  2.6 0.0 copy-start
  2.6 0.0 copy-start.1
  2.6 7.9 %qkv.1 = (bf16[1024,1024]{1,0:T(8,128)(2,1)}, bf16[1024,512]{1,0:T(8,128)(2,1)}, bf16[1024,512]{1,0:T(8,128)(2,1)}, bf16[1024,512]{1,0:T(8,128)(2,1)}, f32[1024,128]{1,0:T(8,128)}, /*index=5*/f32[1024,128]{1,0:T(8,128)}) custom-call(bf16[1024,1024]{1,0:T(8,128)(2,1)} %xin.1, f32[1,1024]{1,0:T(1,128)} %bitcast.34, bf16[3,1024,512]{2,1,0:T(8,128)(2,1)} %bitcast.29, ...), custom_call_target="tpu_custom_call" | custom-call | tf_op jit(solution)/shard_map/qkv/pallas_call | solution.py:92
  10.6 0.0 copy-done
  10.6 0.0 copy-done.1
  10.6 1.5 select_convert_fusion
  12.1 15.3 %attn_fwd.1 = (bf16[1024,512]{1,0:T(8,128)(2,1)}, f32[1024,512]{1,0:T(8,128)}, bf16[4,2,1024,128]{3,2,1,0:T(8,128)(2,1)}) custom-call(bf16[1024,512]{1,0:T(8,128)(2,1)} %get-tuple-element.50.q_ref, bf16[1024,512]{1,0:T(8,128)(2,1)} %get-tuple-element.51.k_ref, bf16[1024,512]{1,0:T(8,128)(2,1)} %get-tuple-element.52.v_ref, ...), custom_call_target="tpu_custom_call" | custom-call | tf_op jit(solution)/shard_map/attn_fwd/pallas_call | solution.py:158
  27.4 7.7 %attn_out.1 = (f32[1024,1024]{1,0:T(8,128)}, bf16[1024,1024]{1,0:T(8,128)(2,1)}) custom-call(bf16[1024,512]{1,0:T(8,128)(2,1)} %get-tuple-element.53.o_ref.at_ref, bf16[512,1024]{1,0:T(8,128)(2,1)} %w_ref.3, f32[1,1024]{1,0:T(1,128)} %bitcast.31, bf16[1024,1024]{1,0:T(8,128)(2,1)} %xin.1), custom_call_target="tpu_custom_call" | custom-call | tf_op jit(solution)/shard_map/attn_out/pallas_call | solution.py:316
  35.1 59.1 %ffn.1 = (bf16[1024,1024]{1,0:T(8,128)(2,1)}, bf16[1024,1024]{1,0:T(8,128)(2,1)}, bf16[2,512,1024]{2,1,0:T(8,128)(2,1)}, bf16[2,512,1024]{2,1,0:T(8,128)(2,1)}, ...) custom-call(bf16[1024,1024]{1,0:T(8,128)(2,1)} %get-tuple-element.54, ...), custom_call_target="tpu_custom_call" | custom-call | tf_op jit(solution)/shard_map/ffn/pallas_call | solution.py:509
  94.3 1.6 collective-permute-start
  95.8 0.5 collective-permute-start.1
  96.4 12.3 %ffn_back.1 = (bf16[1024,512]{1,0:T(8,128)(2,1)}, bf16[512,1024]{1,0:T(8,128)(2,1)}, f32[1,1024]{1,0:T(1,128)}, bf16[1024,1024]{1,0:T(8,128)(2,1)}, f32[1024,1024]{1,0:T(8,128)}) custom-call(f32[1,1024]{1,0:T(1,128)} %bitcast.32, bf16[512,1024]{1,0:T(8,128)(2,1)} %w_ref.3, bf16[1024,512]{1,0:T(8,128)(2,1)} %get-tuple-element.53.o_ref.at_ref, ...), custom_call_target="tpu_custom_call" | custom-call | tf_op jit(solution)/shard_map/ffn_back/pallas_call | solution.py:704
  108.7 26.9 %attn_bwd.1 = (bf16[3,1024,512]{2,1,0:T(8,128)(2,1)}, f32[4,2,2,8,256]{4,3,2,1,0:T(8,128)}) custom-call(bf16[1024,512]{1,0:T(8,128)(2,1)} %get-tuple-element.50.q_ref, bf16[1024,512]{1,0:T(8,128)(2,1)} %get-tuple-element.51.k_ref, bf16[1024,512]{1,0:T(8,128)(2,1)} %get-tuple-element.52.v_ref, bf16[1024,512]{1,0:T(8,128)(2,1)} %get-tuple-element.67.do_ref, ...), custom_call_target="tpu_custom_call" | custom-call | tf_op jit(solution)/shard_map/attn_bwd/pallas_call | solution.py:229
  135.6 0.0 collective-permute-done.late_x
  135.6 0.0 collective-permute-done.1.late_y
  135.6 210.4 %grad_sum.1 = (bf16[2,2048,1024]{2,1,0:T(8,128)(2,1)}, bf16[2,2048,1024]{2,1,0:T(8,128)(2,1)}, f32[1024,1024]{1,0:T(8,128)}, f32[8,1024]{1,0:T(8,128)}) custom-call(bf16[2,512,1024]{2,1,0:T(8,128)(2,1)} %get-tuple-element.55.gk, bf16[512,1024]{1,0:T(8,128)(2,1)} %get-tuple-element.56.rg, bf16[2,512,1024]{2,1,0:T(8,128)(2,1)} %get-tuple-element.57.uk, ...), custom_call_target="tpu_custom_call" | custom-call | tf_op jit(solution)/shard_map/grad_sum/pallas_call | solution.py:1166
  346.0 21.5 %widen.1 = (f32[1024,32,128]{2,1,0:T(8,128)}, f32[4,2,2,128,1024]{4,3,2,1,0:T(8,128)}, f32[3,1024,512]{2,1,0:T(8,128)}, f32[512,1024]{1,0:T(8,128)}, f32[1,1024]...) custom-call(bf16[2,4,512,1024]{3,2,1,0:T(8,128)(2,1)} %bitcast.24, ...), custom_call_target="tpu_custom_call" | custom-call | tf_op jit(solution)/shard_map/widen/pallas_call | solution.py:585
  (5 shorter events, 0.0 us)
Async XLA Ops:
  2.6 8.0 %copy-start = (s32[1024]{0:T(1024)S(1)}, s32[1024]{0:T(1024)}, u32[]{:S(2)}) copy-start(s32[1024]{0:T(1024)} %param.14) | copy-start | bytes 12292
  2.6 8.0 %copy-start.1 = (s32[1024]{0:T(1024)S(1)}, s32[1024]{0:T(1024)}, u32[]{:S(2)}) copy-start(s32[1024]{0:T(1024)} %param.13) | copy-start | bytes 12292
  94.3 41.3 %collective-permute-start = (bf16[768,1024]{1,0:T(8,128)(2,1)}, bf16[768,1024]{1,0:T(8,128)(2,1)}, u32[]{:S(2)}, u32[]{:S(2)}) collective-permute-start(bf16[768,1024]{1,0:T(8,128)(2,1)} %get-tuple-element.59), channel_id=1, source_target_pairs={{0,2},{2,0},{4,6},{6,4},{8,10},{10,8},{12,14},{14,12},{16,18},{18,... | collective-permute-start | bytes 4718600 | tf_op jit(solution)/shard_map/ppermute | solution.py:1227
  95.8 39.8 %collective-permute-start.1 = (bf16[768,1024]{1,0:T(8,128)(2,1)}, bf16[768,1024]{1,0:T(8,128)(2,1)}, u32[]{:S(2)}, u32[]{:S(2)}) collective-permute-start(bf16[768,1024]{1,0:T(8,128)(2,1)} %get-tuple-element.60), channel_id=1, source_target_pairs={{0,4},{2,6},{4,0},{6,2},{8,12},{10,14},{12,8},{14,10},{16,20},{18,... | collective-permute-start | bytes 4718600 | tf_op jit(solution)/shard_map/ppermute | solution.py:1228
